TPU v7x, 32 devices: a whole 2x2x4 slice. The times are simulated.
32 devices in a mesh: dp: 8 (over z, x), tensor: 4 (over y, core).
Axes of the slice: x: 2, y: 2, z: 4, core: 2. Of those that a mesh axis runs over, the one named last changes fastest.
Arguments:
- block_input: bfloat16 [1024, 8, 1024], P('tensor', 'dp'), may hold values from -6 to 6
- pre_gain: float32 [1024], replicated, may hold values from 0.25 to 1.75
- w_zx: bfloat16 [1024, 2, 2048], P('dp', None, 'tensor'), may hold values from -0.1875 to 0.1875
- w_dt: bfloat16 [1024, 32], P('dp', 'tensor'), may hold values from -0.1875 to 0.1875
- w_bc: bfloat16 [1024, 256], P('dp'), may hold values from -0.1875 to 0.1875
- conv_x_w: float32 [4, 2048], P(None, 'tensor'), may hold values from -3 to 3
- conv_x_b: float32 [2048], P('tensor'), may hold values from -3 to 3
- conv_bc_w: float32 [4, 256], replicated, may hold values from -3 to 3
- conv_bc_b: float32 [256], replicated, may hold values from -3 to 3
- dt_bias: float32 [32], P('tensor'), may hold values from -4 to -1
- a_log: float32 [32], P('tensor'), may hold values from -7.6 to -0.7
- d_skip: float32 [32], P('tensor'), may hold values from 0.5 to 1.5
- gate_gain: float32 [2048], P('tensor'), may hold values from 0.25 to 1.75
- w_out: bfloat16 [2048, 1024], P('tensor', 'dp'), may hold values from -0.125 to 0.125
- cotangent: bfloat16 [1024, 8, 1024], P('tensor', 'dp'), may hold values from -6 to 6
Outputs:
- block_output: float32 [1024, 8, 1024], P('tensor', 'dp')
- input_grad: float32 [1024, 8, 1024], P('tensor', 'dp')
- grad_pre_gain: float32 [1024], replicated
- grad_w_zx: float32 [1024, 2, 2048], P('dp', None, 'tensor')
- grad_w_dt: float32 [1024, 32], P('dp', 'tensor')
- grad_w_bc: float32 [1024, 256], P('dp')
- grad_conv_x_w: float32 [4, 2048], P(None, 'tensor')
- grad_conv_x_b: float32 [2048], P('tensor')
- grad_conv_bc_w: float32 [4, 256], replicated
- grad_conv_bc_b: float32 [256], replicated
- grad_dt_bias: float32 [32], P('tensor')
- grad_a_log: float32 [32], P('tensor')
- grad_d_skip: float32 [32], P('tensor')
- grad_gate_gain: float32 [2048], P('tensor')
- grad_w_out: float32 [2048, 1024], P('tensor', 'dp')
All inputs are finite; a program needn't handle non-finite values.
Results may differ from a plain program's by a relative error of at most 0.0094.
Values may be sent and summed in bfloat16 or wider, within the bound.
No kernel may reach another device: no remote copies, remote signals or barrier semaphores. Data moves between devices by JAX's collectives and lax.ppermute only.
A program may use at most 128 MiB of HBM per device.

v0:
```python
import jax
import jax.numpy as jnp
from jax import lax
from jax.sharding import PartitionSpec as P

SPAN = 256


epsilon = 1e-05
highest = lax.Precision.HIGHEST


def causal_conv(values, kernel, offset):
    width = kernel.shape[0]
    length = values.shape[0]
    padded = jnp.pad(values, ((width - 1, 0), (0, 0)))
    total = jnp.zeros_like(values) + offset
    for tap in range(width):
        total = total + kernel[tap] * padded[tap : tap + length]
    return total


def scan_heads(inputs, steps, rates, keys, queries, skip):
    length, heads, width = inputs.shape
    count = length // SPAN
    inputs_block = inputs.reshape(count, SPAN, heads, width)
    steps_block = steps.reshape(count, SPAN, heads)
    keys_block = keys.reshape(count, SPAN, keys.shape[-1])
    queries_block = queries.reshape(count, SPAN, queries.shape[-1])
    logs = jnp.cumsum(steps_block * rates, axis=1)
    gaps = logs[:, :, None, :] - logs[:, None, :, :]
    lower = jnp.arange(SPAN)[:, None] >= jnp.arange(SPAN)[None, :]
    decay = jnp.exp(jnp.where(lower[None, :, :, None], gaps, -jnp.inf))
    scores = jnp.einsum("ctn,csn->cts", queries_block, keys_block, precision=highest)
    weights = scores[..., None] * decay * steps_block[:, None, :, :]
    within = jnp.einsum("ctsh,cshp->cthp", weights, inputs_block, precision=highest)
    ends = logs[:, -1:, :] - logs
    scaled = inputs_block * (jnp.exp(ends) * steps_block)[..., None]
    states = jnp.einsum("csn,cshp->chnp", keys_block, scaled, precision=highest)
    totals = jnp.exp(logs[:, -1, :])

    def carry_step(state, pair):
        factor, fresh = pair
        return (factor[:, None, None] * state + fresh, state)

    initial = jnp.zeros(states.shape[1:], jnp.float32)
    final_state, previous = lax.scan(carry_step, initial, (totals, states))
    across = (
        jnp.einsum("ctn,chnp->cthp", queries_block, previous, precision=highest)
        * jnp.exp(logs)[..., None]
    )
    output = (within + across).reshape(length, heads, width)
    return output + skip[:, None] * inputs


def mixer_one(
    raw_x, raw_dt, raw_bc, kernel_x, offset_x, kernel_bc, offset_bc, dt_offset, log_rates, skip
):
    inner = jax.nn.silu(causal_conv(raw_x, kernel_x, offset_x))
    mixed_bc = jax.nn.silu(causal_conv(raw_bc, kernel_bc, offset_bc))
    half = mixed_bc.shape[-1] // 2
    steps = jax.nn.softplus(raw_dt + dt_offset)
    rates = -jnp.exp(log_rates)
    heads = steps.shape[-1]
    inputs = inner.reshape(inner.shape[0], heads, inner.shape[1] // heads)
    result = scan_heads(inputs, steps, rates, mixed_bc[:, :half], mixed_bc[:, half:], skip)
    return result.reshape(inner.shape)


def batched_mixer(
    raw_x, raw_dt, raw_bc, kernel_x, offset_x, kernel_bc, offset_bc, dt_offset, log_rates, skip
):
    mapped = jax.vmap(
        mixer_one, in_axes=(1, 1, 1, None, None, None, None, None, None, None), out_axes=1
    )
    return mapped(
        raw_x, raw_dt, raw_bc, kernel_x, offset_x, kernel_bc, offset_bc, dt_offset, log_rates, skip
    )


def silu_slope(values):
    sigmoid = jax.nn.sigmoid(values)
    return sigmoid * (1.0 + values * (1.0 - sigmoid))


def per_device(
    block_input,
    pre_gain,
    w_zx,
    w_dt,
    w_bc,
    conv_x_w,
    conv_x_b,
    conv_bc_w,
    conv_bc_b,
    dt_bias,
    a_log,
    d_skip,
    gate_gain,
    w_out,
    cotangent,
):
    rows_local = block_input.shape[0]
    seqs = block_input.shape[1]
    model = block_input.shape[2]
    wide = block_input.astype(jnp.float32)
    inverse = lax.rsqrt(jnp.mean(wide * wide, axis=-1, keepdims=True) + epsilon)
    normed_local = (wide * inverse * pre_gain).astype(jnp.bfloat16)
    normed = lax.all_gather(normed_local, "tensor", axis=0, tiled=True)
    length = normed.shape[0]
    tokens = length * seqs
    full_zx, full_dt, full_bc, full_out = (
        lax.all_gather(w_zx, "dp", axis=0, tiled=True),
        lax.all_gather(w_dt, "dp", axis=0, tiled=True),
        lax.all_gather(w_bc, "dp", axis=0, tiled=True),
        lax.all_gather(w_out, "dp", axis=1, tiled=True),
    )
    local_inner = full_zx.shape[2]
    state_twice = full_bc.shape[1]
    columns = jnp.concatenate([full_zx.reshape(model, 2 * local_inner), full_bc, full_dt], axis=1)
    projected = jnp.dot(normed.reshape(tokens, model), columns, preferred_element_type=jnp.float32)
    projected = projected.reshape(length, seqs, -1)
    gate_raw = projected[:, :, :local_inner]
    raw_x = projected[:, :, local_inner : 2 * local_inner]
    raw_bc = projected[:, :, 2 * local_inner : 2 * local_inner + state_twice]
    raw_dt = projected[:, :, 2 * local_inner + state_twice :]
    mixed, pullback = jax.vjp(
        batched_mixer,
        raw_x,
        raw_dt,
        raw_bc,
        conv_x_w,
        conv_x_b,
        conv_bc_w,
        conv_bc_b,
        dt_bias,
        a_log,
        d_skip,
    )
    gate_act = jax.nn.silu(gate_raw)
    gated = mixed * gate_act
    inner_total = local_inner * lax.axis_size("tensor")
    square_sum = lax.psum(jnp.sum(gated * gated, axis=-1), "tensor")
    gate_inverse = lax.rsqrt(square_sum / inner_total + epsilon)[..., None]
    scaled_gate = (gated * gate_inverse * gate_gain).astype(jnp.bfloat16)
    piece = scaled_gate
    branch = lax.psum_scatter(
        jnp.einsum("lsi,id->lsd", piece, full_out, preferred_element_type=jnp.float32).astype(
            jnp.bfloat16
        ),
        "tensor",
        scatter_dimension=0,
        tiled=True,
    ).astype(jnp.float32)
    block_output = wide + branch
    back_zx, back_dt, back_bc, back_out = (
        lax.all_gather(w_zx, "dp", axis=0, tiled=True),
        lax.all_gather(w_dt, "dp", axis=0, tiled=True),
        lax.all_gather(w_bc, "dp", axis=0, tiled=True),
        lax.all_gather(w_out, "dp", axis=1, tiled=True),
    )
    upstream = lax.all_gather(cotangent, "tensor", axis=0, tiled=True)
    grad_scaled = jnp.einsum("lsd,id->lsi", upstream, back_out, preferred_element_type=jnp.float32)
    grad_out_part = jnp.einsum(
        "lsi,lsd->id", scaled_gate, upstream, preferred_element_type=jnp.float32
    )
    weighted = grad_scaled * gate_gain
    dot_term = lax.psum(jnp.sum(weighted * gated, axis=-1), "tensor")[..., None]
    grad_gated = gate_inverse * weighted - gated * gate_inverse**3 * dot_term / inner_total
    gate_gain_part = jnp.sum(grad_scaled * gated * gate_inverse, axis=(0, 1))
    grad_mixed = grad_gated * gate_act
    grad_gate_raw = grad_gated * mixed * silu_slope(gate_raw)
    (
        grad_raw_x,
        grad_raw_dt,
        grad_raw_bc,
        grad_kx,
        grad_bx,
        grad_kbc,
        grad_bbc,
        grad_dtb,
        grad_alog,
        grad_skip,
    ) = pullback(grad_mixed)
    bc_total = lax.psum(grad_raw_bc, "tensor")
    grad_zx_half = (
        jnp.stack([grad_gate_raw, grad_raw_x], axis=2)
        .reshape(length, seqs, 2 * local_inner)
        .astype(jnp.bfloat16)
    )
    grad_dt_half = grad_raw_dt.astype(jnp.bfloat16)
    grad_bc_half = bc_total.astype(jnp.bfloat16)
    grad_all = jnp.concatenate([grad_zx_half, grad_bc_half, grad_dt_half], axis=-1)
    weight_part = jnp.einsum("lsd,lsc->dc", normed, grad_all, preferred_element_type=jnp.float32)
    grad_zx_part = weight_part[:, : 2 * local_inner].reshape(model, 2, local_inner)
    grad_bc_part = weight_part[:, 2 * local_inner : 2 * local_inner + state_twice]
    grad_dt_part = weight_part[:, 2 * local_inner + state_twice :]
    head_grads = jnp.concatenate([grad_zx_half, grad_dt_half], axis=-1)
    head_weights = jnp.concatenate([back_zx.reshape(model, 2 * local_inner), back_dt], axis=1)
    piece = head_grads
    grad_normed = lax.psum_scatter(
        jnp.einsum("lsc,dc->lsd", piece, head_weights, preferred_element_type=jnp.float32),
        "tensor",
        scatter_dimension=0,
        tiled=True,
    )
    own_rows = lax.dynamic_slice_in_dim(
        grad_bc_half, lax.axis_index("tensor") * rows_local, rows_local, 0
    )
    grad_normed = grad_normed + jnp.einsum(
        "lsc,dc->lsd", own_rows, back_bc, preferred_element_type=jnp.float32
    )
    weighted_in = grad_normed * pre_gain
    inner_dot = jnp.mean(weighted_in * wide, axis=-1, keepdims=True)
    input_grad = (
        cotangent.astype(jnp.float32) + inverse * weighted_in - wide * inverse**3 * inner_dot
    )
    pre_gain_part = jnp.sum(grad_normed * wide * inverse, axis=(0, 1))
    grad_w_zx, grad_w_dt, grad_w_bc, grad_w_out = (
        lax.psum_scatter(grad_zx_part, "dp", scatter_dimension=0, tiled=True),
        lax.psum_scatter(grad_dt_part, "dp", scatter_dimension=0, tiled=True),
        lax.psum_scatter(grad_bc_part, "dp", scatter_dimension=0, tiled=True),
        lax.psum_scatter(grad_out_part, "dp", scatter_dimension=1, tiled=True),
    )
    conv_w_sum, conv_b_sum, dt_sum, rate_sum, skip_sum, gain_sum = lax.psum(
        (grad_kx, grad_bx, grad_dtb, grad_alog, grad_skip, gate_gain_part), "dp"
    )
    pre_sum, kbc_sum, bbc_sum = lax.psum((pre_gain_part, grad_kbc, grad_bbc), ("dp", "tensor"))
    return (
        block_output,
        input_grad,
        pre_sum,
        grad_w_zx,
        grad_w_dt,
        grad_w_bc,
        conv_w_sum,
        conv_b_sum,
        kbc_sum,
        bbc_sum,
        dt_sum,
        rate_sum,
        skip_sum,
        gain_sum,
        grad_w_out,
    )


def solution(mesh):
    placed = (
        P("tensor", "dp", None),
        P(),
        P("dp", None, "tensor"),
        P("dp", "tensor"),
        P("dp", None),
        P(None, "tensor"),
        P("tensor"),
        P(),
        P(),
        P("tensor"),
        P("tensor"),
        P("tensor"),
        P("tensor"),
        P("tensor", "dp"),
        P("tensor", "dp", None),
    )
    return jax.shard_map(
        per_device,
        mesh=mesh,
        in_specs=placed,
        out_specs=(
            P("tensor", "dp", None),
            P("tensor", "dp", None),
            P(),
            P("dp", None, "tensor"),
            P("dp", "tensor"),
            P("dp", None),
            P(None, "tensor"),
            P("tensor"),
            P(),
            P(),
            P("tensor"),
            P("tensor"),
            P("tensor"),
            P("tensor"),
            P("tensor", "dp"),
        ),
        check_vma=False,
    )
```

profile of v0, /device:TPU:0, one launch (start us, length us, event | category | flops | bytes accessed | tf_op | source)
XLA Modules:
  0.0 815.6 jit_solution(9301264668837840181)
XLA Ops:
  14.2 28.2 %all_gather.25 = bf16[1024,8]{0,1:T(8,128)(2,1)S(1)} all-gather(bf16[128,8]{0,1:T(8,128)(2,1)S(1)} %copy-done.94), channel_id=1, replica_groups=mesh['dp'=8,'tensor'=4] {'dp'}, dimensions={0}, use_global_device_ids=true | all-gather | bytes 18432 | tf_op jit(solution)/shard_map/all_gather | solution.py:114
  43.6 32.7 %all_gather.24 = bf16[1024,256]{1,0:T(8,128)(2,1)S(1)} all-gather(bf16[128,256]{1,0:T(8,128)(2,1)S(1)} %copy-done.39), channel_id=1, replica_groups=mesh['dp'=8,'tensor'=4] {'dp'}, dimensions={0}, use_global_device_ids=true | all-gather | bytes 589824 | tf_op jit(solution)/shard_map/all_gather | solution.py:115
  76.3 4.1 copy.298
  80.3 11.5 %all-gather.5.cloned.1.call-done = bf16[1024,1,1024]{2,0,1:T(8,128)(2,1)} async-done(((bf16[256,1,1024]{2,0,1:T(8,128)(2,1)}), bf16[1024,1,1024]{2,0,1:T(8,128)(2,1)}) %all-gather.5.cloned.1.call-update) | async-done | bytes 2097168 | tf_op jit(solution)/shard_map/all_gather | solution.py:109
  91.9 5.3 convolution_bitcast_fusion
  100.0 2.2 transpose.148
  102.2 4.3 pad_slice_fusion.2
  106.6 2.3 reduce-window.14
  110.1 4.9 fusion.135
  116.1 2.1 reshape.3068
  118.2 2.1 copy.277
  120.2 3.2 transpose.145
  123.5 3.2 transpose.146
  126.6 3.2 transpose.147
  129.8 5.7 divide_multiply_fusion
  135.5 3.0 fusion.93
  140.2 20.5 %while.34 = (s32[]{:T(128)}, f32[1,8,128,64]{3,2,1,0:T(8,128)S(1)}, f32[4,1,8,128,64]{4,3,2,1,0:T(8,128)}, f32[4,1,8,1,1]{2,4,3,1,0:T(1,128)}, f32[4,1,8]{2,1,0:...) while((s32[]{:T(128)}, f32[1,8,128,64]{3,2,1,0:T(8,128)S(1)}, ...), condition=%wide.region_4.5_spmd.clone, body=%wide.region_3.4_spmd.clone.sunk | while | flops 262147 | bytes 2623280 | solution.py:47
  163.7 3.2 transpose.166
  167.0 3.2 transpose.167
  170.1 3.6 transpose.168
  176.1 3.2 copy.242
  179.4 2.2 fusion.183
  183.6 9.3 %bitcast_add_fusion.3 = f32[1,4,256,8,64]{2,4,3,1,0:T(8,128)S(1)} fusion(f32[4,256,8,64]{1,3,2,0:T(8,128)S(1)} %bitcast.455, f32[4,256,8,64]{1,3,2,0:T(8,128)S(1)} %copy-done.4, f32[4,256,8]{1,2,0:T(8,128)S(1)} %compare_select_fusion.5, f32[4,256,8]{1,2,0:T(8,128)S(1)} %fusion.156, f32[4,256,256]{2,1,0:T(8,128)S(1)} %fusion.183, ...), kind=kOutput, calls=%fused_computation.82 | convolution fusion | flops 1620049920 | bytes 7503872 | tf_op jit(solution)/shard_map/jvp(vmap(ctsh,cshp->cthp))/dot_general | solution.py:36
  192.9 2.8 copy.243
  195.8 3.3 reshape.3075
  199.2 6.0 multiply_reduce_fusion.3
  205.1 5.9 psum.84
  211.1 5.9 fusion.48
  217.1 5.6 psum.85
  222.7 6.8 multiply_reduce_fusion.1
  229.5 3.2 transpose.163
  232.7 3.2 transpose.159
  235.9 3.5 multiply_reduce_fusion.2
  239.4 6.9 fusion.97
  246.3 14.7 %fusion.7 = (f32[4,256,8]{1,2,0:T(8,128)}, f32[4,256,8]{1,2,0:T(8,128)}, f32[4,256,8]{1,2,0:T(8,128)}, f32[4,256,256]{2,1,0:T(8,128)S(1)}) fusion(f32[4,256,8]{1,2,0:T(8,128)S(1)} %compare_select_fusion.5, f32[4,256,8]{1,2,0:T(8,128)S(1)} %fusion.156, f32[4,256,256]{2,1,0:T(8,128)} %copy-done.33, pred[256,256]{1,0:T(8,128)(4,1)S(1)} %copy-done.40, ...), kind=kOutput, calls=%fused_computation.24 | convolution fusion | flops 1637588992 | bytes 6520832 | tf_op jit(solution)/shard_map/transpose(jvp(vmap(ctsh,cshp->cthp)))/dot_general | solution.py:36
  262.9 3.1 fusion.92
  269.7 16.0 %while.35 = (s32[]{:T(128)}, f32[1,8,128,64]{3,2,1,0:T(8,128)S(1)}, f32[4,1,8]{2,1,0:T(1,128)S(1)}, f32[4,1,8,128,64]{4,3,2,1,0:T(8,128)}, f32[4,1,8,128,64]{3,4...) while((s32[]{:T(128)}, f32[1,8,128,64]{3,2,1,0:T(8,128)S(1)}, ...), condition=%wide.region_12.13_spmd.clone, body=%wide.region_10.12_spmd.clone.sunk | while | flops 393212 | bytes 2884888 | solution.py:47
  285.7 6.7 fusion.60
  292.5 2.1 fusion.108
  294.9 8.9 %bitcast_add_fusion.2 = f32[1,4,256,8,64]{2,4,3,1,0:T(8,128)S(1)} fusion(f32[4,8,64,256]{3,2,1,0:T(8,128)} %fusion.60, f32[4,256,8]{1,2,0:T(8,128)S(1)} %copy-done.55, f32[4,256,8]{1,2,0:T(8,128)S(1)} %copy-done.57, f32[4,256,256]{2,1,0:T(8,128)} %copy-done.33, pred[256,256]{1,0:T(8,128)(4,1)S(1)} %copy-done.41, f32[1,4,256,8,64]{2,1,4,3,0:T(4,128)} %transpose.163, ...), kind=kOutput, calls=%fused_computation.81 | convolution fusion | flops 1620049920 | bytes 7503872 | tf_op jit(solution)/shard_map/transpose(jvp(vmap(ctsh,cshp->cthp)))/dot_general | solution.py:36
  303.9 2.7 copy.251
  306.7 2.8 fusion.45
  309.8 10.1 %reduce-window.16 = f32[1,4,8,2,128]{4,2,3,1,0:T(8,128)S(1)} reduce-window(f32[1,4,8,2,128]{4,2,3,1,0:T(8,128)S(1)} %fusion.151, f32[]{:T(128)} %constant.106.clone.1), window={size=1x1x1x1x128 pad=0_0x0_0x0_0x0_0x0_127}, to_apply=%region_19.20 | reduce-window | flops 1040384 | bytes 65540 | tf_op jit(solution)/shard_map/reduce-window.2
  321.2 3.3 reshape.3080
  324.6 5.9 broadcast_multiply_fusion
  330.5 2.4 multiply_reduce_fusion.6
  334.3 26.4 %all-reduce.29 = bf16[1024,1,256]{0,2,1:T(8,128)(2,1)} all-reduce(f32[1024,1,256]{0,2,1:T(8,128)S(1)} %pad_add_fusion.3), channel_id=1, replica_groups=mesh['dp'=8,'tensor'=4] {'tensor'}, use_global_device_ids=true, to_apply=%region_23.24 | all-reduce | flops 262144 | bytes 1572864 | tf_op jit(solution)/shard_map/psum | solution.py:185
  360.6 2.2 broadcast_multiply_fusion.1
  367.1 2.9 fusion.25
  370.0 2.4 copy-done.19
  373.6 4.8 slice.141
  378.4 7.2 copy.270
  386.6 7.2 fusion.34
  394.5 4.6 convert_bitcast_fusion
  400.6 4.9 fusion.67
  407.4 3.3 reshape.3094
  411.0 6.7 fusion.52
  417.8 38.4 %all-reduce.24 = (f32[4,512]{1,0:T(4,128)}, f32[512]{0:T(512)}, f32[8]{0:T(128)}, f32[8]{0:T(128)}, f32[8]{0:T(128)}, /*index=5*/f32[512]{0:T(512)}) all-reduce(f32[4,512]{1,0:T(4,128)S(1)} %pad_add_fusion.6, f32[512]{0:T(512)S(1)} %reduce_sum.298, f32[8]{0:T(128)S(1)} %get-tuple-element.399, ...), channel_id=1, replica_groups=mesh['dp'=8,'tensor'=4] {'dp'}, use_global_device_ids=true, to_apply=%region_34.35 | all-reduce | flops 3096 | bytes 24768 | tf_op jit(solution)/shard_map/psum | solution.py:225
  457.8 140.2 %all-reduce.28.cloned.1.call-done = f32[1024,2,512]{2,1,0:T(2,128)} async-done(((f32[1024,2,512]{2,1,0:T(2,128)}), f32[1024,2,512]{2,1,0:T(2,128)}) %all-reduce.28.cloned.1.call-update) | async-done | bytes 4194320
  599.9 44.3 %reduce-scatter.8.cloned.1.call-done = f32[256,1,1024]{2,0,1:T(8,128)} async-done(((f32[1024,1,1024]{2,0,1:T(8,128)}), f32[256,1,1024]{2,0,1:T(8,128)}) %reduce-scatter.8.cloned.1.call-update) | async-done | bytes 1048592 | tf_op jit(solution)/shard_map/reduce_scatter | solution.py:201
  646.0 31.8 %reduce-scatter.6.cloned.1.call-done = bf16[256,1,1024]{2,0,1:T(8,128)(2,1)} async-done(((bf16[1024,1,1024]{2,0,1:T(8,128)(2,1)}), bf16[256,1,1024]{2,0,1:T(8,128)(2,1)}) %reduce-scatter.6.cloned.1.call-update) | async-done | bytes 524304 | tf_op jit(solution)/shard_map/reduce_scatter | solution.py:147
  683.5 39.5 %all-reduce.23 = (f32[1024]{0:T(1024)}, f32[4,256]{1,0:T(4,128)}, f32[256]{0:T(256)}) all-reduce(f32[1024]{0:T(1024)S(1)} %get-tuple-element.394, f32[4,256]{1,0:T(4,128)S(1)} %pad_add_fusion.7, f32[256]{0:T(256)S(1)} %get-tuple-element.396), channel_id=1, replica_groups=mesh['dp'=8,'tensor'=4] {'dp','tensor'}, use_global_device_ids=true, to_apply=%region_26.27 | all-reduce | flops 2304 | bytes 18432 | tf_op jit(solution)/shard_map/psum | solution.py:228
  723.0 13.4 %reduce-scatter.10.cloned.1.call-done = f32[128,8]{0,1:T(8,128)} async-done(((f32[1024,8]{0,1:T(8,128)}), f32[128,8]{0,1:T(8,128)}) %reduce-scatter.10.cloned.1.call-update) | async-done | bytes 4112 | tf_op jit(solution)/shard_map/reduce_scatter | solution.py:221
  736.4 72.2 %reduce-scatter.14.cloned.1.call-done = f32[512,128]{1,0:T(8,128)} async-done(((f32[512,1024]{1,0:T(8,128)}), f32[512,128]{1,0:T(8,128)}) %reduce-scatter.14.cloned.1.call-update) | async-done | bytes 262160 | tf_op jit(solution)/shard_map/reduce_scatter | solution.py:223
  (367 shorter events, 88.0 us)
Async XLA Ops:
  7.2 6.7 copy-start.100
  7.2 6.7 copy-start.71
  7.2 6.8 copy-start.88
  7.2 7.0 copy-start.86
  7.2 7.0 copy-start.94
  7.2 35.2 %copy-start.85 = (f32[4,512]{1,0:T(4,128)S(1)}, f32[4,512]{1,0:T(4,128)}, u32[]{:S(2)}) copy-start(f32[4,512]{1,0:T(4,128)} %param.24) | copy-start | bytes 24580
  7.2 36.3 %copy-start.39 = (bf16[128,256]{1,0:T(8,128)(2,1)S(1)}, bf16[128,256]{1,0:T(8,128)(2,1)}, u32[]{:S(2)}) copy-start(bf16[128,256]{1,0:T(8,128)(2,1)} %param.23) | copy-start | bytes 196612
  7.3 69.0 %all-gather.7.cloned.1.call-start = ((), (), s32[]{:S(2)}) async-start(), calls=%async_computation.6 | async-start | bytes 2359296 | tf_op jit(solution)/shard_map/all_gather | solution.py:113
  8.0 83.9 %all-gather.5.cloned.1.call-start = ((), (), s32[]{:S(2)}) async-start(), calls=%async_computation.5 | async-start | bytes 2621440 | tf_op jit(solution)/shard_map/all_gather | solution.py:109
  11.9 199.2 %all-gather.9.cloned.1.call-start = ((), (), s32[]{:S(2)}) async-start(), calls=%async_computation.7 | async-start | bytes 1179648 | tf_op jit(solution)/shard_map/all_gather | solution.py:116
  12.6 198.5 %all-gather.11.cloned.1.call-start = ((), (), s32[]{:S(2)}) async-start(), calls=%async_computation.9 | async-start | bytes 2621440 | tf_op jit(solution)/shard_map/all_gather | solution.py:162
  13.2 443.0 %reduce-scatter.12.cloned.1.call-start = ((), (), s32[]{:S(2)}) async-start(), calls=%async_computation.12 | async-start | bytes 1179648 | tf_op jit(solution)/shard_map/reduce_scatter | solution.py:222
  13.9 92.6 %copy-start.92 = (f32[8]{0:T(128)}, f32[8]{0:T(128)S(1)}, u32[]{:S(2)}) copy-start(f32[8]{0:T(128)S(1)} %exponential_negate_fusion) | copy-start | bytes 100
  14.2 95.9 %copy-start.76 = (f32[1,256]{1,0:T(1,128)}, f32[1,256]{1,0:T(1,128)S(1)}, u32[]{:S(2)}) copy-start(f32[1,256]{1,0:T(1,128)S(1)} %get-tuple-element.475) | copy-start | bytes 3076
  14.2 95.9 %copy-start.78 = (f32[1,256]{1,0:T(1,128)}, f32[1,256]{1,0:T(1,128)S(1)}, u32[]{:S(2)}) copy-start(f32[1,256]{1,0:T(1,128)S(1)} %get-tuple-element.476) | copy-start | bytes 3076
  14.2 95.9 %copy-start.80 = (f32[1,256]{1,0:T(1,128)}, f32[1,256]{1,0:T(1,128)S(1)}, u32[]{:S(2)}) copy-start(f32[1,256]{1,0:T(1,128)S(1)} %get-tuple-element.477) | copy-start | bytes 3076
  14.2 95.9 %copy-start.82 = (f32[1,256]{1,0:T(1,128)}, f32[1,256]{1,0:T(1,128)S(1)}, u32[]{:S(2)}) copy-start(f32[1,256]{1,0:T(1,128)S(1)} %get-tuple-element.478) | copy-start | bytes 3076
  43.2 86.6 %copy-start.42 = (f32[8,64]{1,0:T(8,128)}, f32[8,64]{1,0:T(8,128)S(1)}, u32[]{:S(2)}) copy-start(f32[8,64]{1,0:T(8,128)S(1)} %mul.1265) | copy-start | bytes 6148
  43.3 86.5 %copy-start.44 = (f32[8,64]{1,0:T(8,128)}, f32[8,64]{1,0:T(8,128)S(1)}, u32[]{:S(2)}) copy-start(f32[8,64]{1,0:T(8,128)S(1)} %mul.1268) | copy-start | bytes 6148
  43.4 86.4 %copy-start.46 = (f32[8,64]{1,0:T(8,128)}, f32[8,64]{1,0:T(8,128)S(1)}, u32[]{:S(2)}) copy-start(f32[8,64]{1,0:T(8,128)S(1)} %mul.1271) | copy-start | bytes 6148
  43.6 48.3 %copy-start.36 = (bf16[1024,8]{1,0:T(8,128)(2,1)}, bf16[1024,8]{1,0:T(8,128)(2,1)S(1)}, u32[]{:S(2)}) copy-start(bf16[1024,8]{1,0:T(8,128)(2,1)S(1)} %copy.229) | copy-start | bytes 49156
  76.3 15.6 %copy-start.27 = (bf16[1024,256]{1,0:T(8,128)(2,1)}, bf16[1024,256]{1,0:T(8,128)(2,1)S(1)}, u32[]{:S(2)}) copy-start(bf16[1024,256]{1,0:T(8,128)(2,1)S(1)} %all_gather.24) | copy-start | bytes 1572868
  102.2 8.0 copy-start.98
  129.8 5.7 copy-start.20
  179.3 67.0 %copy-start.54 = (f32[4,256,8]{1,2,0:T(8,128)}, f32[4,256,8]{1,2,0:T(8,128)S(1)}, u32[]{:S(2)}) copy-start(f32[4,256,8]{1,2,0:T(8,128)S(1)} %compare_select_fusion.5) | copy-start | bytes 98308
  179.4 66.9 %copy-start.56 = (f32[4,256,8]{1,2,0:T(8,128)}, f32[4,256,8]{1,2,0:T(8,128)S(1)}, u32[]{:S(2)}) copy-start(f32[4,256,8]{1,2,0:T(8,128)S(1)} %fusion.156) | copy-start | bytes 98308
  181.6 11.3 %copy-start.33 = (f32[4,256,256]{2,1,0:T(8,128)}, f32[4,256,256]{2,1,0:T(8,128)S(1)}, u32[]{:S(2)}) copy-start(f32[4,256,256]{2,1,0:T(8,128)S(1)} %fusion.183) | copy-start | bytes 3145732
  183.5 9.5 %copy-start.16 = (f32[4,256,512]{1,2,0}, f32[4,256,512]{1,2,0:S(1)}, u32[]{:S(2)}) copy-start(f32[4,256,512]{1,2,0:S(1)} %fusion.184) | copy-start | bytes 6291460
  199.2 12.0 %copy-start.90 = (f32[512]{0:T(512)S(1)}, f32[512]{0:T(512)}, u32[]{:S(2)}) copy-start(f32[512]{0:T(512)} %param.31) | copy-start | bytes 6148
  211.1 11.6 %copy-start.48 = (f32[1024,1]{0,1:T(1,128)}, f32[1024,1]{0,1:T(1,128)S(1)}, u32[]{:S(2)}) copy-start(f32[1024,1]{0,1:T(1,128)S(1)} %add_rsqrt_fusion) | copy-start | bytes 12292
  239.4 6.9 copy-start.5
  239.4 6.9 copy-start.13
  285.7 6.7 copy-start.6
  285.7 6.7 copy-start.7
  285.7 6.7 copy-start.31
  294.8 11.7 %copy-start.11 = (f32[1,4,256,8,64]{2,1,4,3,0:T(4,128)S(1)}, f32[1,4,256,8,64]{2,1,4,3,0:T(4,128)}, u32[]{:S(2)}) copy-start(f32[1,4,256,8,64]{2,1,4,3,0:T(4,128)} %transpose.167) | copy-start | bytes 6291460
  294.9 11.7 %copy-start.12 = (f32[1,4,256,8,64]{2,1,4,3,0:T(4,128)S(1)}, f32[1,4,256,8,64]{2,1,4,3,0:T(4,128)}, u32[]{:S(2)}) copy-start(f32[1,4,256,8,64]{2,1,4,3,0:T(4,128)} %transpose.168) | copy-start | bytes 6291460
  294.9 11.7 %copy-start.14 = (f32[1,4,256,8,64]{2,1,4,3,0:T(4,128)S(1)}, f32[1,4,256,8,64]{2,1,4,3,0:T(4,128)}, u32[]{:S(2)}) copy-start(f32[1,4,256,8,64]{2,1,4,3,0:T(4,128)} %transpose.163) | copy-start | bytes 6291460
  294.9 11.7 %copy-start.15 = (f32[4,8,64,256]{3,2,1,0:T(8,128)S(1)}, f32[4,8,64,256]{3,2,1,0:T(8,128)}, u32[]{:S(2)}) copy-start(f32[4,8,64,256]{3,2,1,0:T(8,128)} %fusion.60) | copy-start | bytes 6291460
  294.9 11.7 %copy-start.43 = (f32[8,64]{1,0:T(8,128)S(1)}, f32[8,64]{1,0:T(8,128)}, u32[]{:S(2)}) copy-start(f32[8,64]{1,0:T(8,128)} %copy-done.42) | copy-start | bytes 6148
  294.9 11.7 %copy-start.45 = (f32[8,64]{1,0:T(8,128)S(1)}, f32[8,64]{1,0:T(8,128)}, u32[]{:S(2)}) copy-start(f32[8,64]{1,0:T(8,128)} %copy-done.44) | copy-start | bytes 6148
  294.9 11.7 %copy-start.47 = (f32[8,64]{1,0:T(8,128)S(1)}, f32[8,64]{1,0:T(8,128)}, u32[]{:S(2)}) copy-start(f32[8,64]{1,0:T(8,128)} %copy-done.46) | copy-start | bytes 6148
  294.9 11.7 %copy-start.89 = (f32[8]{0:T(128)S(1)}, f32[8]{0:T(128)}, u32[]{:S(2)}) copy-start(f32[8]{0:T(128)} %param.30) | copy-start | bytes 100
  306.7 13.4 %copy-start.53 = (f32[4,256,8]{1,2,0:T(8,128)S(1)}, f32[4,256,8]{1,2,0:T(8,128)}, u32[]{:S(2)}) copy-start(f32[4,256,8]{1,2,0:T(8,128)} %get-tuple-element.381) | copy-start | bytes 98308
  306.7 13.4 %copy-start.93 = (f32[8]{0:T(128)S(1)}, f32[8]{0:T(128)}, u32[]{:S(2)}) copy-start(f32[8]{0:T(128)} %copy-done.92) | copy-start | bytes 100
  324.5 6.0 copy-start.8
  324.5 6.0 copy-start.24
  324.5 6.0 copy-start.29
  333.3 27.3 %copy-start.61 = (f32[1,512]{1,0:T(1,128)S(1)}, f32[1,512]{1,0:T(1,128)}, u32[]{:S(2)}) copy-start(f32[1,512]{1,0:T(1,128)} %get-tuple-element.471) | copy-start | bytes 6148
  333.4 27.3 %copy-start.63 = (f32[1,512]{1,0:T(1,128)S(1)}, f32[1,512]{1,0:T(1,128)}, u32[]{:S(2)}) copy-start(f32[1,512]{1,0:T(1,128)} %get-tuple-element.472) | copy-start | bytes 6148
  333.4 27.3 %copy-start.65 = (f32[1,512]{1,0:T(1,128)S(1)}, f32[1,512]{1,0:T(1,128)}, u32[]{:S(2)}) copy-start(f32[1,512]{1,0:T(1,128)} %get-tuple-element.473) | copy-start | bytes 6148
  364.8 5.2 copy-start.30
  373.5 224.5 %all-reduce.28.cloned.1.call-start = ((), (), s32[]{:S(2)}) async-start(), calls=%async_computation.14 | async-start | bytes 8388608
  385.7 258.5 %reduce-scatter.8.cloned.1.call-start = ((), (), s32[]{:S(2)}) async-start(), calls=%async_computation.10 | async-start | bytes 5242880 | tf_op jit(solution)/shard_map/reduce_scatter | solution.py:201
  393.8 284.0 %reduce-scatter.6.cloned.1.call-start = ((), (), s32[]{:S(2)}) async-start(), calls=%async_computation.8 | async-start | bytes 2621440 | tf_op jit(solution)/shard_map/reduce_scatter | solution.py:147
  399.1 337.3 %reduce-scatter.10.cloned.1.call-start = ((), (), s32[]{:S(2)}) async-start(), calls=%async_computation.11 | async-start | bytes 36864 | tf_op jit(solution)/shard_map/reduce_scatter | solution.py:221
  400.5 408.0 %reduce-scatter.14.cloned.1.call-start = ((), (), s32[]{:S(2)}) async-start(), calls=%async_computation.13 | async-start | bytes 2359296 | tf_op jit(solution)/shard_map/reduce_scatter | solution.py:223
  410.9 6.8 copy-start.101
  411.0 6.8 copy-start.95
  411.0 233.2 %copy-start.18 = (bf16[256,1,1024]{2,0,1:T(8,128)(2,1)S(1)}, bf16[256,1,1024]{2,0,1:T(8,128)(2,1)}, u32[]{:S(2)}) copy-start(bf16[256,1,1024]{2,0,1:T(8,128)(2,1)} %param.19) | copy-start | bytes 1572868
  411.0 233.2 %copy-start.28 = (bf16[1024,256]{1,0:T(8,128)(2,1)S(1)}, bf16[1024,256]{1,0:T(8,128)(2,1)}, u32[]{:S(2)}) copy-start(bf16[1024,256]{1,0:T(8,128)(2,1)} %copy-done.27) | copy-start | bytes 1572868
  411.0 233.1 %copy-start.52 = (f32[1024]{0:T(1024)S(1)}, f32[1024]{0:T(1024)}, u32[]{:S(2)}) copy-start(f32[1024]{0:T(1024)} %param.20) | copy-start | bytes 12292
  411.0 233.1 %copy-start.75 = (f32[256]{0:T(256)S(1)}, f32[256]{0:T(256)}, u32[]{:S(2)}) copy-start(f32[256]{0:T(256)} %copy-done.74) | copy-start | bytes 3076
  457.8 220.0 %copy-start.87 = (f32[256]{0:T(256)S(1)}, f32[256]{0:T(256)}, u32[]{:S(2)}) copy-start(f32[256]{0:T(256)} %get-tuple-element.479) | copy-start | bytes 3076
  (55 other events, 136.6 us)
Sparse Core Ops, SparseCore 0:
  10.2 57.3 all-gather.6
  69.7 22.0 all-gather.4
  93.9 39.3 all-gather.8
  134.7 21.5 all-gather.10
  373.7 65.4 reduce-scatter.11
  442.7 155.2 all-reduce.27
  600.5 43.5 reduce-scatter.7
  646.6 31.1 reduce-scatter.5
  681.5 54.8 reduce-scatter.9
  740.4 68.1 reduce-scatter.13
where the time goes:
time: 822 us; the launch traced here: 816 us
  waiting for transfers between devices  315 us (38%)
  blocking collectives  177 us (22%)
  local copies, waits for them, and re-layouts  124 us (15%)
  matrix products  94.3 us (11%)
  other arithmetic  87.5 us (11%)
  between operations  16.3 us (2%)
    unnamed x11, waiting for transfers between devices  142 us
    reduce_scatter x1, waiting for transfers between devices, per_device(): lax.psum_scatter(grad_out_part, 'dp', scatter_dimension=1, tiled=True)  72.2 us
    reduce_scatter x1, waiting for transfers between devices, per_device(): lax.psum_scatter(jnp.einsum('lsc,dc->lsd', piece, head_weights, preferred...  44.3 us
    psum x1, blocking collectives, per_device(): lax.psum((pre_gain_part, grad_kbc, grad_bbc), ('dp', 'tensor'))  39.5 us
    psum x1, blocking collectives, per_device(): lax.psum((grad_kx, grad_bx, grad_dtb, grad_alog, grad_skip, gate_gain_par...  38.4 us
    dot_general x3, matrix products, scan_heads(): jnp.einsum('ctsh,cshp->cthp', weights, inputs_block, precision=highest)  32.9 us
    all_gather x1, blocking collectives, per_device(): lax.all_gather(w_bc, 'dp', axis=0, tiled=True)  32.7 us
    reduce_scatter x1, waiting for transfers between devices, per_device(): lax.psum_scatter(jnp.einsum('lsi,id->lsd', piece, full_out, preferred_ele...  31.8 us
  transfers between devices with their start and end apart: 10, of which 6 were waited for; matrix products, arithmetic and copies ran while one was open for 21% of the time, Pallas kernels for 0%

commit v1 on v0

v1 whole, which is shorter than its diff:
```python
import jax
import jax.numpy as jnp
from jax import lax
from jax.experimental import pallas as pl
from jax.experimental.pallas import tpu as pltpu
from jax.sharding import PartitionSpec as P


CHUNK = 128
ROWS = 256
LANES = 128
epsilon = 1e-05
highest = lax.Precision.HIGHEST
f32 = jnp.float32
bf16 = jnp.bfloat16

NN = (((1,), (0,)), ((), ()))
NT = (((1,), (1,)), ((), ()))
TN = (((0,), (0,)), ((), ()))


def mm(a, b, dims=NN):
    return lax.dot_general(a, b, dims, preferred_element_type=f32)


def halves(v):
    high = v.astype(bf16)
    return high, (v - high.astype(f32)).astype(bf16)


def fine(a, b, dims=NN):
    a_high, a_low = halves(a)
    b_high, b_low = halves(b)
    return mm(a_high, b_high, dims) + mm(a_high, b_low, dims) + mm(a_low, b_high, dims)


def swap(value, axis, bits):
    size = lax.axis_size(axis)
    return lax.ppermute(value, axis, [(i, i ^ bits) for i in range(size)])


def gather(value, axis):
    size = lax.axis_size(axis)
    pieces = {0: value}
    for k in range(2, size, 2):
        pieces[k] = swap(value, axis, k)
    if size > 1:
        for k in range(0, size, 2):
            pieces[k ^ 1] = swap(pieces[k], axis, 1)
    return [pieces[k] for k in range(size)]


def near_first(parts, axis):
    size = lax.axis_size(axis)
    rows = parts.shape[0] // size

    def piece(k):
        return parts[k * rows : (k + 1) * rows]

    terms = [piece(0)]
    if size == 1:
        return terms
    for k in range(size - 2, 0, -2):
        other = swap(piece(k ^ 1), axis, 1)
        both = piece(k).astype(f32) + other.astype(f32)
        terms.append(swap(both.astype(bf16), axis, k))
    terms.append(swap(piece(1), axis, 1))
    return terms


def far_first(parts, axis):
    size = lax.axis_size(axis)
    rows = parts.shape[0] // size
    if size == 1:
        return [parts]
    pairs = [parts[: 2 * rows]]
    for k in range(2, size, 2):
        pairs.append(swap(parts[k * rows : (k + 2) * rows], axis, k))
    other = sum(pair[rows:].astype(f32) for pair in pairs).astype(bf16)
    return [pair[:rows] for pair in pairs] + [swap(other, axis, 1)]


def total_of(terms):
    return sum(term.astype(f32) for term in terms)


def direct_terms(value, axis):
    terms = [value]
    for k in range(1, lax.axis_size(axis)):
        terms.append(swap(value, axis, k))
    return terms


def all_sum(value, axis):
    size = lax.axis_size(axis)
    if size == 1:
        return value
    value = value + swap(value, axis, 1)
    total = value
    for k in range(2, size, 2):
        total = total + swap(value, axis, k)
    return total


def softplus(v):
    return jnp.maximum(v, 0.0) + jnp.log1p(jnp.exp(-jnp.abs(v)))


def lower(size):
    return lax.broadcasted_iota(jnp.int32, (size, size), 0) >= lax.broadcasted_iota(
        jnp.int32, (size, size), 1
    )


def pick(values, lane_head):
    out = values[0]
    for j in range(1, len(values)):
        out = jnp.where(lane_head == j, values[j], out)
    return out


def take(out, refs, which):
    for k, ref in enumerate(refs):

        @pl.when(which == k)
        def _(ref=ref):
            out[...] = ref[...]


def join(out, refs):
    rows = refs[0].shape[0]
    for k, ref in enumerate(refs):
        out[k * rows : (k + 1) * rows, :] = ref[...]


def forward_kernel(width, head_dim, count, pieces, per, start):
    per_group = LANES // head_dim

    def kernel(place, *refs):
        token_refs, refs = refs[:count], refs[count:]
        weight_refs, refs = refs[:pieces], refs[pieces:]
        taps_x, taps_bc, per_head, skip, *carried = refs[:7]
        refs = refs[7 + (0 if start == 0 else 7) :]
        pre_x, pre_bc, raw_x, raw_bc, dt_out, mixed, before, state, halo_x, halo_bc = refs[:10]
        if start == 0:
            weights, refs = refs[10], refs[11:]
        else:
            weights, refs = weight_refs[0], refs[10:]
        ext_x, ext_bc, normed = refs
        size = normed.shape[0]
        take(normed, token_refs, ((pl.program_id(0) + start) // per) ^ place[0])
        inner = mixed.shape[1]
        twice = pre_bc.shape[1]
        states = twice // 2

        @pl.when(pl.program_id(0) == 0)
        def _():
            state[...] = carried[0][...]
            ext_x[0:8, :] = carried[1][...]
            ext_bc[0:8, :] = carried[2][...]
            if start == 0:
                join(weights, weight_refs)

        raw = mm(normed[...], weights[...])

        def conv(ext, values, taps, raw_ref, pre_ref, halo):
            ext[8 : 8 + size, :] = values
            raw_ref[...] = values.astype(bf16)
            total = taps[width : width + 1, :]
            for k in range(width):
                start = 8 - (width - 1) + k
                total = total + taps[k : k + 1, :] * ext[start : start + size, :]
            halo[...] = ext[size : size + 8, :]
            ext[0:8, :] = halo[...]
            pre_ref[...] = total
            return total * jax.nn.sigmoid(total)

        x = conv(ext_x, raw[:, :inner], taps_x, raw_x, pre_x, halo_x)
        bc = conv(ext_bc, raw[:, inner : inner + twice], taps_bc, raw_bc, pre_bc, halo_bc)
        dt = raw[:, inner + twice :] + per_head[0:1, :]
        dt_out[...] = dt
        steps = softplus(dt)
        below = lower(size)
        logs = lax.dot_general(
            below.astype(f32), steps * per_head[1:2, :], NN, precision=highest,
            preferred_element_type=f32,
        )
        logs_t = logs.T
        keys = bc[:, :states]
        keys_t = keys.T
        queries = bc[:, states:]
        scores = jnp.where(below, fine(queries, keys, NT), 0.0)
        lane_head = lax.broadcasted_iota(jnp.int32, (size, LANES), 1) // head_dim
        for group in range(inner // LANES):
            lanes = slice(group * LANES, (group + 1) * LANES)
            x_g = x[:, lanes]
            heads = [group * per_group + j for j in range(per_group)]
            step_e = pick(
                [jnp.broadcast_to(steps[:, h : h + 1], (size, LANES)) for h in heads], lane_head
            )
            log_e = pick(
                [jnp.broadcast_to(logs[:, h : h + 1], (size, LANES)) for h in heads], lane_head
            )
            xs = x_g * step_e
            total = skip[0:1, lanes] * x_g
            for j, h in enumerate(heads):
                gap = logs[:, h : h + 1] - logs_t[h : h + 1, :]
                weights_h = scores * jnp.exp(jnp.minimum(gap, 0.0))
                total = total + fine(weights_h, jnp.where(lane_head == j, xs, 0.0))
            old = state[:, lanes]
            before[0, :, lanes] = old.astype(bf16)
            total = total + jnp.exp(log_e) * fine(queries, old)
            mixed[:, lanes] = total
            last = log_e[size - 1 : size, :]
            fresh = fine(keys_t, jnp.exp(last - log_e) * xs)
            state[:, lanes] = jnp.exp(last) * old + fresh

    return kernel


def backward_kernel(width, head_dim, resumed):
    per_group = LANES // head_dim

    def kernel(place, *refs):
        d_mixed, pre_x, pre_bc, raw_x, raw_bc, dt_in, mixed, before, *refs = refs
        taps_x, taps_bc, per_head, skip, *refs = refs
        carried, refs = refs[:7], refs[7 + resumed :]
        columns, *results, ext_x, ext_bc = refs
        grad_x, grad_bc, grad_head, d_state, after, halo_x, halo_bc = results
        size = d_mixed.shape[0]
        inner = d_mixed.shape[1]
        twice = pre_bc.shape[1]
        states = twice // 2

        @pl.when(pl.program_id(0) == 0)
        def _():
            for result, value in zip(results, carried):
                result[...] = value[...]
            ext_x[size : size + 8, :] = halo_x[...]
            ext_bc[size : size + 8, :] = halo_bc[...]

        dt = dt_in[...]
        steps = softplus(dt)
        rates = per_head[1:2, :]
        below = lower(size)
        logs = lax.dot_general(
            below.astype(f32), steps * rates, NN, precision=highest, preferred_element_type=f32
        )
        logs_t = logs.T
        p_bc = pre_bc[...]
        sig_bc = jax.nn.sigmoid(p_bc)
        bc = p_bc * sig_bc
        keys = bc[:, :states].astype(bf16)
        queries = bc[:, states:].astype(bf16)
        queries_t = bc[:, states:].T
        above = lax.broadcasted_iota(jnp.int32, (size, size), 0) <= lax.broadcasted_iota(
            jnp.int32, (size, size), 1
        )
        scores_t = jnp.where(above, mm(keys, queries, NT), 0.0)
        lane_head = lax.broadcasted_iota(jnp.int32, (size, LANES), 1) // head_dim
        d_scores_t = jnp.zeros((size, size), f32)
        d_keys = jnp.zeros((size, states), f32)
        d_queries = jnp.zeros((size, states), f32)
        head_of = lax.broadcasted_iota(jnp.int32, (LANES, LANES), 0) // head_dim
        lane_of = lax.broadcasted_iota(jnp.int32, (LANES, LANES), 1)
        log_sum = jnp.zeros((size, LANES), f32)
        step_sum = jnp.zeros((size, LANES), f32)
        end_sum = jnp.zeros((8, LANES), f32)
        for group in range(inner // LANES):
            lanes = slice(group * LANES, (group + 1) * LANES)
            heads = [group * per_group + j for j in range(per_group)]
            p_x = pre_x[:, lanes]
            sig_x = jax.nn.sigmoid(p_x)
            x_g = p_x * sig_x
            dy = d_mixed[:, lanes]
            step_e = pick(
                [jnp.broadcast_to(steps[:, h : h + 1], (size, LANES)) for h in heads], lane_head
            )
            log_e = pick(
                [jnp.broadcast_to(logs[:, h : h + 1], (size, LANES)) for h in heads], lane_head
            )
            xs = x_g * step_e
            last = log_e[size - 1 : size, :]
            fade = jnp.exp(last - log_e)
            old = before[0, :, lanes]
            d_new = d_state[:, lanes]
            d_new_half = d_new.astype(bf16)
            dxs = fade * mm(keys, d_new_half)
            for j, h in enumerate(heads):
                mine = lane_head == j
                gap = logs_t[h : h + 1, :] - logs[:, h : h + 1]
                decay = jnp.exp(jnp.minimum(gap, 0.0))
                dxs = dxs + mm(
                    (scores_t * decay).astype(bf16), jnp.where(mine, dy, 0.0).astype(bf16)
                )
                d_scores_t = d_scores_t + decay * fine(jnp.where(mine, xs, 0.0), dy, NT)
            e_dy = jnp.exp(log_e) * dy
            d_queries = d_queries + sum(mm(half, old, NT) for half in halves(e_dy))
            d_keys = d_keys + fine(fade * xs, d_new, NT)
            skip_g = skip[0:1, lanes]
            log_lane = dy * (mixed[:, lanes] - skip_g * x_g) - xs * dxs
            step_lane = dxs * x_g
            end_lane = jnp.sum(d_new * after[:, lanes], axis=0, keepdims=True)
            to_head = (head_of + group * per_group == lane_of).astype(bf16)
            for high_low in halves(log_lane):
                log_sum = log_sum + mm(high_low, to_head)
            for high_low in halves(step_lane):
                step_sum = step_sum + mm(high_low, to_head)
            for high_low in halves(jnp.broadcast_to(end_lane, (8, LANES))):
                end_sum = end_sum + mm(high_low, to_head)
            d_state[:, lanes] = jnp.exp(last) * d_new + fine(queries_t, e_dy)
            after[:, lanes] = old.astype(f32)
            grad_x[width + 1 : width + 2, lanes] += jnp.sum(dy * x_g, axis=0, keepdims=True)
            dx = dxs * step_e + skip_g * dy
            d_pre = dx * (sig_x + x_g * (1.0 - sig_x))
            ext_x[0:size, lanes] = d_pre
            grad_x[width : width + 1, lanes] += jnp.sum(d_pre, axis=0, keepdims=True)
            total = jnp.zeros((size, LANES), f32)
            raw = raw_x[:, lanes].astype(f32)
            for k in range(width):
                moved = ext_x[width - 1 - k : width - 1 - k + size, lanes]
                total = total + taps_x[k : k + 1, lanes] * moved
                grad_x[k : k + 1, lanes] += jnp.sum(raw * moved, axis=0, keepdims=True)
            columns[:, lanes] = total.astype(bf16)
            halo_x[:, lanes] = ext_x[0:8, lanes]
            ext_x[size : size + 8, lanes] = halo_x[:, lanes]
        d_scores_t = jnp.where(above, d_scores_t, 0.0)
        d_keys = d_keys + fine(d_scores_t, bc[:, states:])
        d_queries = d_queries + fine(d_scores_t.T, bc[:, :states])
        at_end = lax.broadcasted_iota(jnp.int32, (size, LANES), 0) == size - 1
        d_log = log_sum + jnp.where(at_end, end_sum[0:1, :], 0.0)
        d_rate = lax.dot_general(
            above.astype(f32), d_log, NN, precision=highest, preferred_element_type=f32
        )
        grad_head[1:2, :] += rates * jnp.sum(steps * d_rate, axis=0, keepdims=True)
        d_dt = (step_sum + rates * d_rate) * jax.nn.sigmoid(dt)
        grad_head[0:1, :] += jnp.sum(d_dt, axis=0, keepdims=True)
        columns[:, inner + twice :] = d_dt.astype(bf16)
        slope = sig_bc + bc * (1.0 - sig_bc)
        ext_bc[0:size, :states] = d_keys * slope[:, :states]
        ext_bc[0:size, states:] = d_queries * slope[:, states:]
        grad_bc[width : width + 1, :] += jnp.sum(ext_bc[0:size, :], axis=0, keepdims=True)
        total = jnp.zeros((size, twice), f32)
        raw = raw_bc[...].astype(f32)
        for k in range(width):
            moved = ext_bc[width - 1 - k : width - 1 - k + size, :]
            total = total + taps_bc[k : k + 1, :] * moved
            grad_bc[k : k + 1, :] += jnp.sum(raw * moved, axis=0, keepdims=True)
        columns[:, inner : inner + twice] = total.astype(bf16)
        halo_bc[...] = ext_bc[0:8, :]
        ext_bc[size : size + 8, :] = halo_bc[...]

    return kernel


def gate_kernel(count, pieces, parts):
    def kernel(place, *refs):
        token_refs, refs = refs[:count], refs[count:]
        weight_refs, refs = refs[:pieces], refs[pieces:]
        mixed, gain, gate_raw, grad_scaled, sums, tokens, weights = refs

        @pl.when(pl.program_id(0) == 0)
        def _():
            join(weights, weight_refs)

        take(tokens, token_refs, pl.program_id(0) // parts)
        gate_body(tokens, weights, mixed, gain, gate_raw, grad_scaled, sums)

    return kernel


def gate_body(tokens, weights, mixed, gain, gate_raw, grad_scaled, sums):
    model = weights.shape[0]
    inner = mixed.shape[1]
    gate = mm(tokens[:, :model], weights[:, :inner])
    grads = mm(tokens[:, model:], weights[:, inner:])
    gate_raw[...] = gate
    grad_scaled[...] = grads
    gated = mixed[...] * (gate * jax.nn.sigmoid(gate))
    ones = jnp.ones((8, gated.shape[1]), bf16)
    rows = lax.broadcasted_iota(jnp.int32, sums.shape[1:], 0)
    square = sum(mm(ones, part, NT) for part in halves(gated * gated))
    cross = sum(mm(ones, part, NT) for part in halves(gated * (grads * gain[...])))
    sums[0] = jnp.where(rows == 0, square, cross)


def norm_kernel(inner_total, count):
    def kernel(place, *refs):
        terms, refs = refs[:count], refs[count:]
        gate_raw, grad_scaled, mixed, gain, scaled, d_mixed, d_gate, grad_gain = refs

        @pl.when(pl.program_id(0) == 0)
        def _():
            grad_gain[...] = jnp.zeros(grad_gain.shape, f32)

        total = terms[0][0]
        for term in terms[1:]:
            total = total + term[0]
        column = total.T
        inverse = lax.rsqrt(column[:, 0:1] / inner_total + epsilon)
        pull = inverse * inverse * inverse * (column[:, 1:2] / inner_total)
        gate = gate_raw[...]
        sig = jax.nn.sigmoid(gate)
        act = gate * sig
        mix = mixed[...]
        grads = grad_scaled[...]
        unit = mix * act * inverse
        scaled[...] = (unit * gain[...]).astype(bf16)
        grad_gain[0:1, :] += jnp.sum(grads * unit, axis=0, keepdims=True)
        d_gated = inverse * (grads * gain[...]) - (mix * act) * pull
        d_mixed[...] = d_gated * act
        d_gate[...] = (d_gated * mix * (sig + act * (1.0 - sig))).astype(bf16)

    return kernel


def entry_kernel(blocks):
    def kernel(place, tokens, upstream, gain, out):
        model = tokens.shape[1]
        size = model // blocks
        wide = tokens[...].astype(f32)
        inverse = lax.rsqrt(jnp.mean(wide * wide, axis=-1, keepdims=True) + epsilon)
        normed = (wide * inverse * gain[...]).astype(bf16)
        for k in range(blocks):
            at = pl.multiple_of((place[0] ^ k) * size, size)
            out[:, pl.ds(at, size)] = normed[:, k * size : (k + 1) * size]
            out[:, pl.ds(model + at, size)] = upstream[:, k * size : (k + 1) * size]

    return kernel


def output_kernel(blocks, count):
    def kernel(place, tokens, *refs):
        out = refs[count]
        size = tokens.shape[1] // blocks
        for k in range(blocks):
            at = pl.multiple_of((place[0] ^ k) * size, size)
            total = tokens[:, k * size : (k + 1) * size].astype(f32)
            for term in refs[:count]:
                total = total + term[:, pl.ds(at, size)].astype(f32)
            out[:, 0, k * size : (k + 1) * size] = total

    return kernel


def input_kernel(blocks, count):
    def kernel(place, tokens, upstream, gain, *refs):
        out, grads = refs[count:]
        model = tokens.shape[1]
        size = model // blocks
        wide = tokens[...].astype(f32)
        inverse = lax.rsqrt(jnp.mean(wide * wide, axis=-1, keepdims=True) + epsilon)
        for k in range(blocks):
            at = pl.multiple_of((place[0] ^ k) * size, size)
            total = refs[0][:, pl.ds(at, size)].astype(f32)
            for term in refs[1:count]:
                total = total + term[:, pl.ds(at, size)].astype(f32)
            grads[:, k * size : (k + 1) * size] = total
        weighted = grads[...] * gain[...]
        inner_dot = jnp.mean(weighted * wide, axis=-1, keepdims=True)
        out[:, 0, :] = (
            upstream[...].astype(f32)
            + inverse * weighted
            - wide * (inverse * inverse * inverse * inner_dot)
        )

    return kernel


def normed_kernel(place, tokens, d_gate, columns, w_gate, w_scan, out, grad_gain):
    total = mm(d_gate[...], w_gate[...], NT) + mm(columns[...], w_scan[...], NT)
    out[...] = total.astype(bf16)
    total = total * tokens[...].astype(f32)
    grad_gain[...] = jnp.broadcast_to(jnp.sum(total, axis=0, keepdims=True), grad_gain.shape)


def whole(shape):
    return pl.BlockSpec(shape, lambda c, place: (0,) * len(shape))


def rows_of(size, cols, column=0):
    return pl.BlockSpec((size, cols), lambda c, place: (c, column))


def call(kernel, grid, ins, outs, shapes, scratch=(), aliases=None):
    return pl.pallas_call(
        kernel,
        grid_spec=pltpu.PrefetchScalarGridSpec(
            num_scalar_prefetch=1, grid=(grid,), in_specs=ins, out_specs=outs,
            scratch_shapes=scratch,
        ),
        out_shape=[jax.ShapeDtypeStruct(*one) for one in shapes],
        input_output_aliases=aliases or {},
    )


def exchange_blocks(values, axis, blocks):
    index = lax.axis_index(axis)
    rows, cols = values.shape
    bits = 1
    while bits < blocks:
        split = values.reshape(rows, blocks // (2 * bits), 2, bits * (cols // blocks))
        split = jnp.where((index & bits) != 0, split[:, :, ::-1], split)
        values = split.reshape(rows, cols)
        bits *= 2
    return values


def per_device(
    block_input, pre_gain, w_zx, w_dt, w_bc, conv_x_w, conv_x_b, conv_bc_w, conv_bc_b,
    dt_bias, a_log, d_skip, gate_gain, w_out, cotangent,
):
    rows_local, seqs, model = block_input.shape
    assert seqs == 1
    dp = lax.axis_size("dp")
    tensor = lax.axis_size("tensor")
    length = rows_local * tensor
    inner = w_zx.shape[2]
    twice = w_bc.shape[1]
    states = twice // 2
    heads = w_dt.shape[1]
    head_dim = inner // heads
    width = conv_x_w.shape[0]
    wide_cols = inner + twice + LANES
    inner_total = inner * tensor
    chunk = min(CHUNK, rows_local)
    block = min(ROWS, rows_local)
    chunks = length // chunk
    place_dp = lax.axis_index("dp").astype(jnp.int32).reshape(1)
    place_tensor = lax.axis_index("tensor").astype(jnp.int32).reshape(1)
    narrow = (model // dp) % LANES != 0
    blocks = 1 if narrow else dp
    place_entry = place_dp * 0 if narrow else place_dp

    tokens_local = block_input.reshape(rows_local, model)
    upstream_local = cotangent.reshape(rows_local, model)
    gain_in = pre_gain.reshape(1, model)
    w_scan = jnp.concatenate(
        [w_zx[:, 1, :], w_bc, w_dt, jnp.zeros((w_dt.shape[0], LANES - heads), bf16)], axis=1
    )
    w_late = jnp.concatenate([w_zx[:, 0, :], w_out.T], axis=1)
    (both_local,) = call(
        entry_kernel(blocks), 1,
        [whole((rows_local, model)), whole((rows_local, model)), whole((1, model))],
        [whole((rows_local, 2 * model))],
        [((rows_local, 2 * model), bf16)],
    )(place_entry, tokens_local, upstream_local, gain_in)
    if narrow:
        both_local = jnp.concatenate(
            [exchange_blocks(half, "dp", dp) for half in jnp.split(both_local, 2, axis=1)], axis=1
        )
    scan_pieces = gather(w_scan, "dp")
    token_pieces = gather(both_local, "tensor")
    late_pieces = gather(w_late, "dp")

    def stack(rows, cols):
        rows = [r.reshape(-1, r.shape[-1]) for r in rows]
        packed = jnp.concatenate(rows, axis=0)
        return jnp.pad(packed, ((0, 8 - packed.shape[0]), (0, cols - packed.shape[1])))

    taps_x = stack([conv_x_w, conv_x_b], inner)
    taps_bc = stack([conv_bc_w, conv_bc_b], twice)
    per_head = stack([dt_bias, -jnp.exp(a_log)], LANES)
    skip = jnp.repeat(d_skip, head_dim).reshape(1, inner)
    gain = gate_gain.reshape(1, inner)

    per = rows_local // chunk

    def stored(c, place):
        return ((c // per) ^ place[0]) * per + c % per

    def ahead(cols, start):
        return pl.BlockSpec((chunk, cols), lambda c, place: (stored(c + start, place), 0))

    def back(cols, start):
        return pl.BlockSpec((chunk, cols), lambda c, place: (stored(start - c, place), 0))

    def token_piece(k, start):
        def index(c, place):
            c = c + start
            return jnp.where((c // per) ^ place[0] == k, c % per, 0), 0

        return pl.BlockSpec((chunk, model), index)

    anywhere = pl.BlockSpec(memory_space=pl.ANY)
    calls = 2 if chunks % 2 == 0 else 1
    span = chunks // calls
    carry_shapes = [((states, inner), f32), ((8, inner), f32), ((8, twice), f32)]
    carry = [jnp.zeros(*one) for one in carry_shapes]
    saved, weights = [], scan_pieces
    for start in range(0, chunks, span):
        results = call(
            forward_kernel(width, head_dim, tensor, len(weights), per, start),
            span,
            [token_piece(k, start) for k in range(tensor)]
            + [whole(one.shape) for one in weights]
            + [whole((8, inner)), whole((8, twice)), whole((8, LANES)), whole((1, inner))]
            + [whole(one.shape) for one in carry]
            + [anywhere] * len(saved),
            [ahead(cols, start) for cols in (inner, twice, inner, twice, LANES, inner)]
            + [pl.BlockSpec((1, states, inner), lambda c, place, start=start: (c + start, 0, 0))]
            + [whole(one.shape) for one in carry]
            + [whole((model, wide_cols))] * (start == 0),
            [
                ((length, inner), f32), ((length, twice), f32), ((length, inner), bf16),
                ((length, twice), bf16), ((length, LANES), f32), ((length, inner), f32),
                ((chunks, states, inner), bf16), *carry_shapes,
            ]
            + [((model, wide_cols), bf16)] * (start == 0),
            [
                pltpu.VMEM((chunk + 8, inner), f32), pltpu.VMEM((chunk + 8, twice), f32),
                pltpu.VMEM((chunk, model), bf16),
            ],
            {1 + tensor + len(weights) + 7 + k: k for k in range(len(saved))},
        )(place_tensor, *token_pieces, *weights, taps_x, taps_bc, per_head, skip, *carry, *saved)
        saved, carry = results[:7], results[7:10]
        if start == 0:
            full_scan = results[10]
            weights = [full_scan]
    pre_x, pre_bc, raw_x, raw_bc, dt, mixed, before = saved

    parts = rows_local // block
    in_order = pl.BlockSpec(
        (1, 8, block), lambda c, place: (((c // parts) ^ place[0]) * parts + c % parts, 0, 0)
    )

    def gate_piece(k):
        return pl.BlockSpec(
            (block, 2 * model), lambda c, place: (jnp.where(c // parts == k, c % parts, 0), 0)
        )

    gate_raw, grad_scaled, sums, tokens, full_late = call(
        gate_kernel(tensor, dp, parts), length // block,
        [gate_piece(k) for k in range(tensor)]
        + [whole((model // dp, 2 * inner))] * dp
        + [rows_of(block, inner), whole((1, inner))],
        [
            rows_of(block, inner), rows_of(block, inner), in_order, rows_of(block, 2 * model),
            whole((model, 2 * inner)),
        ],
        [
            ((length, inner), f32), ((length, inner), f32), ((length // block, 8, block), f32),
            ((length, 2 * model), bf16), ((model, 2 * inner), bf16),
        ],
    )(place_tensor, *token_pieces, *late_pieces, mixed, gain)

    sum_terms = direct_terms(sums, "tensor")

    scaled, d_mixed, d_gate, grad_gain = call(
        norm_kernel(inner_total, tensor), length // block,
        [in_order] * tensor
        + [rows_of(block, inner), rows_of(block, inner), rows_of(block, inner), whole((1, inner))],
        [rows_of(block, inner), rows_of(block, inner), rows_of(block, inner), whole((8, inner))],
        [
            ((length, inner), bf16), ((length, inner), f32), ((length, inner), bf16),
            ((8, inner), f32),
        ],
    )(place_tensor, *sum_terms, gate_raw, grad_scaled, mixed, gain)

    normed = tokens[:, :model]
    upstream = tokens[:, model:]
    out_part = lax.dot_general(upstream, scaled, TN, preferred_element_type=f32).astype(bf16)
    gate_part = lax.dot_general(normed, d_gate, TN, preferred_element_type=f32).astype(bf16)
    branch_part = mm(scaled, full_late[:, inner:], NT).astype(bf16)
    out_terms = far_first(out_part, "dp")
    gate_terms = near_first(gate_part, "dp")
    branch_terms = near_first(branch_part, "tensor")
    if narrow:
        branch_terms = [exchange_blocks(term, "dp", dp) for term in branch_terms]
    out_block = pl.BlockSpec((rows_local, 1, model), lambda c, place: (0, 0, 0))
    (block_output,) = call(
        output_kernel(blocks, len(branch_terms)), 1,
        [whole((rows_local, model))] * (1 + len(branch_terms)),
        [out_block],
        [((rows_local, 1, model), f32)],
    )(place_entry, tokens_local, *branch_terms)

    carry_shapes = [((8, inner), f32), ((8, twice), f32), ((8, LANES), f32)]
    carry_shapes += [((states, inner), f32)] * 2 + [((8, inner), f32), ((8, twice), f32)]
    carry = [jnp.zeros(*one) for one in carry_shapes]
    columns = []
    for at in range(calls):
        start = chunks - 1 - at * span
        columns, *carry = call(
            backward_kernel(width, head_dim, len(columns)), span,
            [back(cols, start) for cols in (inner, inner, twice, inner, twice, LANES, inner)]
            + [pl.BlockSpec((1, states, inner), lambda c, place, start=start: (start - c, 0, 0))]
            + [whole((8, inner)), whole((8, twice)), whole((8, LANES)), whole((1, inner))]
            + [whole(one.shape) for one in carry]
            + [anywhere] * len(columns),
            [back(wide_cols, start)] + [whole(one.shape) for one in carry],
            [((length, wide_cols), bf16), *carry_shapes],
            [pltpu.VMEM((chunk + 8, inner), f32), pltpu.VMEM((chunk + 8, twice), f32)],
            {1 + 8 + 4 + 7: 0} if columns else {},
        )(
            place_tensor, d_mixed, pre_x, pre_bc, raw_x, raw_bc, dt, mixed, before, taps_x,
            taps_bc, per_head, skip, *carry, *columns,
        )
        columns = [columns]
    columns = columns[0]
    grad_x, grad_bc, grad_head = carry[:3]

    scan_part = lax.dot_general(normed, columns, TN, preferred_element_type=f32).astype(bf16)
    scan_terms = near_first(scan_part, "dp")
    features = model // 4
    normed_part, pre_part = call(
        normed_kernel, 4,
        [
            pl.BlockSpec((length, features), lambda c, place: (0, c)),
            whole((length, inner)), whole((length, wide_cols)),
            rows_of(features, inner), rows_of(features, wide_cols),
        ],
        [
            pl.BlockSpec((length, features), lambda c, place: (0, c)),
            pl.BlockSpec((8, features), lambda c, place: (0, c)),
        ],
        [((length, model), bf16), ((8, model), f32)],
    )(place_tensor, tokens, d_gate, columns, full_late, full_scan)
    normed_terms = near_first(normed_part, "tensor")
    if narrow:
        normed_terms = [exchange_blocks(term, "dp", dp) for term in normed_terms]
    input_grad, _ = call(
        input_kernel(blocks, len(normed_terms)), 1,
        [whole((rows_local, model))] * 2 + [whole((1, model))]
        + [whole((rows_local, model))] * len(normed_terms),
        [out_block, whole((rows_local, model))],
        [((rows_local, 1, model), f32), ((rows_local, model), f32)],
    )(place_entry, tokens_local, upstream_local, gain_in, *normed_terms)

    grad_w_scan = total_of(scan_terms)
    grad_w_out = total_of(out_terms).T
    grad_w_gate = total_of(gate_terms)
    grad_w_bc = total_of(direct_terms(grad_w_scan[:, inner : inner + twice], "tensor"))
    grad_w_dt = grad_w_scan[:, inner + twice : inner + twice + heads]
    grad_w_zx = jnp.stack([grad_w_gate, grad_w_scan[:, :inner]], axis=1)

    pre_part = exchange_blocks(pre_part[:1], "dp", dp)[0] / pre_gain
    kept = width + 2
    local = jnp.concatenate([grad_x[:kept].reshape(-1), grad_gain[0], grad_head[:2].reshape(-1)])
    shared = jnp.concatenate([grad_bc[: width + 1].reshape(-1), pre_part])
    small = all_sum(jnp.concatenate([local, shared]), "dp")
    local = small[: local.shape[0]]
    shared = total_of(direct_terms(small[local.shape[0] :], "tensor"))
    of_x = local[: kept * inner].reshape(kept, inner)
    sum_gain = local[kept * inner : (kept + 1) * inner]
    of_head = local[(kept + 1) * inner :].reshape(2, LANES)
    of_bc = shared[: (width + 1) * twice].reshape(width + 1, twice)
    return (
        block_output,
        input_grad,
        shared[(width + 1) * twice :],
        grad_w_zx,
        grad_w_dt,
        grad_w_bc,
        of_x[:width],
        of_x[width],
        of_bc[:width],
        of_bc[width],
        of_head[0, :heads],
        of_head[1, :heads],
        of_x[width + 1].reshape(heads, head_dim).sum(axis=1),
        sum_gain,
        grad_w_out,
    )


def solution(mesh):
    placed = (
        P("tensor", "dp", None), P(), P("dp", None, "tensor"), P("dp", "tensor"), P("dp", None),
        P(None, "tensor"), P("tensor"), P(), P(), P("tensor"), P("tensor"), P("tensor"),
        P("tensor"), P("tensor", "dp"), P("tensor", "dp", None),
    )
    results = (
        P("tensor", "dp", None), P("tensor", "dp", None), P(), P("dp", None, "tensor"),
        P("dp", "tensor"), P("dp", None), P(None, "tensor"), P("tensor"), P(), P(), P("tensor"),
        P("tensor"), P("tensor"), P("tensor"), P("tensor", "dp"),
    )

    return jax.shard_map(per_device, mesh=mesh, in_specs=placed, out_specs=results, check_vma=False)
```

time: 822 us -> 299 us (0.36)
  waiting for transfers between devices: 315 us -> 103 us
  blocking collectives: 177 us -> 0 us
  local copies, waits for them, and re-layouts: 124 us -> 25.7 us
  Pallas kernels: 0 us -> 80.6 us
  matrix products: 94.3 us -> 14.2 us
  other arithmetic: 87.5 us -> 17.9 us
  starting transfers between devices: 0.62 us -> 55.5 us
  between operations: 16.3 us -> 1.14 us
    reduce_scatter x5 -> x0, waiting for transfers between devices: 162 us -> none  [the longest x1 72.2 us: per_device(): lax.psum_scatter(grad_out_part, 'dp', scatter_dimension=1, tiled=True)]
    unnamed x11 -> x0, waiting for transfers between devices: 142 us -> none
    psum x5 -> x0, blocking collectives: 116 us -> none  [the longest x1 39.5 us: per_device(): lax.psum((pre_gain_part, grad_kbc, grad_bbc), ('dp', 'tensor'))]
    ppermute x0 -> x54, waiting for transfers between devices: none -> 103 us  [swap(): return lax.ppermute(value, axis, [(i, i ^ bits) for i in range(size)])]
    pallas_call x0 -> x10, Pallas kernels: none -> 80.6 us  [the longest x2 26.1 us: per_device(): call(backward_kernel(width, head_dim, len(columns)), span, [back(cols, st...]
    dot_general x18 -> x4, matrix products: 92.5 us -> 14.2 us  [the longest x1 5.9 us: per_device(): lax.dot_general(normed, columns, TN, preferred_element_type=f32)]
    all_gather x2 -> x0, blocking collectives: 60.9 us -> none  [the longest x1 32.7 us: per_device(): lax.all_gather(w_bc, 'dp', axis=0, tiled=True)]
    ppermute x0 -> x54, starting transfers between devices: none -> 55.5 us  [swap(): return lax.ppermute(value, axis, [(i, i ^ bits) for i in range(size)])]
  transfers between devices with their start and end apart: 10 -> 54, of which waited for: 6 -> 23; matrix products, arithmetic and copies ran while one was open for 21% -> 13% of each run, Pallas kernels for 0% -> 8%
where the time goes in v1:
time: 299 us; the launch traced here: 298 us
  waiting for transfers between devices  103 us (34%)
  Pallas kernels  80.6 us (27%)
  starting transfers between devices  55.5 us (19%)
  local copies, waits for them, and re-layouts  25.7 us (9%)
  other arithmetic  17.9 us (6%)
  matrix products  14.2 us (5%)
    ppermute x54, waiting for transfers between devices, swap(): return lax.ppermute(value, axis, [(i, i ^ bits) for i in range(size)])  103 us
    ppermute x54, starting transfers between devices, swap(): return lax.ppermute(value, axis, [(i, i ^ bits) for i in range(size)])  55.5 us
    pallas_call x2, Pallas kernels, per_device(): call(backward_kernel(width, head_dim, len(columns)), span, [back(cols, st...  26.1 us
    pallas_call x2, Pallas kernels, per_device(): call(forward_kernel(width, head_dim, tensor, len(weights), per, start), s...  21.3 us
    pallas_call x1, Pallas kernels, per_device(): call(gate_kernel(tensor, dp, parts), length // block, [gate_piece(k) for...  9.61 us
    unnamed x68, local copies, waits for them, and re-layouts  8.54 us
    pallas_call x1, Pallas kernels, per_device(): call(normed_kernel, 4, [pl.BlockSpec((length, features), lambda c, place:...  7.77 us
    pallas_call x1, Pallas kernels, per_device(): call(norm_kernel(inner_total, tensor), length // block, [in_order] * tens...  6.33 us
  transfers between devices with their start and end apart: 54, of which 23 were waited for; matrix products, arithmetic and copies ran while one was open for 13% of the time, Pallas kernels for 8%

profile of v1, /device:TPU:0, one launch (start us, length us, event | category | flops | bytes accessed | tf_op | source)
XLA Modules:
  0.0 297.7 jit_solution(10714263469476603609)
XLA Ops:
  0.7 2.7 shard_map.262.refs_0_
  3.4 3.0 %collective-permute-start.1 = (bf16[256,2048]{1,0:T(8,128)(2,1)}, bf16[256,2048]{1,0:T(8,128)(2,1)S(1)}, u32[]{:S(2)}, u32[]{:S(2)}) collective-permute-start(bf16[256,2048]{1,0:T(8,128)(2,1)} %shard_map.262.refs_0_), channel_id=1, source_target_pairs={{0,2},{1,3},{2,0},{3,1},{4,6},{5,7},{6,4},{7,5},{8,10},{9,11},{10,... | collective-permute-start | bytes 3145736 | tf_op jit(solution)/shard_map/ppermute | solution.py:39
  7.8 1.6 collective-permute-start.11
  9.4 2.6 collective-permute-start.13
  12.2 8.3 %collective-permute-done.11.refs_6_ = bf16[128,896]{1,0:T(8,128)(2,1)S(1)} collective-permute-done((bf16[128,896]{1,0:T(8,128)(2,1)}, bf16[128,896]{1,0:T(8,128)(2,1)S(1)}, u32[]{:S(2)}, u32[]{:S(2)}) %collective-permute-start.11) | collective-permute-done | bytes 229408 | tf_op jit(solution)/shard_map/ppermute | solution.py:39
  20.5 1.5 collective-permute-start.10
  22.0 7.8 %collective-permute-done.1.refs_2_ = bf16[256,2048]{1,0:T(8,128)(2,1)S(1)} collective-permute-done((bf16[256,2048]{1,0:T(8,128)(2,1)}, bf16[256,2048]{1,0:T(8,128)(2,1)S(1)}, u32[]{:S(2)}, u32[]{:S(2)}) %collective-permute-start.1) | collective-permute-done | bytes 1048608 | tf_op jit(solution)/shard_map/ppermute | solution.py:39
  29.8 1.8 copy.47
  32.6 1.9 collective-permute-start.4
  34.4 2.6 collective-permute-start.6
  37.1 9.4 %collective-permute-done.4.refs_6_ = bf16[128,1024]{1,0:T(8,128)(2,1)} collective-permute-done((bf16[128,1024]{1,0:T(8,128)(2,1)S(1)}, bf16[128,1024]{1,0:T(8,128)(2,1)}, u32[]{:S(2)}, u32[]{:S(2)}) %collective-permute-start.4) | collective-permute-done | bytes 262176 | tf_op jit(solution)/shard_map/ppermute | solution.py:39
  46.5 1.6 collective-permute-start.12
  48.1 7.8 %collective-permute-done.6.refs_8_ = bf16[128,1024]{1,0:T(8,128)(2,1)} collective-permute-done((bf16[128,1024]{1,0:T(8,128)(2,1)S(1)}, bf16[128,1024]{1,0:T(8,128)(2,1)}, u32[]{:S(2)}, u32[]{:S(2)}) %collective-permute-start.6) | collective-permute-done | bytes 262176 | tf_op jit(solution)/shard_map/ppermute | solution.py:39
  55.9 1.5 collective-permute-start.14
  58.6 1.6 collective-permute-start.3
  60.2 4.4 %collective-permute-done.14.refs_9_ = bf16[128,896]{1,0:T(8,128)(2,1)S(1)} collective-permute-done((bf16[128,896]{1,0:T(8,128)(2,1)}, bf16[128,896]{1,0:T(8,128)(2,1)S(1)}, u32[]{:S(2)}, u32[]{:S(2)}) %collective-permute-start.14) | collective-permute-done | bytes 229408 | tf_op jit(solution)/shard_map/ppermute | solution.py:39
  64.6 1.5 collective-permute-start.5
  66.1 3.4 %collective-permute-done.16.refs_11_ = bf16[128,896]{1,0:T(8,128)(2,1)S(1)} collective-permute-done((bf16[128,896]{1,0:T(8,128)(2,1)}, bf16[128,896]{1,0:T(8,128)(2,1)S(1)}, u32[]{:S(2)}, u32[]{:S(2)}) %collective-permute-start.16) | collective-permute-done | bytes 229408 | tf_op jit(solution)/shard_map/ppermute | solution.py:39
  69.5 1.5 collective-permute-start.7
  78.2 10.8 %shard_map.263 = (f32[1024,512]{1,0:T(8,128)}, f32[1024,256]{1,0:T(8,128)}, bf16[1024,512]{1,0:T(8,128)(2,1)}, bf16[1024,256]{1,0:T(8,128)(2,1)}, f32[1024,128]{...) custom-call(s32[1]{0:T(128)} %bitcast.2.place, ...), custom_call_target="tpu_custom_call" | custom-call | tf_op jit(solution)/shard_map/pallas_call | solution.py:592
  89.0 10.5 %shard_map.264 = (f32[1024,512]{1,0:T(8,128)}, f32[1024,256]{1,0:T(8,128)}, bf16[1024,512]{1,0:T(8,128)(2,1)}, bf16[1024,256]{1,0:T(8,128)(2,1)}, f32[1024,128]{...) custom-call(s32[1]{0:T(128)} %bitcast.2.place, ...), custom_call_target="tpu_custom_call", output_to_operand_aliasing={{0}: (13, {}), {1}: (14, {}), {2}: (15, {}), {3}: (16, {}),... | custom-call | tf_op jit(solution)/shard_map/pallas_call | solution.py:592
  99.5 9.6 %shard_map.265 = (f32[1024,512]{1,0:T(8,128)}, f32[1024,512]{1,0:T(8,128)}, f32[4,8,256]{2,1,0:T(8,128)}, bf16[1024,2048]{1,0:T(8,128)(2,1)}, bf16[1024,1024]{1,0:T(8,128)(2,1)}) custom-call(s32[1]{0:T(128)} %bitcast.2.place, bf16[256,2048]{1,0:T(8,128)(2,1)} %shard_map.262.refs_0_, bf16[256,2048]{1,0:T(8,128)(2,1)} %copy-done.1, bf16[256,2048]{1,0:T(8,128)(2,1)} %copy-done, ...), custom_call_target="tpu_custom_call" | custom-call | tf_op jit(solution)/shard_map/pallas_call | solution.py:632
  109.2 1.6 collective-permute-start.18
  111.1 2.3 collective-permute-done.18.refs_2_
  115.0 6.3 %shard_map.266 = (bf16[1024,512]{1,0:T(8,128)(2,1)}, f32[1024,512]{1,0:T(8,128)}, bf16[1024,512]{1,0:T(8,128)(2,1)}, f32[8,512]{1,0:T(8,128)}) custom-call(s32[1]{0:T(128)} %bitcast.2.place, f32[4,8,256]{2,1,0:T(8,128)} %get-tuple-element.69.refs_0_, f32[4,8,256]{2,1,0:T(8,128)} %copy-done.19, f32[4,8,256]{2,1,0:T(8,128)} %copy-done.20, ...), custom_call_target="tpu_custom_call" | custom-call | tf_op jit(solution)/shard_map/pallas_call | solution.py:649
  121.4 3.1 %fusion.12 = bf16[1024,512]{1,0:T(8,128)(2,1)S(1)} fusion(bf16[1024,512]{1,0:T(8,128)(2,1)} %get-tuple-element.72, bf16[1024,2048]{1,0:T(8,128)(2,1)} %get-tuple-element.74.tokens), kind=kOutput, calls=%fused_computation.9 | convolution fusion | flops 1074266112 | bytes 4194304 | tf_op jit(solution)/shard_map/dot_general | solution.py:662
  125.1 13.0 %shard_map.268 = (bf16[1024,896]{1,0:T(8,128)(2,1)}, f32[8,512]{1,0:T(8,128)}, f32[8,256]{1,0:T(8,128)}, f32[8,128]{1,0:T(8,128)}, f32[128,512]{1,0:T(8,128)}, /...) custom-call(s32[1]{0:T(128)} %bitcast.2.place, f32[1024,512]{1,0:T(8,128)} %get-tuple-element.76.refs_0_, ...), custom_call_target="tpu_custom_call" | custom-call | tf_op jit(solution)/shard_map/pallas_call | solution.py:684
  138.1 13.1 %shard_map.269 = (bf16[1024,896]{1,0:T(8,128)(2,1)}, f32[8,512]{1,0:T(8,128)}, f32[8,256]{1,0:T(8,128)}, f32[8,128]{1,0:T(8,128)}, f32[128,512]{1,0:T(8,128)}, /...) custom-call(s32[1]{0:T(128)} %bitcast.2.place, ...), custom_call_target="tpu_custom_call", output_to_operand_aliasing={{0}: (20, {})} | custom-call | tf_op jit(solution)/shard_map/pallas_call | solution.py:684
  151.2 5.9 %fusion.6 = bf16[1024,896]{1,0:T(8,128)(2,1)} fusion(bf16[1024,896]{1,0:T(8,128)(2,1)} %get-tuple-element.91.columns, bf16[1024,2048]{1,0:T(8,128)(2,1)} %get-tuple-element.74.tokens), kind=kOutput, calls=%fused_computation.7 | convolution fusion | flops 1879965696 | bytes 5767168 | tf_op jit(solution)/shard_map/dot_general | solution.py:703
  157.1 2.3 fusion.9
  159.4 7.8 %shard_map.270 = (bf16[1024,1024]{1,0:T(8,128)(2,1)}, f32[8,1024]{1,0:T(8,128)}) custom-call(s32[1]{0:T(128)} %bitcast.2.place, bf16[1024,2048]{1,0:T(8,128)(2,1)} %get-tuple-element.74.tokens, bf16[1024,512]{1,0:T(8,128)(2,1)} %get-tuple-element.75.d_gate, bf16[1024,896]{1,0:T(8,128)(2,1)} %get-tuple-element.91.columns, ...), custom_call_target="tpu_custom_call" | custom-call | tf_op jit(solution)/shard_map/pallas_call | solution.py:706
  167.2 2.8 convolution_convert_fusion
  171.3 2.7 collective-permute-start.51
  176.9 1.5 collective-permute-start.26
  178.4 2.6 fusion.16
  184.4 1.5 collective-permute-start.28
  186.0 2.5 collective-permute-start.29
  189.3 2.3 collective-permute-done.29
  196.5 1.5 collective-permute-start.35
  200.3 2.4 collective-permute-done.33
  203.2 2.3 collective-permute-done.35
  206.0 2.3 collective-permute-done.37
  208.8 1.3 add_convert_fusion.8
  210.1 3.0 collective-permute-done.40
  213.1 2.5 collective-permute-start.52
  215.6 2.4 collective-permute-done.42
  218.6 4.4 %collective-permute-done.44 = bf16[128,896]{1,0:T(8,128)(2,1)S(1)} collective-permute-done((bf16[128,896]{1,0:T(8,128)(2,1)}, bf16[128,896]{1,0:T(8,128)(2,1)S(1)}, u32[]{:S(2)}, u32[]{:S(2)}) %collective-permute-start.44) | collective-permute-done | bytes 229408 | tf_op jit(solution)/shard_map/ppermute | solution.py:39
  223.5 2.1 add_convert_fusion.4
  225.6 2.5 collective-permute-start.34
  228.1 1.9 collective-permute-start.38
  231.1 2.7 collective-permute-done.34
  233.8 2.5 collective-permute-start.41
  236.3 11.7 %collective-permute-done.36 = bf16[128,512]{1,0:T(8,128)(2,1)S(1)} collective-permute-done((bf16[128,512]{1,0:T(8,128)(2,1)S(1)}, bf16[128,512]{1,0:T(8,128)(2,1)S(1)}, u32[]{:S(2)}, u32[]{:S(2)}) %collective-permute-start.36) | collective-permute-done | bytes 131104 | tf_op jit(solution)/shard_map/ppermute | solution.py:39
  248.0 1.5 collective-permute-start.53
  249.5 1.7 add_bitcast_fusion.1
  251.2 1.8 collective-permute-done.53
  255.4 2.1 collective-permute-done.43
  257.5 2.4 collective-permute-done.45
  259.9 1.5 convert_add_fusion
  263.0 2.2 add_convert_fusion
  271.8 11.1 %collective-permute-done.24.refs_1_ = bf16[256,1024]{1,0:T(8,128)(2,1)S(1)} collective-permute-done((bf16[256,1024]{1,0:T(8,128)(2,1)}, bf16[256,1024]{1,0:T(8,128)(2,1)S(1)}, u32[]{:S(2)}, u32[]{:S(2)}) %collective-permute-start.24) | collective-permute-done | bytes 524320 | tf_op jit(solution)/shard_map/ppermute | solution.py:39
  283.7 3.6 %shard_map.271 = (f32[256,1,1024]{2,1,0:T(1,128)}, f32[256,1024]{1,0:T(8,128)}) custom-call(s32[1]{0:T(128)} %bitcast.place, bf16[256,1024]{1,0:T(8,128)(2,1)} %bitcast.47, bf16[256,1024]{1,0:T(8,128)(2,1)} %bitcast.50, f32[1,1024]{1,0:T(1,128)} %bitcast.55, bf16[256,1024]{1,0:T(8,128)(2,1)} %get-tuple-element.131.refs_0_, bf16[256,1024]{1,0:T(8,128)(2,1)} %copy-done.11, ...), custom_call_target="tpu_custom_call" | custom-call | tf_op jit(solution)/shard_map/pallas_call | solution.py:722
  287.3 6.4 %collective-permute-done.21.refs_1_ = bf16[256,1024]{1,0:T(8,128)(2,1)S(1)} collective-permute-done((bf16[256,1024]{1,0:T(8,128)(2,1)S(1)}, bf16[256,1024]{1,0:T(8,128)(2,1)S(1)}, u32[]{:S(2)}, u32[]{:S(2)}) %collective-permute-start.21) | collective-permute-done | bytes 524320 | tf_op jit(solution)/shard_map/ppermute | solution.py:39
  294.5 3.2 %shard_map.267 = f32[256,1,1024]{2,1,0:T(1,128)} custom-call(s32[1]{0:T(128)} %bitcast.place, bf16[256,1024]{1,0:T(8,128)(2,1)} %bitcast.48, bf16[256,1024]{1,0:T(8,128)(2,1)} %get-tuple-element.134.refs_0_, bf16[256,1024]{1,0:T(8,128)(2,1)} %copy-done.10, bf16[256,1024]{1,0:T(8,128)(2,1)} %collective-permute-done.22.refs_2_), custom_call_target="tpu_custom_call" | custom-call | tf_op jit(solution)/shard_map/pallas_call | solution.py:671
  (186 shorter events, 44.8 us)
Async XLA Ops:
  3.4 70.8 %copy-start.25 = (f32[4,256]{1,0:T(4,128)S(1)}, f32[4,256]{1,0:T(4,128)}, u32[]{:S(2)}) copy-start(f32[4,256]{1,0:T(4,128)} %param.22) | copy-start | bytes 12292
  3.4 72.1 %copy-start.23 = (f32[4,512]{1,0:T(4,128)S(1)}, f32[4,512]{1,0:T(4,128)}, u32[]{:S(2)}) copy-start(f32[4,512]{1,0:T(4,128)} %param.20) | copy-start | bytes 24580
  3.4 72.1 %copy-start.27 = (f32[512]{0:T(512)S(1)}, f32[512]{0:T(512)}, u32[]{:S(2)}) copy-start(f32[512]{0:T(512)} %param.21) | copy-start | bytes 6148
  3.4 26.4 %collective-permute-start.1 = (bf16[256,2048]{1,0:T(8,128)(2,1)}, bf16[256,2048]{1,0:T(8,128)(2,1)S(1)}, u32[]{:S(2)}, u32[]{:S(2)}) collective-permute-start(bf16[256,2048]{1,0:T(8,128)(2,1)} %shard_map.262.refs_0_), channel_id=1, source_target_pairs={{0,2},{1,3},{2,0},{3,1},{4,6},{5,7},{6,4},{7,5},{8,10},{9,11},{10,... | collective-permute-start | bytes 3145736 | tf_op jit(solution)/shard_map/ppermute | solution.py:39
  6.4 64.6 %collective-permute-start = (bf16[256,2048]{1,0:T(8,128)(2,1)}, bf16[256,2048]{1,0:T(8,128)(2,1)S(1)}, u32[]{:S(2)}, u32[]{:S(2)}) collective-permute-start(bf16[256,2048]{1,0:T(8,128)(2,1)} %shard_map.262.refs_0_), channel_id=1, source_target_pairs={{0,1},{1,0},{2,3},{3,2},{4,5},{5,4},{6,7},{7,6},{8,9},{9,8},{10,11... | collective-permute-start | bytes 3145736 | tf_op jit(solution)/shard_map/ppermute | solution.py:39
  7.8 12.7 %collective-permute-start.11 = (bf16[128,896]{1,0:T(8,128)(2,1)}, bf16[128,896]{1,0:T(8,128)(2,1)S(1)}, u32[]{:S(2)}, u32[]{:S(2)}) collective-permute-start(bf16[128,896]{1,0:T(8,128)(2,1)} %maximum_maximum_fusion.refs_4_), channel_id=1, source_target_pairs={{0,8},{4,12},{8,0},{12,4},{16,24},{20,28},{24,16},{28,20},{1,9},{5... | collective-permute-start | bytes 688136 | tf_op jit(solution)/shard_map/ppermute | solution.py:39
  9.4 23.2 %collective-permute-start.13 = (bf16[128,896]{1,0:T(8,128)(2,1)}, bf16[128,896]{1,0:T(8,128)(2,1)}, u32[]{:S(2)}, u32[]{:S(2)}) collective-permute-start(bf16[128,896]{1,0:T(8,128)(2,1)} %maximum_maximum_fusion.refs_4_), channel_id=1, source_target_pairs={{0,16},{4,20},{8,24},{12,28},{16,0},{20,4},{24,8},{28,12},{1,17},{... | collective-permute-start | bytes 688136 | tf_op jit(solution)/shard_map/ppermute | solution.py:39
  12.0 22.5 %collective-permute-start.15 = (bf16[128,896]{1,0:T(8,128)(2,1)}, bf16[128,896]{1,0:T(8,128)(2,1)}, u32[]{:S(2)}, u32[]{:S(2)}) collective-permute-start(bf16[128,896]{1,0:T(8,128)(2,1)} %maximum_maximum_fusion.refs_4_), channel_id=1, source_target_pairs={{0,24},{4,28},{8,16},{12,20},{16,8},{20,12},{24,0},{28,4},{1,25},{... | collective-permute-start | bytes 688136 | tf_op jit(solution)/shard_map/ppermute | solution.py:39
  20.5 16.5 %collective-permute-start.10 = (bf16[128,896]{1,0:T(8,128)(2,1)}, bf16[128,896]{1,0:T(8,128)(2,1)}, u32[]{:S(2)}, u32[]{:S(2)}) collective-permute-start(bf16[128,896]{1,0:T(8,128)(2,1)} %maximum_maximum_fusion.refs_4_), channel_id=1, source_target_pairs={{0,4},{4,0},{8,12},{12,8},{16,20},{20,16},{24,28},{28,24},{1,5},{5... | collective-permute-start | bytes 688136 | tf_op jit(solution)/shard_map/ppermute | solution.py:39
  29.8 48.4 %copy-start = (bf16[256,2048]{1,0:T(8,128)(2,1)}, bf16[256,2048]{1,0:T(8,128)(2,1)S(1)}, u32[]{:S(2)}) copy-start(bf16[256,2048]{1,0:T(8,128)(2,1)S(1)} %collective-permute-done.1.refs_2_) | copy-start | bytes 3145732
  29.8 46.4 %collective-permute-start.2 = (bf16[256,2048]{1,0:T(8,128)(2,1)S(1)}, bf16[256,2048]{1,0:T(8,128)(2,1)S(1)}, u32[]{:S(2)}, u32[]{:S(2)}) collective-permute-start(bf16[256,2048]{1,0:T(8,128)(2,1)S(1)} %collective-permute-done.1.refs_2_), channel_id=1, source_target_pairs={{0,1},{1,0},{2,3},{3,2},{4,5},{5,4},{6,7},{7,6},{8,9},{9,8},{10,11... | collective-permute-start | bytes 3145736 | tf_op jit(solution)/shard_map/ppermute | solution.py:39
  32.6 56.4 %copy-start.5 = (bf16[128,1024]{1,0:T(8,128)(2,1)}, bf16[128,1024]{1,0:T(8,128)(2,1)S(1)}, u32[]{:S(2)}) copy-start(bf16[128,1024]{1,0:T(8,128)(2,1)S(1)} %pad_maximum_fusion.1.refs_4_) | copy-start | bytes 786436
  32.6 13.9 %collective-permute-start.4 = (bf16[128,1024]{1,0:T(8,128)(2,1)S(1)}, bf16[128,1024]{1,0:T(8,128)(2,1)}, u32[]{:S(2)}, u32[]{:S(2)}) collective-permute-start(bf16[128,1024]{1,0:T(8,128)(2,1)S(1)} %pad_maximum_fusion.1.refs_4_), channel_id=1, source_target_pairs={{0,8},{4,12},{8,0},{12,4},{16,24},{20,28},{24,16},{28,20},{1,9},{5... | collective-permute-start | bytes 786440 | tf_op jit(solution)/shard_map/ppermute | solution.py:39
  34.4 21.5 %collective-permute-start.6 = (bf16[128,1024]{1,0:T(8,128)(2,1)S(1)}, bf16[128,1024]{1,0:T(8,128)(2,1)}, u32[]{:S(2)}, u32[]{:S(2)}) collective-permute-start(bf16[128,1024]{1,0:T(8,128)(2,1)S(1)} %pad_maximum_fusion.1.refs_4_), channel_id=1, source_target_pairs={{0,16},{4,20},{8,24},{12,28},{16,0},{20,4},{24,8},{28,12},{1,17},{... | collective-permute-start | bytes 786440 | tf_op jit(solution)/shard_map/ppermute | solution.py:39
  37.0 20.4 %collective-permute-start.8 = (bf16[128,1024]{1,0:T(8,128)(2,1)S(1)}, bf16[128,1024]{1,0:T(8,128)(2,1)}, u32[]{:S(2)}, u32[]{:S(2)}) collective-permute-start(bf16[128,1024]{1,0:T(8,128)(2,1)S(1)} %pad_maximum_fusion.1.refs_4_), channel_id=1, source_target_pairs={{0,24},{4,28},{8,16},{12,20},{16,8},{20,12},{24,0},{28,4},{1,25},{... | collective-permute-start | bytes 786440 | tf_op jit(solution)/shard_map/ppermute | solution.py:39
  46.5 12.1 %collective-permute-start.12 = (bf16[128,896]{1,0:T(8,128)(2,1)}, bf16[128,896]{1,0:T(8,128)(2,1)S(1)}, u32[]{:S(2)}, u32[]{:S(2)}) collective-permute-start(bf16[128,896]{1,0:T(8,128)(2,1)} %copy-done.13), channel_id=1, source_target_pairs={{0,4},{4,0},{8,12},{12,8},{16,20},{20,16},{24,28},{28,24},{1,5},{5... | collective-permute-start | bytes 688136 | tf_op jit(solution)/shard_map/ppermute | solution.py:39
  55.9 8.7 %collective-permute-start.14 = (bf16[128,896]{1,0:T(8,128)(2,1)}, bf16[128,896]{1,0:T(8,128)(2,1)S(1)}, u32[]{:S(2)}, u32[]{:S(2)}) collective-permute-start(bf16[128,896]{1,0:T(8,128)(2,1)} %collective-permute-done.13.refs_8_), channel_id=1, source_target_pairs={{0,4},{4,0},{8,12},{12,8},{16,20},{20,16},{24,28},{28,24},{1,5},{5... | collective-permute-start | bytes 688136 | tf_op jit(solution)/shard_map/ppermute | solution.py:39
  57.4 12.1 %collective-permute-start.16 = (bf16[128,896]{1,0:T(8,128)(2,1)}, bf16[128,896]{1,0:T(8,128)(2,1)S(1)}, u32[]{:S(2)}, u32[]{:S(2)}) collective-permute-start(bf16[128,896]{1,0:T(8,128)(2,1)} %collective-permute-done.15.refs_10_), channel_id=1, source_target_pairs={{0,4},{4,0},{8,12},{12,8},{16,20},{20,16},{24,28},{28,24},{1,5},{5... | collective-permute-start | bytes 688136 | tf_op jit(solution)/shard_map/ppermute | solution.py:39
  58.6 12.4 %copy-start.14 = (bf16[128,896]{1,0:T(8,128)(2,1)}, bf16[128,896]{1,0:T(8,128)(2,1)S(1)}, u32[]{:S(2)}) copy-start(bf16[128,896]{1,0:T(8,128)(2,1)S(1)} %collective-permute-done.12.refs_7_) | copy-start | bytes 688132
  58.6 40.9 %collective-permute-start.3 = (bf16[128,1024]{1,0:T(8,128)(2,1)S(1)}, bf16[128,1024]{1,0:T(8,128)(2,1)}, u32[]{:S(2)}, u32[]{:S(2)}) collective-permute-start(bf16[128,1024]{1,0:T(8,128)(2,1)S(1)} %pad_maximum_fusion.1.refs_4_), channel_id=1, source_target_pairs={{0,4},{4,0},{8,12},{12,8},{16,20},{20,16},{24,28},{28,24},{1,5},{5... | collective-permute-start | bytes 786440 | tf_op jit(solution)/shard_map/ppermute | solution.py:39
  64.6 34.9 %collective-permute-start.5 = (bf16[128,1024]{1,0:T(8,128)(2,1)}, bf16[128,1024]{1,0:T(8,128)(2,1)}, u32[]{:S(2)}, u32[]{:S(2)}) collective-permute-start(bf16[128,1024]{1,0:T(8,128)(2,1)} %collective-permute-done.4.refs_6_), channel_id=1, source_target_pairs={{0,4},{4,0},{8,12},{12,8},{16,20},{20,16},{24,28},{28,24},{1,5},{5... | collective-permute-start | bytes 786440 | tf_op jit(solution)/shard_map/ppermute | solution.py:39
  69.5 30.0 %collective-permute-start.7 = (bf16[128,1024]{1,0:T(8,128)(2,1)}, bf16[128,1024]{1,0:T(8,128)(2,1)}, u32[]{:S(2)}, u32[]{:S(2)}) collective-permute-start(bf16[128,1024]{1,0:T(8,128)(2,1)} %collective-permute-done.6.refs_8_), channel_id=1, source_target_pairs={{0,4},{4,0},{8,12},{12,8},{16,20},{20,16},{24,28},{28,24},{1,5},{5... | collective-permute-start | bytes 786440 | tf_op jit(solution)/shard_map/ppermute | solution.py:39
  71.0 28.5 %collective-permute-start.9 = (bf16[128,1024]{1,0:T(8,128)(2,1)}, bf16[128,1024]{1,0:T(8,128)(2,1)}, u32[]{:S(2)}, u32[]{:S(2)}) collective-permute-start(bf16[128,1024]{1,0:T(8,128)(2,1)} %collective-permute-done.8.refs_10_), channel_id=1, source_target_pairs={{0,4},{4,0},{8,12},{12,8},{16,20},{20,16},{24,28},{28,24},{1,5},{5... | collective-permute-start | bytes 786440 | tf_op jit(solution)/shard_map/ppermute | solution.py:39
  109.2 1.9 collective-permute-start.17
  109.2 4.2 %collective-permute-start.18 = (f32[4,8,256]{2,1,0:T(8,128)}, f32[4,8,256]{2,1,0:T(8,128)S(1)}, u32[]{:S(2)}, u32[]{:S(2)}) collective-permute-start(f32[4,8,256]{2,1,0:T(8,128)} %get-tuple-element.69.refs_0_), channel_id=1, source_target_pairs={{0,2},{1,3},{2,0},{3,1},{4,6},{5,7},{6,4},{7,5},{8,10},{9,11},{10,... | collective-permute-start | bytes 98312 | tf_op jit(solution)/shard_map/ppermute | solution.py:39
  110.8 3.6 %collective-permute-start.19 = (f32[4,8,256]{2,1,0:T(8,128)}, f32[4,8,256]{2,1,0:T(8,128)S(1)}, u32[]{:S(2)}, u32[]{:S(2)}) collective-permute-start(f32[4,8,256]{2,1,0:T(8,128)} %get-tuple-element.69.refs_0_), channel_id=1, source_target_pairs={{0,3},{1,2},{2,1},{3,0},{4,7},{5,6},{6,5},{7,4},{8,11},{9,10},{10,... | collective-permute-start | bytes 98312 | tf_op jit(solution)/shard_map/ppermute | solution.py:39
  167.2 8.2 %copy-start.22 = (f32[8,512]{1,0:T(8,128)S(1)}, f32[8,512]{1,0:T(8,128)}, u32[]{:S(2)}) copy-start(f32[8,512]{1,0:T(8,128)} %get-tuple-element.94) | copy-start | bytes 49156
  167.2 8.9 %copy-start.24 = (f32[8,256]{1,0:T(8,128)S(1)}, f32[8,256]{1,0:T(8,128)}, u32[]{:S(2)}) copy-start(f32[8,256]{1,0:T(8,128)} %get-tuple-element.97) | copy-start | bytes 24580
  167.2 9.6 %copy-start.18 = (f32[1024]{0:T(1024)S(1)}, f32[1024]{0:T(1024)}, u32[]{:S(2)}) copy-start(f32[1024]{0:T(1024)} %param.16) | copy-start | bytes 12292
  170.9 54.6 %collective-permute-start.50 = (bf16[256,512]{1,0:T(8,128)(2,1)}, bf16[256,512]{1,0:T(8,128)(2,1)S(1)}, u32[]{:S(2)}, u32[]{:S(2)}) collective-permute-start(bf16[256,512]{1,0:T(8,128)(2,1)} %get-tuple-element.142), channel_id=1, source_target_pairs={{0,8},{4,12},{8,0},{12,4},{16,24},{20,28},{24,16},{28,20},{1,9},{5... | collective-permute-start | bytes 786440 | tf_op jit(solution)/shard_map/ppermute | solution.py:39
  171.3 56.8 %collective-permute-start.51 = (bf16[256,512]{1,0:T(8,128)(2,1)}, bf16[256,512]{1,0:T(8,128)(2,1)}, u32[]{:S(2)}, u32[]{:S(2)}) collective-permute-start(bf16[256,512]{1,0:T(8,128)(2,1)} %get-tuple-element.144), channel_id=1, source_target_pairs={{0,16},{4,20},{8,24},{12,28},{16,0},{20,4},{24,8},{28,12},{1,17},{... | collective-permute-start | bytes 786440 | tf_op jit(solution)/shard_map/ppermute | solution.py:39
  176.9 7.1 %collective-permute-start.26 = (f32[6144]{0:T(1024)S(1)}, f32[6144]{0:T(1024)S(1)}, u32[]{:S(2)}, u32[]{:S(2)}) collective-permute-start(f32[6144]{0:T(1024)S(1)} %constant_dynamic-update-slice_fusion), channel_id=1, source_target_pairs={{0,4},{4,0},{8,12},{12,8},{16,20},{20,16},{24,28},{28,24},{1,5},{5... | collective-permute-start | bytes 73736 | tf_op jit(solution)/shard_map/ppermute | solution.py:39
  184.0 5.3 %collective-permute-start.27 = (f32[6144]{0:T(1024)S(1)}, f32[6144]{0:T(1024)S(1)}, u32[]{:S(2)}, u32[]{:S(2)}) collective-permute-start(f32[6144]{0:T(1024)S(1)} %add.107), channel_id=1, source_target_pairs={{0,8},{4,12},{8,0},{12,4},{16,24},{20,28},{24,16},{28,20},{1,9},{5... | collective-permute-start | bytes 73736 | tf_op jit(solution)/shard_map/ppermute | solution.py:39
  184.4 4.8 %collective-permute-start.28 = (f32[6144]{0:T(1024)S(1)}, f32[6144]{0:T(1024)S(1)}, u32[]{:S(2)}, u32[]{:S(2)}) collective-permute-start(f32[6144]{0:T(1024)S(1)} %add.107), channel_id=1, source_target_pairs={{0,16},{4,20},{8,24},{12,28},{16,0},{20,4},{24,8},{28,12},{1,17},{... | collective-permute-start | bytes 73736 | tf_op jit(solution)/shard_map/ppermute | solution.py:39
  186.0 5.6 %collective-permute-start.29 = (f32[6144]{0:T(1024)S(1)}, f32[6144]{0:T(1024)S(1)}, u32[]{:S(2)}, u32[]{:S(2)}) collective-permute-start(f32[6144]{0:T(1024)S(1)} %add.107), channel_id=1, source_target_pairs={{0,24},{4,28},{8,16},{12,20},{16,8},{20,12},{24,0},{28,4},{1,25},{... | collective-permute-start | bytes 73736 | tf_op jit(solution)/shard_map/ppermute | solution.py:39
  191.6 4.4 %collective-permute-start.30 = (f32[2304]{0:T(1024)S(1)}, f32[2304]{0:T(1024)S(1)}, u32[]{:S(2)}, u32[]{:S(2)}) collective-permute-start(f32[2304]{0:T(1024)S(1)} %slice.309), channel_id=1, source_target_pairs={{0,1},{1,0},{2,3},{3,2},{4,5},{5,4},{6,7},{7,6},{8,9},{9,8},{10,11... | collective-permute-start | bytes 27656 | tf_op jit(solution)/shard_map/ppermute | solution.py:39
  191.7 4.8 %collective-permute-start.31 = (f32[2304]{0:T(1024)S(1)}, f32[2304]{0:T(1024)S(1)}, u32[]{:S(2)}, u32[]{:S(2)}) collective-permute-start(f32[2304]{0:T(1024)S(1)} %slice.309), channel_id=1, source_target_pairs={{0,2},{1,3},{2,0},{3,1},{4,6},{5,7},{6,4},{7,5},{8,10},{9,11},{10,... | collective-permute-start | bytes 27656 | tf_op jit(solution)/shard_map/ppermute | solution.py:39
  192.8 5.3 %collective-permute-start.32 = (f32[2304]{0:T(1024)S(1)}, f32[2304]{0:T(1024)S(1)}, u32[]{:S(2)}, u32[]{:S(2)}) collective-permute-start(f32[2304]{0:T(1024)S(1)} %slice.309), channel_id=1, source_target_pairs={{0,3},{1,2},{2,1},{3,0},{4,7},{5,6},{6,5},{7,4},{8,11},{9,10},{10,... | collective-permute-start | bytes 27656 | tf_op jit(solution)/shard_map/ppermute | solution.py:39
  196.0 6.7 %collective-permute-start.33 = (bf16[128,512]{1,0:T(8,128)(2,1)}, bf16[128,512]{1,0:T(8,128)(2,1)}, u32[]{:S(2)}, u32[]{:S(2)}) collective-permute-start(bf16[128,512]{1,0:T(8,128)(2,1)} %get-tuple-element.148), channel_id=1, source_target_pairs={{0,4},{4,0},{8,12},{12,8},{16,20},{20,16},{24,28},{28,24},{1,5},{5... | collective-permute-start | bytes 393224 | tf_op jit(solution)/shard_map/ppermute | solution.py:39
  196.5 9.0 %collective-permute-start.35 = (bf16[128,512]{1,0:T(8,128)(2,1)}, bf16[128,512]{1,0:T(8,128)(2,1)}, u32[]{:S(2)}, u32[]{:S(2)}) collective-permute-start(bf16[128,512]{1,0:T(8,128)(2,1)} %get-tuple-element.151), channel_id=1, source_target_pairs={{0,4},{4,0},{8,12},{12,8},{16,20},{20,16},{24,28},{28,24},{1,5},{5... | collective-permute-start | bytes 393224 | tf_op jit(solution)/shard_map/ppermute | solution.py:39
  198.0 10.3 %collective-permute-start.37 = (bf16[128,512]{1,0:T(8,128)(2,1)}, bf16[128,512]{1,0:T(8,128)(2,1)}, u32[]{:S(2)}, u32[]{:S(2)}) collective-permute-start(bf16[128,512]{1,0:T(8,128)(2,1)} %get-tuple-element.150), channel_id=1, source_target_pairs={{0,4},{4,0},{8,12},{12,8},{16,20},{20,16},{24,28},{28,24},{1,5},{5... | collective-permute-start | bytes 393224 | tf_op jit(solution)/shard_map/ppermute | solution.py:39
  202.7 10.4 %collective-permute-start.40 = (bf16[128,896]{1,0:T(8,128)(2,1)}, bf16[128,896]{1,0:T(8,128)(2,1)S(1)}, u32[]{:S(2)}, u32[]{:S(2)}) collective-permute-start(bf16[128,896]{1,0:T(8,128)(2,1)} %get-tuple-element.138), channel_id=1, source_target_pairs={{0,4},{4,0},{8,12},{12,8},{16,20},{20,16},{24,28},{28,24},{1,5},{5... | collective-permute-start | bytes 688136 | tf_op jit(solution)/shard_map/ppermute | solution.py:39
  205.5 12.5 %collective-permute-start.42 = (bf16[128,896]{1,0:T(8,128)(2,1)}, bf16[128,896]{1,0:T(8,128)(2,1)S(1)}, u32[]{:S(2)}, u32[]{:S(2)}) collective-permute-start(bf16[128,896]{1,0:T(8,128)(2,1)} %get-tuple-element.141), channel_id=1, source_target_pairs={{0,4},{4,0},{8,12},{12,8},{16,20},{20,16},{24,28},{28,24},{1,5},{5... | collective-permute-start | bytes 688136 | tf_op jit(solution)/shard_map/ppermute | solution.py:39
  208.3 14.6 %collective-permute-start.44 = (bf16[128,896]{1,0:T(8,128)(2,1)}, bf16[128,896]{1,0:T(8,128)(2,1)S(1)}, u32[]{:S(2)}, u32[]{:S(2)}) collective-permute-start(bf16[128,896]{1,0:T(8,128)(2,1)} %get-tuple-element.140), channel_id=1, source_target_pairs={{0,4},{4,0},{8,12},{12,8},{16,20},{20,16},{24,28},{28,24},{1,5},{5... | collective-permute-start | bytes 688136 | tf_op jit(solution)/shard_map/ppermute | solution.py:39
  213.1 15.0 %collective-permute-start.52 = (bf16[256,512]{1,0:T(8,128)(2,1)}, bf16[256,512]{1,0:T(8,128)(2,1)S(1)}, u32[]{:S(2)}, u32[]{:S(2)}) collective-permute-start(bf16[256,512]{1,0:T(8,128)(2,1)} %get-tuple-element.143), channel_id=1, source_target_pairs={{0,24},{4,28},{8,16},{12,20},{16,8},{20,12},{24,0},{28,4},{1,25},{... | collective-permute-start | bytes 786440 | tf_op jit(solution)/shard_map/ppermute | solution.py:39
  218.0 36.9 %collective-permute-start.46 = (bf16[128,896]{1,0:T(8,128)(2,1)}, bf16[128,896]{1,0:T(8,128)(2,1)}, u32[]{:S(2)}, u32[]{:S(2)}) collective-permute-start(bf16[128,896]{1,0:T(8,128)(2,1)} %get-tuple-element.139), channel_id=1, source_target_pairs={{0,4},{4,0},{8,12},{12,8},{16,20},{20,16},{24,28},{28,24},{1,5},{5... | collective-permute-start | bytes 688136 | tf_op jit(solution)/shard_map/ppermute | solution.py:39
  222.9 8.0 %collective-permute-start.39 = (bf16[128,512]{1,0:T(8,128)(2,1)}, bf16[128,512]{1,0:T(8,128)(2,1)S(1)}, u32[]{:S(2)}, u32[]{:S(2)}) collective-permute-start(bf16[128,512]{1,0:T(8,128)(2,1)} %get-tuple-element.149), channel_id=1, source_target_pairs={{0,4},{4,0},{8,12},{12,8},{16,20},{20,16},{24,28},{28,24},{1,5},{5... | collective-permute-start | bytes 393224 | tf_op jit(solution)/shard_map/ppermute | solution.py:39
  225.6 27.4 %copy-start.12 = (bf16[256,512]{1,0:T(8,128)(2,1)}, bf16[256,512]{1,0:T(8,128)(2,1)S(1)}, u32[]{:S(2)}) copy-start(bf16[256,512]{1,0:T(8,128)(2,1)S(1)} %collective-permute-done.50) | copy-start | bytes 786436
  225.6 8.2 %collective-permute-start.34 = (bf16[128,512]{1,0:T(8,128)(2,1)S(1)}, bf16[128,512]{1,0:T(8,128)(2,1)S(1)}, u32[]{:S(2)}, u32[]{:S(2)}) collective-permute-start(bf16[128,512]{1,0:T(8,128)(2,1)S(1)} %get-tuple-element.145), channel_id=1, source_target_pairs={{0,24},{4,28},{8,16},{12,20},{16,8},{20,12},{24,0},{28,4},{1,25},{... | collective-permute-start | bytes 393224 | tf_op jit(solution)/shard_map/ppermute | solution.py:39
  228.1 19.9 %collective-permute-start.36 = (bf16[128,512]{1,0:T(8,128)(2,1)S(1)}, bf16[128,512]{1,0:T(8,128)(2,1)S(1)}, u32[]{:S(2)}, u32[]{:S(2)}) collective-permute-start(bf16[128,512]{1,0:T(8,128)(2,1)S(1)} %get-tuple-element.147), channel_id=1, source_target_pairs={{0,16},{4,20},{8,24},{12,28},{16,0},{20,4},{24,8},{28,12},{1,17},{... | collective-permute-start | bytes 393224 | tf_op jit(solution)/shard_map/ppermute | solution.py:39
  228.1 19.9 %collective-permute-start.38 = (bf16[128,512]{1,0:T(8,128)(2,1)S(1)}, bf16[128,512]{1,0:T(8,128)(2,1)S(1)}, u32[]{:S(2)}, u32[]{:S(2)}) collective-permute-start(bf16[128,512]{1,0:T(8,128)(2,1)S(1)} %get-tuple-element.146), channel_id=1, source_target_pairs={{0,8},{4,12},{8,0},{12,4},{16,24},{20,28},{24,16},{28,20},{1,9},{5... | collective-permute-start | bytes 393224 | tf_op jit(solution)/shard_map/ppermute | solution.py:39
  231.0 31.1 %collective-permute-start.23 = (bf16[256,1024]{1,0:T(8,128)(2,1)}, bf16[256,1024]{1,0:T(8,128)(2,1)}, u32[]{:S(2)}, u32[]{:S(2)}) collective-permute-start(bf16[256,1024]{1,0:T(8,128)(2,1)} %get-tuple-element.130), channel_id=1, source_target_pairs={{0,1},{1,0},{2,3},{3,2},{4,5},{5,4},{6,7},{7,6},{8,9},{9,8},{10,11... | collective-permute-start | bytes 1572872 | tf_op jit(solution)/shard_map/ppermute | solution.py:39
  233.8 21.1 %collective-permute-start.41 = (bf16[128,896]{1,0:T(8,128)(2,1)}, bf16[128,896]{1,0:T(8,128)(2,1)}, u32[]{:S(2)}, u32[]{:S(2)}) collective-permute-start(bf16[128,896]{1,0:T(8,128)(2,1)} %get-tuple-element.135), channel_id=1, source_target_pairs={{0,24},{4,28},{8,16},{12,20},{16,8},{20,12},{24,0},{28,4},{1,25},{... | collective-permute-start | bytes 688136 | tf_op jit(solution)/shard_map/ppermute | solution.py:39
  248.0 9.5 %collective-permute-start.43 = (bf16[128,896]{1,0:T(8,128)(2,1)}, bf16[128,896]{1,0:T(8,128)(2,1)}, u32[]{:S(2)}, u32[]{:S(2)}) collective-permute-start(bf16[128,896]{1,0:T(8,128)(2,1)} %get-tuple-element.137), channel_id=1, source_target_pairs={{0,16},{4,20},{8,24},{12,28},{16,0},{20,4},{24,8},{28,12},{1,17},{... | collective-permute-start | bytes 688136 | tf_op jit(solution)/shard_map/ppermute | solution.py:39
  248.0 5.0 %collective-permute-start.53 = (bf16[128,512]{1,0:T(8,128)(2,1)S(1)}, bf16[128,512]{1,0:T(8,128)(2,1)S(1)}, u32[]{:S(2)}, u32[]{:S(2)}) collective-permute-start(bf16[128,512]{1,0:T(8,128)(2,1)S(1)} %add_convert_fusion.5), channel_id=1, source_target_pairs={{0,4},{4,0},{8,12},{12,8},{16,20},{20,16},{24,28},{28,24},{1,5},{5... | collective-permute-start | bytes 393224 | tf_op jit(solution)/shard_map/ppermute | solution.py:39
  253.0 6.9 %collective-permute-start.45 = (bf16[128,896]{1,0:T(8,128)(2,1)}, bf16[128,896]{1,0:T(8,128)(2,1)}, u32[]{:S(2)}, u32[]{:S(2)}) collective-permute-start(bf16[128,896]{1,0:T(8,128)(2,1)} %get-tuple-element.136), channel_id=1, source_target_pairs={{0,8},{4,12},{8,0},{12,4},{16,24},{20,28},{24,16},{28,20},{1,9},{5... | collective-permute-start | bytes 688136 | tf_op jit(solution)/shard_map/ppermute | solution.py:39
  254.9 16.9 %collective-permute-start.25 = (bf16[256,1024]{1,0:T(8,128)(2,1)}, bf16[256,1024]{1,0:T(8,128)(2,1)}, u32[]{:S(2)}, u32[]{:S(2)}) collective-permute-start(bf16[256,1024]{1,0:T(8,128)(2,1)} %get-tuple-element.129), channel_id=1, source_target_pairs={{0,1},{1,0},{2,3},{3,2},{4,5},{5,4},{6,7},{7,6},{8,9},{9,8},{10,11... | collective-permute-start | bytes 1572872 | tf_op jit(solution)/shard_map/ppermute | solution.py:39
  254.9 10.3 %collective-permute-start.20 = (bf16[256,1024]{1,0:T(8,128)(2,1)}, bf16[256,1024]{1,0:T(8,128)(2,1)S(1)}, u32[]{:S(2)}, u32[]{:S(2)}) collective-permute-start(bf16[256,1024]{1,0:T(8,128)(2,1)} %get-tuple-element.133), channel_id=1, source_target_pairs={{0,1},{1,0},{2,3},{3,2},{4,5},{5,4},{6,7},{7,6},{8,9},{9,8},{10,11... | collective-permute-start | bytes 1572872 | tf_op jit(solution)/shard_map/ppermute | solution.py:39
  257.5 29.8 %collective-permute-start.22 = (bf16[256,1024]{1,0:T(8,128)(2,1)}, bf16[256,1024]{1,0:T(8,128)(2,1)}, u32[]{:S(2)}, u32[]{:S(2)}) collective-permute-start(bf16[256,1024]{1,0:T(8,128)(2,1)} %get-tuple-element.132), channel_id=1, source_target_pairs={{0,1},{1,0},{2,3},{3,2},{4,5},{5,4},{6,7},{7,6},{8,9},{9,8},{10,11... | collective-permute-start | bytes 1572872 | tf_op jit(solution)/shard_map/ppermute | solution.py:39
  262.1 4.3 %collective-permute-start.47 = (f32[128,256]{1,0:T(8,128)}, f32[128,256]{1,0:T(8,128)S(1)}, u32[]{:S(2)}, u32[]{:S(2)}) collective-permute-start(f32[128,256]{1,0:T(8,128)} %slice.329), channel_id=1, source_target_pairs={{0,1},{1,0},{2,3},{3,2},{4,5},{5,4},{6,7},{7,6},{8,9},{9,8},{10,11... | collective-permute-start | bytes 393224 | tf_op jit(solution)/shard_map/ppermute | solution.py:39
  262.1 6.1 %collective-permute-start.48 = (f32[128,256]{1,0:T(8,128)}, f32[128,256]{1,0:T(8,128)S(1)}, u32[]{:S(2)}, u32[]{:S(2)}) collective-permute-start(f32[128,256]{1,0:T(8,128)} %slice.329), channel_id=1, source_target_pairs={{0,2},{1,3},{2,0},{3,1},{4,6},{5,7},{6,4},{7,5},{8,10},{9,11},{10,... | collective-permute-start | bytes 393224 | tf_op jit(solution)/shard_map/ppermute | solution.py:39
  265.2 5.9 %collective-permute-start.49 = (f32[128,256]{1,0:T(8,128)}, f32[128,256]{1,0:T(8,128)S(1)}, u32[]{:S(2)}, u32[]{:S(2)}) collective-permute-start(f32[128,256]{1,0:T(8,128)} %slice.329), channel_id=1, source_target_pairs={{0,3},{1,2},{2,1},{3,0},{4,7},{5,6},{6,5},{7,4},{8,11},{9,10},{10,... | collective-permute-start | bytes 393224 | tf_op jit(solution)/shard_map/ppermute | solution.py:39
  266.3 16.6 %collective-permute-start.24 = (bf16[256,1024]{1,0:T(8,128)(2,1)}, bf16[256,1024]{1,0:T(8,128)(2,1)S(1)}, u32[]{:S(2)}, u32[]{:S(2)}) collective-permute-start(bf16[256,1024]{1,0:T(8,128)(2,1)} %add_convert_fusion), channel_id=1, source_target_pairs={{0,2},{1,3},{2,0},{3,1},{4,6},{5,7},{6,4},{7,5},{8,10},{9,11},{10,... | collective-permute-start | bytes 1572872 | tf_op jit(solution)/shard_map/ppermute | solution.py:39
  268.2 25.5 %collective-permute-start.21 = (bf16[256,1024]{1,0:T(8,128)(2,1)S(1)}, bf16[256,1024]{1,0:T(8,128)(2,1)S(1)}, u32[]{:S(2)}, u32[]{:S(2)}) collective-permute-start(bf16[256,1024]{1,0:T(8,128)(2,1)S(1)} %add_convert_fusion.1), channel_id=1, source_target_pairs={{0,2},{1,3},{2,0},{3,1},{4,6},{5,7},{6,4},{7,5},{8,10},{9,11},{10,... | collective-permute-start | bytes 1572872 | tf_op jit(solution)/shard_map/ppermute | solution.py:39
  (18 other events, 73.8 us)

commit v2 on v1

--- a/solution.py
+++ b/solution.py
@@ -39,45 +39,77 @@
     return lax.ppermute(value, axis, [(i, i ^ bits) for i in range(size)])
 
 
-def gather(value, axis):
+def order_of(size):
+    return list(range(0, size, 2)) + list(range(1, size, 2))
+
+
+def position(k, size):
+    return k // 2 + (k % 2) * ((size + 1) // 2)
+
+
+def at_position(p, size):
+    half = (size + 1) // 2
+    return jnp.where(p < half, 2 * p, 2 * (p - half) + 1)
+
+
+def gather_far(value, axis):
+    pieces = {0: value}
+    for k in range(2, lax.axis_size(axis), 2):
+        pieces[k] = swap(value, axis, k)
+    return pieces
+
+
+def gather_near(pieces, axis):
     size = lax.axis_size(axis)
-    pieces = {0: value}
-    for k in range(2, size, 2):
-        pieces[k] = swap(value, axis, k)
+    pieces = dict(pieces)
     if size > 1:
         for k in range(0, size, 2):
             pieces[k ^ 1] = swap(pieces[k], axis, 1)
     return [pieces[k] for k in range(size)]
 
 
-def near_first(parts, axis):
+def gather(value, axis):
+    return gather_near(gather_far(value, axis), axis)
+
+
+def near_first(own, near, axis):
     size = lax.axis_size(axis)
-    rows = parts.shape[0] // size
-
-    def piece(k):
-        return parts[k * rows : (k + 1) * rows]
-
-    terms = [piece(0)]
     if size == 1:
-        return terms
-    for k in range(size - 2, 0, -2):
-        other = swap(piece(k ^ 1), axis, 1)
-        both = piece(k).astype(f32) + other.astype(f32)
-        terms.append(swap(both.astype(bf16), axis, k))
-    terms.append(swap(piece(1), axis, 1))
+        return [(own, 0)]
+    half = size // 2
+    rows = own.shape[0] // half
+    terms = [(own, 0)]
+    sent_on = []
+    start = half
+    for sent in near:
+        other = swap(sent, axis, 1)
+        other, *_ = lax.optimization_barrier((other, *sent_on))
+        stop, start = start, start - sent.shape[0] // rows
+        for i in range(stop - 1, start - 1, -1):
+            if i == 0:
+                terms.append((other, 0))
+                continue
+            got = other[(i - start) * rows : (i - start + 1) * rows]
+            both = own[i * rows : (i + 1) * rows].astype(f32) + got.astype(f32)
+            sent_on.append(both.astype(bf16))
+            terms.append((swap(sent_on[-1], axis, 2 * i), 0))
     return terms
 
 
-def far_first(parts, axis):
-    size = lax.axis_size(axis)
-    rows = parts.shape[0] // size
-    if size == 1:
-        return [parts]
-    pairs = [parts[: 2 * rows]]
-    for k in range(2, size, 2):
-        pairs.append(swap(parts[k * rows : (k + 2) * rows], axis, k))
-    other = sum(pair[rows:].astype(f32) for pair in pairs).astype(bf16)
-    return [pair[:rows] for pair in pairs] + [swap(other, axis, 1)]
+def far_first(pairs, axis):
+    if lax.axis_size(axis) == 1:
+        return [(pairs[0], 0)]
+    rows = pairs[0].shape[0] // 2
+    got = [pairs[0]]
+    for i in range(1, len(pairs)):
+        got.append(swap(pairs[i], axis, 2 * i))
+    other = sum(both[rows:].astype(f32) for both in got).astype(bf16)
+    return [(both, 0) for both in got] + [(swap(other, axis, 1), 0)]
+
+
+def block_of(term, rows):
+    array, index = term
+    return array[index * rows : (index + 1) * rows].astype(f32)
 
 
 def total_of(terms):
@@ -127,10 +159,11 @@
             out[...] = ref[...]
 
 
-def join(out, refs):
+def join(out, refs, start=0):
     rows = refs[0].shape[0]
+    cols = out.shape[1]
     for k, ref in enumerate(refs):
-        out[k * rows : (k + 1) * rows, :] = ref[...]
+        out[k * rows : (k + 1) * rows, :] = ref[:, start : start + cols]
 
 
 def forward_kernel(width, head_dim, count, pieces, per, start):
@@ -202,11 +235,12 @@
                 [jnp.broadcast_to(logs[:, h : h + 1], (size, LANES)) for h in heads], lane_head
             )
             xs = x_g * step_e
+            xs_half = xs.astype(bf16)
             total = skip[0:1, lanes] * x_g
             for j, h in enumerate(heads):
                 gap = logs[:, h : h + 1] - logs_t[h : h + 1, :]
-                weights_h = scores * jnp.exp(jnp.minimum(gap, 0.0))
-                total = total + fine(weights_h, jnp.where(lane_head == j, xs, 0.0))
+                weights_h = (scores * jnp.exp(jnp.minimum(gap, 0.0))).astype(bf16)
+                total = total + mm(weights_h, jnp.where(lane_head == j, xs_half, 0.0))
             old = state[:, lanes]
             before[0, :, lanes] = old.astype(bf16)
             total = total + jnp.exp(log_e) * fine(queries, old)
@@ -280,6 +314,7 @@
                 [jnp.broadcast_to(logs[:, h : h + 1], (size, LANES)) for h in heads], lane_head
             )
             xs = x_g * step_e
+            xs_half, dy_half = xs.astype(bf16), dy.astype(bf16)
             last = log_e[size - 1 : size, :]
             fade = jnp.exp(last - log_e)
             old = before[0, :, lanes]
@@ -291,9 +326,9 @@
                 gap = logs_t[h : h + 1, :] - logs[:, h : h + 1]
                 decay = jnp.exp(jnp.minimum(gap, 0.0))
                 dxs = dxs + mm(
-                    (scores_t * decay).astype(bf16), jnp.where(mine, dy, 0.0).astype(bf16)
+                    (scores_t * decay).astype(bf16), jnp.where(mine, dy_half, 0.0)
                 )
-                d_scores_t = d_scores_t + decay * fine(jnp.where(mine, xs, 0.0), dy, NT)
+                d_scores_t = d_scores_t + decay * mm(jnp.where(mine, xs_half, 0.0), dy_half, NT)
             e_dy = jnp.exp(log_e) * dy
             d_queries = d_queries + sum(mm(half, old, NT) for half in halves(e_dy))
             d_keys = d_keys + fine(fade * xs, d_new, NT)
@@ -355,25 +390,25 @@
 
 def gate_kernel(count, pieces, parts):
     def kernel(place, *refs):
-        token_refs, refs = refs[:count], refs[count:]
+        normed_refs, upstream_refs, refs = refs[:count], refs[count : 2 * count], refs[2 * count :]
         weight_refs, refs = refs[:pieces], refs[pieces:]
-        mixed, gain, gate_raw, grad_scaled, sums, tokens, weights = refs
+        mixed, gain, gate_raw, grad_scaled, sums, normed, upstream, w_gate, w_out = refs
 
         @pl.when(pl.program_id(0) == 0)
         def _():
-            join(weights, weight_refs)
-
-        take(tokens, token_refs, pl.program_id(0) // parts)
-        gate_body(tokens, weights, mixed, gain, gate_raw, grad_scaled, sums)
+            join(w_gate, [weight_refs[k] for k in order_of(pieces)])
+            join(w_out, weight_refs, w_gate.shape[1])
+
+        take(normed, normed_refs, pl.program_id(0) // parts)
+        take(upstream, upstream_refs, pl.program_id(0) // parts)
+        gate_body(normed, upstream, w_gate, w_out, mixed, gain, gate_raw, grad_scaled, sums)
 
     return kernel
 
 
-def gate_body(tokens, weights, mixed, gain, gate_raw, grad_scaled, sums):
-    model = weights.shape[0]
-    inner = mixed.shape[1]
-    gate = mm(tokens[:, :model], weights[:, :inner])
-    grads = mm(tokens[:, model:], weights[:, inner:])
+def gate_body(normed, upstream, w_gate, w_out, mixed, gain, gate_raw, grad_scaled, sums):
+    gate = mm(normed[...], w_gate[...])
+    grads = mm(upstream[...], w_out[...])
     gate_raw[...] = gate
     grad_scaled[...] = grads
     gated = mixed[...] * (gate * jax.nn.sigmoid(gate))
@@ -414,17 +449,42 @@
     return kernel
 
 
+def place_of(place, k, blocks, size):
+    return pl.multiple_of(position(place[0] ^ k, blocks) * size, size)
+
+
 def entry_kernel(blocks):
-    def kernel(place, tokens, upstream, gain, out):
-        model = tokens.shape[1]
-        size = model // blocks
+    def kernel(place, tokens, upstream, gain, normed_out, upstream_out):
+        size = tokens.shape[1] // blocks
         wide = tokens[...].astype(f32)
         inverse = lax.rsqrt(jnp.mean(wide * wide, axis=-1, keepdims=True) + epsilon)
         normed = (wide * inverse * gain[...]).astype(bf16)
         for k in range(blocks):
-            at = pl.multiple_of((place[0] ^ k) * size, size)
-            out[:, pl.ds(at, size)] = normed[:, k * size : (k + 1) * size]
-            out[:, pl.ds(model + at, size)] = upstream[:, k * size : (k + 1) * size]
+            at = pl.ds(place_of(place, k, blocks, size), size)
+            normed_out[:, at] = normed[:, k * size : (k + 1) * size]
+            at = pl.ds(pl.multiple_of((place[0] ^ k) * size, size), size)
+            upstream_out[:, at] = upstream[:, k * size : (k + 1) * size]
+
+    return kernel
+
+
+def pack_kernel(blocks, cols):
+    def kernel(place, grad_x, grad_gain, grad_bc, grad_head, pre_part, gain, out, row):
+        twice = grad_bc.shape[1]
+        inner = grad_x.shape[1]
+        model = row.shape[1]
+        size = model // blocks
+        out[...] = jnp.zeros(out.shape, f32)
+        out[0:8, :inner] = grad_x[...]
+        out[8:16, :inner] = grad_gain[...]
+        out[16:24, :twice] = grad_bc[...]
+        out[16:24, twice : twice + LANES] = grad_head[...]
+        for k in range(blocks):
+            at = pl.ds(place_of(place, k, blocks, size), size)
+            row[:, k * size : (k + 1) * size] = pre_part[:, at]
+        for k in range(model // cols):
+            part = slice(k * cols, (k + 1) * cols)
+            out[24 + k : 25 + k, :] = row[0:1, part] / gain[0:1, part]
 
     return kernel
 
@@ -451,7 +511,7 @@
         wide = tokens[...].astype(f32)
         inverse = lax.rsqrt(jnp.mean(wide * wide, axis=-1, keepdims=True) + epsilon)
         for k in range(blocks):
-            at = pl.multiple_of((place[0] ^ k) * size, size)
+            at = place_of(place, k, blocks, size)
             total = refs[0][:, pl.ds(at, size)].astype(f32)
             for term in refs[1:count]:
                 total = total + term[:, pl.ds(at, size)].astype(f32)
@@ -467,9 +527,10 @@
     return kernel
 
 
-def normed_kernel(place, tokens, d_gate, columns, w_gate, w_scan, out, grad_gain):
+def normed_kernel(place, tokens, d_gate, columns, w_gate, w_scan, own, near, grad_gain):
     total = mm(d_gate[...], w_gate[...], NT) + mm(columns[...], w_scan[...], NT)
-    out[...] = total.astype(bf16)
+    own[...] = total[: own.shape[0]].astype(bf16)
+    near[...] = total[-near.shape[0] :].astype(bf16)
     total = total * tokens[...].astype(f32)
     grad_gain[...] = jnp.broadcast_to(jnp.sum(total, axis=0, keepdims=True), grad_gain.shape)
 
@@ -494,16 +555,21 @@
     )
 
 
-def exchange_blocks(values, axis, blocks):
+def exchange_blocks(values, axis, blocks, back=False, ordered=True):
     index = lax.axis_index(axis)
-    rows, cols = values.shape
+    order = order_of(blocks)
+    blocked = values.reshape(values.shape[0], blocks, -1)
+    if back and ordered:
+        blocked = jnp.stack([blocked[:, order.index(k)] for k in range(blocks)], axis=1)
     bits = 1
     while bits < blocks:
-        split = values.reshape(rows, blocks // (2 * bits), 2, bits * (cols // blocks))
-        split = jnp.where((index & bits) != 0, split[:, :, ::-1], split)
-        values = split.reshape(rows, cols)
+        split = blocked.reshape(blocked.shape[0], blocks // (2 * bits), 2, -1)
+        blocked = jnp.where((index & bits) != 0, split[:, :, ::-1], split)
+        blocked = blocked.reshape(blocked.shape[0], blocks, -1)
         bits *= 2
-    return values
+    if ordered and not back:
+        blocked = jnp.stack([blocked[:, k] for k in order], axis=1)
+    return blocked.reshape(values.shape)
 
 
 def per_device(
@@ -532,6 +598,7 @@
     blocks = 1 if narrow else dp
     place_entry = place_dp * 0 if narrow else place_dp
 
+    slab = rows_local
     tokens_local = block_input.reshape(rows_local, model)
     upstream_local = cotangent.reshape(rows_local, model)
     gain_in = pre_gain.reshape(1, model)
@@ -539,19 +606,15 @@
         [w_zx[:, 1, :], w_bc, w_dt, jnp.zeros((w_dt.shape[0], LANES - heads), bf16)], axis=1
     )
     w_late = jnp.concatenate([w_zx[:, 0, :], w_out.T], axis=1)
-    (both_local,) = call(
-        entry_kernel(blocks), 1,
-        [whole((rows_local, model)), whole((rows_local, model)), whole((1, model))],
-        [whole((rows_local, 2 * model))],
-        [((rows_local, 2 * model), bf16)],
+    normed_local, upstream_sent = call(
+        entry_kernel(blocks), rows_local // slab,
+        [rows_of(slab, model), rows_of(slab, model), whole((1, model))],
+        [rows_of(slab, model)] * 2,
+        [((rows_local, model), bf16)] * 2,
     )(place_entry, tokens_local, upstream_local, gain_in)
     if narrow:
-        both_local = jnp.concatenate(
-            [exchange_blocks(half, "dp", dp) for half in jnp.split(both_local, 2, axis=1)], axis=1
-        )
-    scan_pieces = gather(w_scan, "dp")
-    token_pieces = gather(both_local, "tensor")
-    late_pieces = gather(w_late, "dp")
+        normed_local = exchange_blocks(normed_local, "dp", dp)
+        upstream_sent = exchange_blocks(upstream_sent, "dp", dp, ordered=False)
 
     def stack(rows, cols):
         rows = [r.reshape(-1, r.shape[-1]) for r in rows]
@@ -563,11 +626,25 @@
     per_head = stack([dt_bias, -jnp.exp(a_log)], LANES)
     skip = jnp.repeat(d_skip, head_dim).reshape(1, inner)
     gain = gate_gain.reshape(1, inner)
+    forward_shapes = [((states, inner), f32), ((8, inner), f32), ((8, twice), f32)]
+    backward_shapes = [((8, inner), f32), ((8, twice), f32), ((8, LANES), f32)]
+    backward_shapes += [((states, inner), f32)] * 2 + [((8, inner), f32), ((8, twice), f32)]
+    forward_carry = [jnp.zeros(*one) for one in forward_shapes]
+
+    scan_far = gather_far(w_scan, "dp")
+    scan_far[0], taps_x, taps_bc, per_head, skip, gain, forward_carry = lax.optimization_barrier(
+        (scan_far[0], taps_x, taps_bc, per_head, skip, gain, forward_carry)
+    )
+    scan_pieces = gather_near(scan_far, "dp")
+    normed_pieces = gather(normed_local, "tensor")
+    late_pieces = gather(w_late, "dp")
+    upstream_pieces = gather(upstream_sent, "tensor")
+    dp_order, tensor_order = order_of(dp), order_of(tensor)
 
     per = rows_local // chunk
 
     def stored(c, place):
-        return ((c // per) ^ place[0]) * per + c % per
+        return position((c // per) ^ place[0], tensor) * per + c % per
 
     def ahead(cols, start):
         return pl.BlockSpec((chunk, cols), lambda c, place: (stored(c + start, place), 0))
@@ -585,13 +662,13 @@
     anywhere = pl.BlockSpec(memory_space=pl.ANY)
     calls = 2 if chunks % 2 == 0 else 1
     span = chunks // calls
-    carry_shapes = [((states, inner), f32), ((8, inner), f32), ((8, twice), f32)]
-    carry = [jnp.zeros(*one) for one in carry_shapes]
-    saved, weights = [], scan_pieces
-    for start in range(0, chunks, span):
+    first = -(-chunks * 5 // 8)
+    carry = forward_carry
+    saved, weights = [], [scan_pieces[k] for k in dp_order]
+    for start, stop in ((0, first), (first, chunks)):
         results = call(
             forward_kernel(width, head_dim, tensor, len(weights), per, start),
-            span,
+            stop - start,
             [token_piece(k, start) for k in range(tensor)]
             + [whole(one.shape) for one in weights]
             + [whole((8, inner)), whole((8, twice)), whole((8, LANES)), whole((1, inner))]
@@ -604,7 +681,7 @@
             [
                 ((length, inner), f32), ((length, twice), f32), ((length, inner), bf16),
                 ((length, twice), bf16), ((length, LANES), f32), ((length, inner), f32),
-                ((chunks, states, inner), bf16), *carry_shapes,
+                ((chunks, states, inner), bf16), *forward_shapes,
             ]
             + [((model, wide_cols), bf16)] * (start == 0),
             [
@@ -612,7 +689,7 @@
                 pltpu.VMEM((chunk, model), bf16),
             ],
             {1 + tensor + len(weights) + 7 + k: k for k in range(len(saved))},
-        )(place_tensor, *token_pieces, *weights, taps_x, taps_bc, per_head, skip, *carry, *saved)
+        )(place_tensor, *normed_pieces, *weights, taps_x, taps_bc, per_head, skip, *carry, *saved)
         saved, carry = results[:7], results[7:10]
         if start == 0:
             full_scan = results[10]
@@ -621,28 +698,33 @@
 
     parts = rows_local // block
     in_order = pl.BlockSpec(
-        (1, 8, block), lambda c, place: (((c // parts) ^ place[0]) * parts + c % parts, 0, 0)
+        (1, 8, block), lambda c, place: ((at_position(c // parts, tensor) ^ place[0]) * parts + c % parts, 0, 0)
     )
 
-    def gate_piece(k):
+    def gate_piece(p):
         return pl.BlockSpec(
-            (block, 2 * model), lambda c, place: (jnp.where(c // parts == k, c % parts, 0), 0)
+            (block, model), lambda c, place: (jnp.where(c // parts == p, c % parts, 0), 0)
         )
 
-    gate_raw, grad_scaled, sums, tokens, full_late = call(
+    gate_raw, grad_scaled, sums, normed, upstream, full_gate, full_out = call(
         gate_kernel(tensor, dp, parts), length // block,
-        [gate_piece(k) for k in range(tensor)]
+        [gate_piece(p) for p in range(tensor)] * 2
         + [whole((model // dp, 2 * inner))] * dp
         + [rows_of(block, inner), whole((1, inner))],
         [
-            rows_of(block, inner), rows_of(block, inner), in_order, rows_of(block, 2 * model),
-            whole((model, 2 * inner)),
+            rows_of(block, inner), rows_of(block, inner), in_order, rows_of(block, model),
+            rows_of(block, model), whole((model, inner)), whole((model, inner)),
         ],
         [
             ((length, inner), f32), ((length, inner), f32), ((length // block, 8, block), f32),
-            ((length, 2 * model), bf16), ((model, 2 * inner), bf16),
+            ((length, model), bf16), ((length, model), bf16), ((model, inner), bf16),
+            ((model, inner), bf16),
         ],
-    )(place_tensor, *token_pieces, *late_pieces, mixed, gain)
+    )(
+        place_tensor, *[normed_pieces[k] for k in tensor_order],
+        *[upstream_pieces[k] for k in tensor_order], *late_pieces,
+        mixed, gain,
+    )
 
     sum_terms = direct_terms(sums, "tensor")
 
@@ -657,27 +739,38 @@
         ],
     )(place_tensor, *sum_terms, gate_raw, grad_scaled, mixed, gain)
 
-    normed = tokens[:, :model]
-    upstream = tokens[:, model:]
-    out_part = lax.dot_general(upstream, scaled, TN, preferred_element_type=f32).astype(bf16)
-    gate_part = lax.dot_general(normed, d_gate, TN, preferred_element_type=f32).astype(bf16)
-    branch_part = mm(scaled, full_late[:, inner:], NT).astype(bf16)
-    out_terms = far_first(out_part, "dp")
-    gate_terms = near_first(gate_part, "dp")
-    branch_terms = near_first(branch_part, "tensor")
+    def tn(left, right):
+        return lax.dot_general(left, right, TN, preferred_element_type=f32).astype(bf16)
+
+    share = model // dp
+    out_pairs = [tn(upstream[:, k * share : (k + 2) * share], scaled) for k in range(0, dp, 2)]
+    even = share * ((dp + 1) // 2)
+    gate_near = tn(normed[:, even:], d_gate)
+    gate_own = tn(normed[:, :even], d_gate)
+    stay = rows_local * ((tensor + 1) // 2)
+    branch_near = mm(scaled[stay:], full_out, NT).astype(bf16)
+    branch_own = mm(scaled[:stay], full_out, NT).astype(bf16)
+    out_terms = far_first(out_pairs, "dp")
+    gate_terms = near_first(gate_own, [gate_near], "dp")
+    branch_terms = near_first(branch_own, [branch_near], "tensor")
     if narrow:
-        branch_terms = [exchange_blocks(term, "dp", dp) for term in branch_terms]
-    out_block = pl.BlockSpec((rows_local, 1, model), lambda c, place: (0, 0, 0))
+        branch_terms = [
+            (exchange_blocks(array, "dp", dp, True, False), k) for array, k in branch_terms
+        ]
+    slabs = rows_local // slab
+    out_block = pl.BlockSpec((slab, 1, model), lambda c, place: (c, 0, 0))
+
+    def one_block(k):
+        return pl.BlockSpec((slab, model), lambda c, place: (k * slabs + c, 0))
+
     (block_output,) = call(
-        output_kernel(blocks, len(branch_terms)), 1,
-        [whole((rows_local, model))] * (1 + len(branch_terms)),
+        output_kernel(blocks, len(branch_terms)), slabs,
+        [rows_of(slab, model)] + [one_block(k) for _, k in branch_terms],
         [out_block],
         [((rows_local, 1, model), f32)],
-    )(place_entry, tokens_local, *branch_terms)
-
-    carry_shapes = [((8, inner), f32), ((8, twice), f32), ((8, LANES), f32)]
-    carry_shapes += [((states, inner), f32)] * 2 + [((8, inner), f32), ((8, twice), f32)]
-    carry = [jnp.zeros(*one) for one in carry_shapes]
+    )(place_entry, tokens_local, *[array for array, _ in branch_terms])
+
+    carry = [jnp.zeros(*one) for one in backward_shapes]
     columns = []
     for at in range(calls):
         start = chunks - 1 - at * span
@@ -689,7 +782,7 @@
             + [whole(one.shape) for one in carry]
             + [anywhere] * len(columns),
             [back(wide_cols, start)] + [whole(one.shape) for one in carry],
-            [((length, wide_cols), bf16), *carry_shapes],
+            [((length, wide_cols), bf16), *backward_shapes],
             [pltpu.VMEM((chunk + 8, inner), f32), pltpu.VMEM((chunk + 8, twice), f32)],
             {1 + 8 + 4 + 7: 0} if columns else {},
         )(
@@ -700,10 +793,15 @@
     columns = columns[0]
     grad_x, grad_bc, grad_head = carry[:3]
 
-    scan_part = lax.dot_general(normed, columns, TN, preferred_element_type=f32).astype(bf16)
-    scan_terms = near_first(scan_part, "dp")
+    later = even + (model - even) // 2 if dp % 4 == 0 else even
+    scan_near = [tn(normed[:, later:], columns)]
+    if later > even:
+        scan_near.append(tn(normed[:, even:later], columns))
+    scan_own = tn(normed[:, :even], columns)
+    scan_terms = near_first(scan_own, scan_near, "dp")
     features = model // 4
-    normed_part, pre_part = call(
+    leave = max(length - stay, rows_local)
+    normed_own, normed_near, pre_part = call(
         normed_kernel, 4,
         [
             pl.BlockSpec((length, features), lambda c, place: (0, c)),
@@ -711,44 +809,60 @@
             rows_of(features, inner), rows_of(features, wide_cols),
         ],
         [
-            pl.BlockSpec((length, features), lambda c, place: (0, c)),
+            pl.BlockSpec((stay, features), lambda c, place: (0, c)),
+            pl.BlockSpec((leave, features), lambda c, place: (0, c)),
             pl.BlockSpec((8, features), lambda c, place: (0, c)),
         ],
-        [((length, model), bf16), ((8, model), f32)],
-    )(place_tensor, tokens, d_gate, columns, full_late, full_scan)
-    normed_terms = near_first(normed_part, "tensor")
+        [((stay, model), bf16), ((leave, model), bf16), ((8, model), f32)],
+    )(place_tensor, normed, d_gate, columns, full_gate, full_scan)
+    normed_terms = near_first(normed_own, [normed_near], "tensor")
     if narrow:
-        normed_terms = [exchange_blocks(term, "dp", dp) for term in normed_terms]
-    input_grad, _ = call(
-        input_kernel(blocks, len(normed_terms)), 1,
-        [whole((rows_local, model))] * 2 + [whole((1, model))]
-        + [whole((rows_local, model))] * len(normed_terms),
-        [out_block, whole((rows_local, model))],
-        [((rows_local, 1, model), f32), ((rows_local, model), f32)],
-    )(place_entry, tokens_local, upstream_local, gain_in, *normed_terms)
-
-    grad_w_scan = total_of(scan_terms)
-    grad_w_out = total_of(out_terms).T
-    grad_w_gate = total_of(gate_terms)
-    grad_w_bc = total_of(direct_terms(grad_w_scan[:, inner : inner + twice], "tensor"))
+        normed_terms = [(exchange_blocks(array, "dp", dp, True), k) for array, k in normed_terms]
+    (input_grad,) = call(
+        input_kernel(blocks, len(normed_terms)), slabs,
+        [rows_of(slab, model)] * 2 + [whole((1, model))]
+        + [one_block(k) for _, k in normed_terms],
+        [out_block], [((rows_local, 1, model), f32)], [pltpu.VMEM((slab, model), f32)],
+    )(place_entry, tokens_local, upstream_local, gain_in, *[array for array, _ in normed_terms])
+
+    grad_w_scan = sum(block_of(term, share) for term in scan_terms)
+    grad_w_out = sum(block_of(term, share) for term in out_terms).T
+    grad_w_gate = sum(block_of(term, share) for term in gate_terms)
+    cols = max(inner, twice + LANES)
+    cols += -cols % 512
+    if narrow:
+        pre_part = exchange_blocks(pre_part, "dp", dp, True)
+    rows = 24 + max(model // cols, 8)
+    (packed,) = call(
+        pack_kernel(blocks, cols), 1,
+        [
+            whole((8, inner)), whole((8, inner)), whole((8, twice)), whole((8, LANES)),
+            whole((8, model)), whole((1, model)),
+        ],
+        [whole((rows, cols))], [((rows, cols), f32)], [pltpu.VMEM((8, model), f32)],
+    )(place_entry, grad_x, grad_gain, grad_bc, grad_head, pre_part, gain_in)
+    small = all_sum(packed, "dp")
+
+    assert cols % twice == 0 and model % cols == 0
+    across = [small[16:, k : k + twice] for k in range(0, cols, twice)]
+    across = jnp.concatenate(across, axis=0)
+    keys_rows = grad_w_scan.shape[0]
+    across = jnp.concatenate([grad_w_scan[:, inner : inner + twice], across], axis=0)
+    across = total_of(direct_terms(across, "tensor"))
+    grad_w_bc = across[:keys_rows]
+    of_bc = across[keys_rows:]
+    count = rows - 16
+    pre_rows = [of_bc[k * count + 8 : k * count + 8 + model // cols] for k in range(cols // twice)]
+    sum_pre = jnp.concatenate(pre_rows, axis=1).reshape(-1)
     grad_w_dt = grad_w_scan[:, inner + twice : inner + twice + heads]
     grad_w_zx = jnp.stack([grad_w_gate, grad_w_scan[:, :inner]], axis=1)
-
-    pre_part = exchange_blocks(pre_part[:1], "dp", dp)[0] / pre_gain
-    kept = width + 2
-    local = jnp.concatenate([grad_x[:kept].reshape(-1), grad_gain[0], grad_head[:2].reshape(-1)])
-    shared = jnp.concatenate([grad_bc[: width + 1].reshape(-1), pre_part])
-    small = all_sum(jnp.concatenate([local, shared]), "dp")
-    local = small[: local.shape[0]]
-    shared = total_of(direct_terms(small[local.shape[0] :], "tensor"))
-    of_x = local[: kept * inner].reshape(kept, inner)
-    sum_gain = local[kept * inner : (kept + 1) * inner]
-    of_head = local[(kept + 1) * inner :].reshape(2, LANES)
-    of_bc = shared[: (width + 1) * twice].reshape(width + 1, twice)
+    of_x = small[:8, :inner]
+    sum_gain = small[8, :inner]
+    of_head = small[16:24, twice : twice + LANES]
     return (
         block_output,
         input_grad,
-        shared[(width + 1) * twice :],
+        sum_pre,
         grad_w_zx,
         grad_w_dt,
         grad_w_bc,

time: 299 us -> 303 us (1.013)
  local copies, waits for them, and re-layouts: 25.7 us -> 16.4 us
  waiting for transfers between devices: 103 us -> 110 us
  matrix products: 14.2 us -> 19.4 us
  starting transfers between devices: 55.5 us -> 60.4 us
    ppermute x54 -> x47, waiting for transfers between devices: 103 us -> 110 us  [swap(): return lax.ppermute(value, axis, [(i, i ^ bits) for i in range(size)])]
    slice x11 -> x4, local copies, waits for them, and re-layouts: 8.58 us -> 1.86 us  [the longest x1 0.66 us: per_device(): grad_w_bc = across[:keys_rows]]
    dot_general x3 -> x9, matrix products: 11.3 us -> 16.9 us  [tn(): lax.dot_general(left, right, TN, preferred_element_type=f32).astype(bf16)]
    ppermute x54 -> x47, starting transfers between devices: 55.5 us -> 60.4 us  [swap(): return lax.ppermute(value, axis, [(i, i ^ bits) for i in range(size)])]
    unnamed x68 -> x82, local copies, waits for them, and re-layouts: 8.54 us -> 6.68 us
    convert_element_type x5 -> x6, other arithmetic: 6.76 us -> 5.91 us  [the longest x5 5.84 us: near_first(): sent_on.append(both.astype(bf16))]
    pallas_call x4 -> x5, Pallas kernels: 19.1 us -> 19.8 us  [the longest x1 8.95 us: per_device(): call(gate_kernel(tensor, dp, parts), length // block, [gate_piece(p) for...]
  transfers between devices with their start and end apart: 54 -> 47, of which waited for: 23 -> 19; matrix products, arithmetic and copies ran while one was open for 13% -> 8% of each run, Pallas kernels for 8% -> 9%
where the time goes in v2:
time: 303 us; the launch traced here: 302 us
  waiting for transfers between devices  110 us (36%)
  Pallas kernels  78.5 us (26%)
  starting transfers between devices  60.4 us (20%)
  matrix products  19.4 us (6%)
  other arithmetic  16.5 us (5%)
  local copies, waits for them, and re-layouts  16.4 us (5%)
    ppermute x47, waiting for transfers between devices, swap(): return lax.ppermute(value, axis, [(i, i ^ bits) for i in range(size)])  110 us
    ppermute x47, starting transfers between devices, swap(): return lax.ppermute(value, axis, [(i, i ^ bits) for i in range(size)])  60.4 us
    pallas_call x2, Pallas kernels, per_device(): call(backward_kernel(width, head_dim, len(columns)), span, [back(cols, st...  24 us
    pallas_call x2, Pallas kernels, per_device(): call(forward_kernel(width, head_dim, tensor, len(weights), per, start), s...  20.5 us
    dot_general x9, matrix products, tn(): lax.dot_general(left, right, TN, preferred_element_type=f32).astype(bf16)  16.9 us
    pallas_call x1, Pallas kernels, per_device(): call(gate_kernel(tensor, dp, parts), length // block, [gate_piece(p) for...  8.95 us
    pallas_call x1, Pallas kernels, per_device(): call(normed_kernel, 4, [pl.BlockSpec((length, features), lambda c, place:...  7.94 us
    unnamed x82, local copies, waits for them, and re-layouts  6.68 us
  transfers between devices with their start and end apart: 47, of which 19 were waited for; matrix products, arithmetic and copies ran while one was open for 8% of the time, Pallas kernels for 9%

profile of v2, /device:TPU:0, one launch (start us, length us, event | category | flops | bytes accessed | tf_op | source)
XLA Modules:
  0.0 302.0 jit_solution(5246274675574032444)
XLA Ops:
  0.7 1.5 fusion.11
  5.1 1.3 select_maximum_fusion.refs_12_.refs_5_.refs_8_
  6.5 1.3 select_maximum_fusion.1.refs_13_.refs_6_.refs_9_
  7.8 1.3 select_maximum_fusion.2.refs_14_.refs_7_.refs_10_
  9.9 3.0 %collective-permute-start.16 = (bf16[128,896]{1,0:T(8,128)(2,1)S(1)}, bf16[128,896]{1,0:T(8,128)(2,1)S(1)}, u32[]{:S(2)}, u32[]{:S(2)}) collective-permute-start(bf16[128,896]{1,0:T(8,128)(2,1)S(1)} %maximum_maximum_fusion.refs_4_), channel_id=1, source_target_pairs={{0,4},{4,0},{8,12},{12,8},{16,20},{20,16},{24,28},{28,24},{1,5},{5... | collective-permute-start | bytes 688136 | tf_op jit(solution)/shard_map/ppermute | solution.py:39
  12.9 1.6 collective-permute-start.13
  14.5 2.6 collective-permute-start.14
  17.1 2.5 shard_map.262
  19.6 1.5 collective-permute-start
  21.7 2.5 collective-permute-start.15
  24.8 2.5 collective-permute-start.11
  27.3 16.1 %collective-permute-done.14.refs_6_ = bf16[128,896]{1,0:T(8,128)(2,1)S(1)} collective-permute-done((bf16[128,896]{1,0:T(8,128)(2,1)S(1)}, bf16[128,896]{1,0:T(8,128)(2,1)S(1)}, u32[]{:S(2)}, u32[]{:S(2)}) %collective-permute-start.14) | collective-permute-done | bytes 229408 | tf_op jit(solution)/shard_map/ppermute | solution.py:39
  43.4 2.0 collective-permute-start.3
  45.5 9.7 %collective-permute-start.7 = (bf16[128,1024]{1,0:T(8,128)(2,1)S(1)}, bf16[128,1024]{1,0:T(8,128)(2,1)}, u32[]{:S(2)}, u32[]{:S(2)}) collective-permute-start(bf16[128,1024]{1,0:T(8,128)(2,1)S(1)} %pad_maximum_fusion.1.refs_8_), channel_id=1, source_target_pairs={{0,8},{4,12},{8,0},{12,4},{16,24},{20,28},{24,16},{28,20},{1,9},{5... | collective-permute-start | bytes 786440 | tf_op jit(solution)/shard_map/ppermute | solution.py:39
  56.3 4.7 %collective-permute-done.7.refs_10_ = bf16[128,1024]{1,0:T(8,128)(2,1)} collective-permute-done((bf16[128,1024]{1,0:T(8,128)(2,1)S(1)}, bf16[128,1024]{1,0:T(8,128)(2,1)}, u32[]{:S(2)}, u32[]{:S(2)}) %collective-permute-start.7) | collective-permute-done | bytes 262176 | tf_op jit(solution)/shard_map/ppermute | solution.py:39
  63.2 6.3 %collective-permute-done.17.refs_9_ = bf16[128,896]{1,0:T(8,128)(2,1)S(1)} collective-permute-done((bf16[128,896]{1,0:T(8,128)(2,1)S(1)}, bf16[128,896]{1,0:T(8,128)(2,1)S(1)}, u32[]{:S(2)}, u32[]{:S(2)}) %collective-permute-start.17) | collective-permute-done | bytes 229408 | tf_op jit(solution)/shard_map/ppermute | solution.py:39
  70.0 2.2 collective-permute-done.18.refs_10_
  72.7 6.1 %collective-permute-done.19.refs_11_ = bf16[128,896]{1,0:T(8,128)(2,1)S(1)} collective-permute-done((bf16[128,896]{1,0:T(8,128)(2,1)S(1)}, bf16[128,896]{1,0:T(8,128)(2,1)S(1)}, u32[]{:S(2)}, u32[]{:S(2)}) %collective-permute-start.19) | collective-permute-done | bytes 229408 | tf_op jit(solution)/shard_map/ppermute | solution.py:39
  79.4 1.5 collective-permute-start.12
  83.4 12.2 %shard_map.263 = (f32[1024,512]{1,0:T(8,128)}, f32[1024,256]{1,0:T(8,128)}, bf16[1024,512]{1,0:T(8,128)(2,1)}, bf16[1024,256]{1,0:T(8,128)(2,1)}, f32[1024,128]{...) custom-call(s32[1]{0:T(128)} %bitcast.2.place, ...), custom_call_target="tpu_custom_call" | custom-call | tf_op jit(solution)/shard_map/pallas_call | solution.py:669
  95.7 8.3 %shard_map.264 = (f32[1024,512]{1,0:T(8,128)}, f32[1024,256]{1,0:T(8,128)}, bf16[1024,512]{1,0:T(8,128)(2,1)}, bf16[1024,256]{1,0:T(8,128)(2,1)}, f32[1024,128]{...) custom-call(s32[1]{0:T(128)} %bitcast.2.place, ...), custom_call_target="tpu_custom_call", output_to_operand_aliasing={{0}: (13, {}), {1}: (14, {}), {2}: (15, {}), {3}: (16, {}),... | custom-call | tf_op jit(solution)/shard_map/pallas_call | solution.py:669
  104.8 9.0 %shard_map.265 = (f32[1024,512]{1,0:T(8,128)}, f32[1024,512]{1,0:T(8,128)}, f32[4,8,256]{2,1,0:T(8,128)}, bf16[1024,1024]{1,0:T(8,128)(2,1)}, bf16[1024,1024]{1,...) custom-call(s32[1]{0:T(128)} %bitcast.2.place, bf16[256,1024]{1,0:T(8,128)(2,1)} %get-tuple-element.71.refs_0_, ...), custom_call_target="tpu_custom_call" | custom-call | tf_op jit(solution)/shard_map/pallas_call | solution.py:709
  115.7 2.3 collective-permute-done.21.refs_2_
  119.0 6.3 %shard_map.266 = (bf16[1024,512]{1,0:T(8,128)(2,1)}, f32[1024,512]{1,0:T(8,128)}, bf16[1024,512]{1,0:T(8,128)(2,1)}, f32[8,512]{1,0:T(8,128)}) custom-call(s32[1]{0:T(128)} %bitcast.2.place, f32[4,8,256]{2,1,0:T(8,128)} %get-tuple-element.94.refs_0_, f32[4,8,256]{2,1,0:T(8,128)} %copy-done.30, f32[4,8,256]{2,1,0:T(8,128)} %copy-done.31, ...), custom_call_target="tpu_custom_call" | custom-call | tf_op jit(solution)/shard_map/pallas_call | solution.py:731
  125.4 2.0 convolution_convert_fusion.10
  127.4 2.2 convolution_convert_fusion.9
  129.6 1.5 convolution_convert_fusion.4
  131.2 1.5 convolution_convert_fusion.3
  133.3 11.9 %shard_map.268 = (bf16[1024,896]{1,0:T(8,128)(2,1)}, f32[8,512]{1,0:T(8,128)}, f32[8,256]{1,0:T(8,128)}, f32[8,128]{1,0:T(8,128)}, f32[128,512]{1,0:T(8,128)}, /...) custom-call(s32[1]{0:T(128)} %bitcast.2.place, f32[1024,512]{1,0:T(8,128)} %get-tuple-element.101.refs_0_, ...), custom_call_target="tpu_custom_call" | custom-call | tf_op jit(solution)/shard_map/pallas_call | solution.py:777
  145.2 12.1 %shard_map.269 = (bf16[1024,896]{1,0:T(8,128)(2,1)}, f32[8,512]{1,0:T(8,128)}, f32[8,256]{1,0:T(8,128)}, f32[8,128]{1,0:T(8,128)}, f32[128,512]{1,0:T(8,128)}, /...) custom-call(s32[1]{0:T(128)} %bitcast.2.place, ...), custom_call_target="tpu_custom_call", output_to_operand_aliasing={{0}: (20, {})} | custom-call | tf_op jit(solution)/shard_map/pallas_call | solution.py:777
  157.3 3.1 %convolution_convert_fusion.6 = bf16[256,896]{1,0:T(8,128)(2,1)} fusion(bf16[1024,896]{1,0:T(8,128)(2,1)} %get-tuple-element.116.columns, bf16[1024,1024]{1,0:T(8,128)(2,1)S(1)} %copy-done.4), kind=kOutput, calls=%fused_computation.6 | convolution fusion | flops 469991424 | bytes 2818048 | tf_op jit(solution)/shard_map/dot_general | solution.py:743
  160.5 1.3 convolution_convert_fusion.2
  161.8 1.5 convolution_convert_fusion.5
  163.3 1.7 convolution_convert_fusion
  165.8 7.9 %shard_map.270 = (bf16[512,1024]{1,0:T(8,128)(2,1)}, bf16[512,1024]{1,0:T(8,128)(2,1)}, f32[8,1024]{1,0:T(8,128)}) custom-call(s32[1]{0:T(128)} %bitcast.2.place, bf16[1024,1024]{1,0:T(8,128)(2,1)} %get-tuple-element.99.tokens, bf16[1024,512]{1,0:T(8,128)(2,1)} %get-tuple-element.100.d_gate, bf16[1024,896]{1,0:T(8,128)(2,1)} %get-tuple-element.116.columns, ...), custom_call_target="tpu_custom_call" | custom-call | tf_op jit(solution)/shard_map/pallas_call | solution.py:804
  173.7 1.5 shard_map.272
  175.2 1.5 collective-permute-start.32
  176.7 1.8 convolution_convert_fusion.8
  178.6 1.3 collective-permute-done.32
  179.9 1.5 collective-permute-start.33
  181.4 1.8 collective-permute-start.34
  184.3 1.8 convolution_convert_fusion.7
  186.8 2.7 collective-permute-start.44
  190.6 1.5 collective-permute-start.39
  193.9 5.2 %collective-permute-done.43 = bf16[256,512]{1,0:T(8,128)(2,1)S(1)} collective-permute-done((bf16[256,512]{1,0:T(8,128)(2,1)S(1)}, bf16[256,512]{1,0:T(8,128)(2,1)S(1)}, u32[]{:S(2)}, u32[]{:S(2)}) %collective-permute-start.43) | collective-permute-done | bytes 262176 | tf_op jit(solution)/shard_map/ppermute | solution.py:39
  199.1 1.6 collective-permute-start.30
  200.7 7.4 %collective-permute-done.44 = bf16[256,512]{1,0:T(8,128)(2,1)S(1)} collective-permute-done((bf16[256,512]{1,0:T(8,128)(2,1)S(1)}, bf16[256,512]{1,0:T(8,128)(2,1)S(1)}, u32[]{:S(2)}, u32[]{:S(2)}) %collective-permute-start.44) | collective-permute-done | bytes 262176 | tf_op jit(solution)/shard_map/ppermute | solution.py:39
  208.2 1.6 collective-permute-start.46
  211.6 13.6 %collective-permute-done.46 = bf16[128,512]{1,0:T(8,128)(2,1)} collective-permute-done((bf16[128,512]{1,0:T(8,128)(2,1)S(1)}, bf16[128,512]{1,0:T(8,128)(2,1)}, u32[]{:S(2)}, u32[]{:S(2)}) %collective-permute-start.46) | collective-permute-done | bytes 131104 | tf_op jit(solution)/shard_map/ppermute | solution.py:39
  228.4 1.3 add_convert_fusion.8
  229.7 2.9 collective-permute-start.40
  232.5 1.6 collective-permute-start.42
  235.1 2.9 collective-permute-done.40
  238.0 2.8 collective-permute-start.28
  240.8 12.4 %collective-permute-done.41 = bf16[128,512]{1,0:T(8,128)(2,1)S(1)} collective-permute-done((bf16[128,512]{1,0:T(8,128)(2,1)S(1)}, bf16[128,512]{1,0:T(8,128)(2,1)S(1)}, u32[]{:S(2)}, u32[]{:S(2)}) %collective-permute-start.41) | collective-permute-done | bytes 131104 | tf_op jit(solution)/shard_map/ppermute | solution.py:39
  254.3 9.9 %collective-permute-done.31 = bf16[128,896]{1,0:T(8,128)(2,1)S(1)} collective-permute-done((bf16[128,896]{1,0:T(8,128)(2,1)S(1)}, bf16[128,896]{1,0:T(8,128)(2,1)S(1)}, u32[]{:S(2)}, u32[]{:S(2)}) %collective-permute-start.31) | collective-permute-done | bytes 229408 | tf_op jit(solution)/shard_map/ppermute | solution.py:39
  267.3 1.2 copy.42
  269.2 1.2 add_convert_fusion
  272.4 1.3 collective-permute-start.24
  273.7 1.4 collective-permute-done.38
  278.6 8.8 %collective-permute-done.26.refs_1_ = bf16[256,1024]{1,0:T(8,128)(2,1)} collective-permute-done((bf16[256,1024]{1,0:T(8,128)(2,1)S(1)}, bf16[256,1024]{1,0:T(8,128)(2,1)}, u32[]{:S(2)}, u32[]{:S(2)}) %collective-permute-start.26) | collective-permute-done | bytes 524320 | tf_op jit(solution)/shard_map/ppermute | solution.py:39
  287.4 3.6 %shard_map.271 = f32[256,1,1024]{2,1,0:T(1,128)} custom-call(s32[1]{0:T(128)} %bitcast.place, bf16[256,1024]{1,0:T(8,128)(2,1)} %bitcast.46, bf16[256,1024]{1,0:T(8,128)(2,1)} %bitcast.49, f32[1,1024]{1,0:T(1,128)} %bitcast.55, bf16[512,1024]{1,0:T(8,128)(2,1)} %get-tuple-element.118.refs_0_, bf16[256,1024]{1,0:T(8,128)(2,1)} %collective-permute-done.26.refs_1_, ...), custom_call_target="tpu_custom_call" | custom-call | tf_op jit(solution)/shard_map/pallas_call | solution.py:821
  291.0 7.0 %collective-permute-done.24.refs_1_ = bf16[256,1024]{1,0:T(8,128)(2,1)S(1)} collective-permute-done((bf16[256,1024]{1,0:T(8,128)(2,1)}, bf16[256,1024]{1,0:T(8,128)(2,1)S(1)}, u32[]{:S(2)}, u32[]{:S(2)}) %collective-permute-start.24) | collective-permute-done | bytes 524320 | tf_op jit(solution)/shard_map/ppermute | solution.py:39
  298.8 3.2 %shard_map.267 = f32[256,1,1024]{2,1,0:T(1,128)} custom-call(s32[1]{0:T(128)} %bitcast.place, bf16[256,1024]{1,0:T(8,128)(2,1)} %bitcast.47, bf16[512,1024]{1,0:T(8,128)(2,1)} %copy-done.5, bf16[256,1024]{1,0:T(8,128)(2,1)} %copy-done.14, bf16[512,1024]{1,0:T(8,128)(2,1)} %copy-done.6), custom_call_target="tpu_custom_call" | custom-call | tf_op jit(solution)/shard_map/pallas_call | solution.py:766
  (178 shorter events, 39.3 us)
Async XLA Ops:
  0.6 20.5 %copy-start.29 = (bf16[512,128]{1,0:T(8,128)(2,1)S(1)}, bf16[512,128]{1,0:T(8,128)(2,1)}, u32[]{:S(2)}) copy-start(bf16[512,128]{1,0:T(8,128)(2,1)} %param.28) | copy-start | bytes 393220
  9.9 73.5 %copy-start.11 = (bf16[128,896]{1,0:T(8,128)(2,1)}, bf16[128,896]{1,0:T(8,128)(2,1)S(1)}, u32[]{:S(2)}) copy-start(bf16[128,896]{1,0:T(8,128)(2,1)S(1)} %maximum_maximum_fusion.refs_4_) | copy-start | bytes 688132
  9.9 11.8 %collective-permute-start.16 = (bf16[128,896]{1,0:T(8,128)(2,1)S(1)}, bf16[128,896]{1,0:T(8,128)(2,1)S(1)}, u32[]{:S(2)}, u32[]{:S(2)}) collective-permute-start(bf16[128,896]{1,0:T(8,128)(2,1)S(1)} %maximum_maximum_fusion.refs_4_), channel_id=1, source_target_pairs={{0,4},{4,0},{8,12},{12,8},{16,20},{20,16},{24,28},{28,24},{1,5},{5... | collective-permute-start | bytes 688136 | tf_op jit(solution)/shard_map/ppermute | solution.py:39
  12.9 11.9 %collective-permute-start.13 = (bf16[128,896]{1,0:T(8,128)(2,1)S(1)}, bf16[128,896]{1,0:T(8,128)(2,1)S(1)}, u32[]{:S(2)}, u32[]{:S(2)}) collective-permute-start(bf16[128,896]{1,0:T(8,128)(2,1)S(1)} %maximum_maximum_fusion.refs_4_), channel_id=1, source_target_pairs={{0,8},{4,12},{8,0},{12,4},{16,24},{20,28},{24,16},{28,20},{1,9},{5... | collective-permute-start | bytes 688136 | tf_op jit(solution)/shard_map/ppermute | solution.py:39
  14.5 28.9 %collective-permute-start.14 = (bf16[128,896]{1,0:T(8,128)(2,1)S(1)}, bf16[128,896]{1,0:T(8,128)(2,1)S(1)}, u32[]{:S(2)}, u32[]{:S(2)}) collective-permute-start(bf16[128,896]{1,0:T(8,128)(2,1)S(1)} %maximum_maximum_fusion.refs_4_), channel_id=1, source_target_pairs={{0,16},{4,20},{8,24},{12,28},{16,0},{20,4},{24,8},{28,12},{1,17},{... | collective-permute-start | bytes 688136 | tf_op jit(solution)/shard_map/ppermute | solution.py:39
  19.6 36.1 %collective-permute-start = (bf16[256,1024]{1,0:T(8,128)(2,1)}, bf16[256,1024]{1,0:T(8,128)(2,1)S(1)}, u32[]{:S(2)}, u32[]{:S(2)}) collective-permute-start(bf16[256,1024]{1,0:T(8,128)(2,1)} %get-tuple-element.71.refs_0_), channel_id=1, source_target_pairs={{0,2},{1,3},{2,0},{3,1},{4,6},{5,7},{6,4},{7,5},{8,10},{9,11},{10,... | collective-permute-start | bytes 1572872 | tf_op jit(solution)/shard_map/ppermute | solution.py:39
  21.3 74.3 %copy-start.10 = (bf16[128,1024]{1,0:T(8,128)(2,1)}, bf16[128,1024]{1,0:T(8,128)(2,1)S(1)}, u32[]{:S(2)}) copy-start(bf16[128,1024]{1,0:T(8,128)(2,1)S(1)} %pad_maximum_fusion.1.refs_8_) | copy-start | bytes 786436
  21.3 33.8 %collective-permute-start.9 = (bf16[128,1024]{1,0:T(8,128)(2,1)S(1)}, bf16[128,1024]{1,0:T(8,128)(2,1)S(1)}, u32[]{:S(2)}, u32[]{:S(2)}) collective-permute-start(bf16[128,1024]{1,0:T(8,128)(2,1)S(1)} %pad_maximum_fusion.1.refs_8_), channel_id=1, source_target_pairs={{0,16},{4,20},{8,24},{12,28},{16,0},{20,4},{24,8},{28,12},{1,17},{... | collective-permute-start | bytes 786440 | tf_op jit(solution)/shard_map/ppermute | solution.py:39
  21.7 34.0 %copy-start.21 = (bf16[128,896]{1,0:T(8,128)(2,1)}, bf16[128,896]{1,0:T(8,128)(2,1)S(1)}, u32[]{:S(2)}) copy-start(bf16[128,896]{1,0:T(8,128)(2,1)S(1)} %collective-permute-done.16.refs_8_) | copy-start | bytes 688132
  21.7 23.7 %collective-permute-start.15 = (bf16[128,896]{1,0:T(8,128)(2,1)S(1)}, bf16[128,896]{1,0:T(8,128)(2,1)S(1)}, u32[]{:S(2)}, u32[]{:S(2)}) collective-permute-start(bf16[128,896]{1,0:T(8,128)(2,1)S(1)} %maximum_maximum_fusion.refs_4_), channel_id=1, source_target_pairs={{0,24},{4,28},{8,16},{12,20},{16,8},{20,12},{24,0},{28,4},{1,25},{... | collective-permute-start | bytes 688136 | tf_op jit(solution)/shard_map/ppermute | solution.py:39
  24.8 38.2 %copy-start.22 = (bf16[128,896]{1,0:T(8,128)(2,1)}, bf16[128,896]{1,0:T(8,128)(2,1)S(1)}, u32[]{:S(2)}) copy-start(bf16[128,896]{1,0:T(8,128)(2,1)S(1)} %collective-permute-done.13.refs_5_) | copy-start | bytes 688132
  24.8 30.9 %collective-permute-start.11 = (bf16[128,1024]{1,0:T(8,128)(2,1)S(1)}, bf16[128,1024]{1,0:T(8,128)(2,1)}, u32[]{:S(2)}, u32[]{:S(2)}) collective-permute-start(bf16[128,1024]{1,0:T(8,128)(2,1)S(1)} %pad_maximum_fusion.1.refs_8_), channel_id=1, source_target_pairs={{0,24},{4,28},{8,16},{12,20},{16,8},{20,12},{24,0},{28,4},{1,25},{... | collective-permute-start | bytes 786440 | tf_op jit(solution)/shard_map/ppermute | solution.py:39
  43.4 12.3 %copy-start.23 = (bf16[128,896]{1,0:T(8,128)(2,1)}, bf16[128,896]{1,0:T(8,128)(2,1)S(1)}, u32[]{:S(2)}) copy-start(bf16[128,896]{1,0:T(8,128)(2,1)S(1)} %collective-permute-done.14.refs_6_) | copy-start | bytes 688132
  43.4 26.0 %collective-permute-start.3 = (bf16[256,1024]{1,0:T(8,128)(2,1)}, bf16[256,1024]{1,0:T(8,128)(2,1)S(1)}, u32[]{:S(2)}, u32[]{:S(2)}) collective-permute-start(bf16[256,1024]{1,0:T(8,128)(2,1)} %get-tuple-element.72.refs_4_), channel_id=1, source_target_pairs={{0,2},{1,3},{2,0},{3,1},{4,6},{5,7},{6,4},{7,5},{8,10},{9,11},{10,... | collective-permute-start | bytes 1572872 | tf_op jit(solution)/shard_map/ppermute | solution.py:39
  45.5 35.4 %copy-start.24 = (bf16[128,896]{1,0:T(8,128)(2,1)}, bf16[128,896]{1,0:T(8,128)(2,1)S(1)}, u32[]{:S(2)}) copy-start(bf16[128,896]{1,0:T(8,128)(2,1)S(1)} %collective-permute-done.15.refs_7_) | copy-start | bytes 688132
  45.5 15.5 %collective-permute-start.7 = (bf16[128,1024]{1,0:T(8,128)(2,1)S(1)}, bf16[128,1024]{1,0:T(8,128)(2,1)}, u32[]{:S(2)}, u32[]{:S(2)}) collective-permute-start(bf16[128,1024]{1,0:T(8,128)(2,1)S(1)} %pad_maximum_fusion.1.refs_8_), channel_id=1, source_target_pairs={{0,8},{4,12},{8,0},{12,4},{16,24},{20,28},{24,16},{28,20},{1,9},{5... | collective-permute-start | bytes 786440 | tf_op jit(solution)/shard_map/ppermute | solution.py:39
  55.2 48.8 %copy-start.15 = (bf16[128,1024]{1,0:T(8,128)(2,1)}, bf16[128,1024]{1,0:T(8,128)(2,1)S(1)}, u32[]{:S(2)}) copy-start(bf16[128,1024]{1,0:T(8,128)(2,1)S(1)} %collective-permute-done.9.refs_12_) | copy-start | bytes 786436
  55.2 7.3 %collective-permute-start.6 = (bf16[128,1024]{1,0:T(8,128)(2,1)S(1)}, bf16[128,1024]{1,0:T(8,128)(2,1)S(1)}, u32[]{:S(2)}, u32[]{:S(2)}) collective-permute-start(bf16[128,1024]{1,0:T(8,128)(2,1)S(1)} %pad_maximum_fusion.1.refs_8_), channel_id=1, source_target_pairs={{0,4},{4,0},{8,12},{12,8},{16,20},{20,16},{24,28},{28,24},{1,5},{5... | collective-permute-start | bytes 786440 | tf_op jit(solution)/shard_map/ppermute | solution.py:39
  55.7 23.7 %collective-permute-start.1 = (bf16[256,1024]{1,0:T(8,128)(2,1)}, bf16[256,1024]{1,0:T(8,128)(2,1)S(1)}, u32[]{:S(2)}, u32[]{:S(2)}) collective-permute-start(bf16[256,1024]{1,0:T(8,128)(2,1)} %get-tuple-element.71.refs_0_), channel_id=1, source_target_pairs={{0,1},{1,0},{2,3},{3,2},{4,5},{5,4},{6,7},{7,6},{8,9},{9,8},{10,11... | collective-permute-start | bytes 1572872 | tf_op jit(solution)/shard_map/ppermute | solution.py:39
  55.7 27.7 %copy-start.1 = (bf16[256,1024]{1,0:T(8,128)(2,1)}, bf16[256,1024]{1,0:T(8,128)(2,1)S(1)}, u32[]{:S(2)}) copy-start(bf16[256,1024]{1,0:T(8,128)(2,1)S(1)} %collective-permute-done.refs_2_.refs_1_) | copy-start | bytes 1572868
  55.7 25.1 %collective-permute-start.2 = (bf16[256,1024]{1,0:T(8,128)(2,1)S(1)}, bf16[256,1024]{1,0:T(8,128)(2,1)S(1)}, u32[]{:S(2)}, u32[]{:S(2)}) collective-permute-start(bf16[256,1024]{1,0:T(8,128)(2,1)S(1)} %collective-permute-done.refs_2_.refs_1_), channel_id=1, source_target_pairs={{0,1},{1,0},{2,3},{3,2},{4,5},{5,4},{6,7},{7,6},{8,9},{9,8},{10,11... | collective-permute-start | bytes 1572872 | tf_op jit(solution)/shard_map/ppermute | solution.py:39
  61.0 8.5 %collective-permute-start.17 = (bf16[128,896]{1,0:T(8,128)(2,1)S(1)}, bf16[128,896]{1,0:T(8,128)(2,1)S(1)}, u32[]{:S(2)}, u32[]{:S(2)}) collective-permute-start(bf16[128,896]{1,0:T(8,128)(2,1)S(1)} %collective-permute-done.13.refs_5_), channel_id=1, source_target_pairs={{0,4},{4,0},{8,12},{12,8},{16,20},{20,16},{24,28},{28,24},{1,5},{5... | collective-permute-start | bytes 688136 | tf_op jit(solution)/shard_map/ppermute | solution.py:39
  62.4 9.7 %collective-permute-start.18 = (bf16[128,896]{1,0:T(8,128)(2,1)}, bf16[128,896]{1,0:T(8,128)(2,1)S(1)}, u32[]{:S(2)}, u32[]{:S(2)}) collective-permute-start(bf16[128,896]{1,0:T(8,128)(2,1)} %copy-done.23), channel_id=1, source_target_pairs={{0,4},{4,0},{8,12},{12,8},{16,20},{20,16},{24,28},{28,24},{1,5},{5... | collective-permute-start | bytes 688136 | tf_op jit(solution)/shard_map/ppermute | solution.py:39
  69.5 11.4 %copy-start.25 = (bf16[128,896]{1,0:T(8,128)(2,1)}, bf16[128,896]{1,0:T(8,128)(2,1)S(1)}, u32[]{:S(2)}) copy-start(bf16[128,896]{1,0:T(8,128)(2,1)S(1)} %collective-permute-done.17.refs_9_) | copy-start | bytes 688132
  69.5 34.5 %collective-permute-start.4 = (bf16[256,1024]{1,0:T(8,128)(2,1)}, bf16[256,1024]{1,0:T(8,128)(2,1)S(1)}, u32[]{:S(2)}, u32[]{:S(2)}) collective-permute-start(bf16[256,1024]{1,0:T(8,128)(2,1)} %get-tuple-element.72.refs_4_), channel_id=1, source_target_pairs={{0,1},{1,0},{2,3},{3,2},{4,5},{5,4},{6,7},{7,6},{8,9},{9,8},{10,11... | collective-permute-start | bytes 1572872 | tf_op jit(solution)/shard_map/ppermute | solution.py:39
  69.5 34.5 %copy-start.12 = (bf16[256,1024]{1,0:T(8,128)(2,1)}, bf16[256,1024]{1,0:T(8,128)(2,1)S(1)}, u32[]{:S(2)}) copy-start(bf16[256,1024]{1,0:T(8,128)(2,1)S(1)} %collective-permute-done.3.refs_5_) | copy-start | bytes 1572868
  69.5 34.5 %collective-permute-start.5 = (bf16[256,1024]{1,0:T(8,128)(2,1)S(1)}, bf16[256,1024]{1,0:T(8,128)(2,1)}, u32[]{:S(2)}, u32[]{:S(2)}) collective-permute-start(bf16[256,1024]{1,0:T(8,128)(2,1)S(1)} %collective-permute-done.3.refs_5_), channel_id=1, source_target_pairs={{0,1},{1,0},{2,3},{3,2},{4,5},{5,4},{6,7},{7,6},{8,9},{9,8},{10,11... | collective-permute-start | bytes 1572872 | tf_op jit(solution)/shard_map/ppermute | solution.py:39
  72.2 8.7 %copy-start.26 = (bf16[128,896]{1,0:T(8,128)(2,1)}, bf16[128,896]{1,0:T(8,128)(2,1)S(1)}, u32[]{:S(2)}) copy-start(bf16[128,896]{1,0:T(8,128)(2,1)S(1)} %collective-permute-done.18.refs_10_) | copy-start | bytes 688132
  72.2 6.7 %collective-permute-start.19 = (bf16[128,896]{1,0:T(8,128)(2,1)S(1)}, bf16[128,896]{1,0:T(8,128)(2,1)S(1)}, u32[]{:S(2)}, u32[]{:S(2)}) collective-permute-start(bf16[128,896]{1,0:T(8,128)(2,1)S(1)} %collective-permute-done.15.refs_7_), channel_id=1, source_target_pairs={{0,4},{4,0},{8,12},{12,8},{16,20},{20,16},{24,28},{28,24},{1,5},{5... | collective-permute-start | bytes 688136 | tf_op jit(solution)/shard_map/ppermute | solution.py:39
  78.8 25.1 %collective-permute-start.10 = (bf16[128,1024]{1,0:T(8,128)(2,1)S(1)}, bf16[128,1024]{1,0:T(8,128)(2,1)}, u32[]{:S(2)}, u32[]{:S(2)}) collective-permute-start(bf16[128,1024]{1,0:T(8,128)(2,1)S(1)} %collective-permute-done.9.refs_12_), channel_id=1, source_target_pairs={{0,4},{4,0},{8,12},{12,8},{16,20},{20,16},{24,28},{28,24},{1,5},{5... | collective-permute-start | bytes 786440 | tf_op jit(solution)/shard_map/ppermute | solution.py:39
  79.4 24.6 %collective-permute-start.12 = (bf16[128,1024]{1,0:T(8,128)(2,1)}, bf16[128,1024]{1,0:T(8,128)(2,1)}, u32[]{:S(2)}, u32[]{:S(2)}) collective-permute-start(bf16[128,1024]{1,0:T(8,128)(2,1)} %collective-permute-done.11.refs_14_), channel_id=1, source_target_pairs={{0,4},{4,0},{8,12},{12,8},{16,20},{20,16},{24,28},{28,24},{1,5},{5... | collective-permute-start | bytes 786440 | tf_op jit(solution)/shard_map/ppermute | solution.py:39
  80.9 23.1 %collective-permute-start.8 = (bf16[128,1024]{1,0:T(8,128)(2,1)}, bf16[128,1024]{1,0:T(8,128)(2,1)}, u32[]{:S(2)}, u32[]{:S(2)}) collective-permute-start(bf16[128,1024]{1,0:T(8,128)(2,1)} %collective-permute-done.7.refs_10_), channel_id=1, source_target_pairs={{0,4},{4,0},{8,12},{12,8},{16,20},{20,16},{24,28},{28,24},{1,5},{5... | collective-permute-start | bytes 786440 | tf_op jit(solution)/shard_map/ppermute | solution.py:39
  113.7 1.9 collective-permute-start.20
  113.8 4.2 %collective-permute-start.21 = (f32[4,8,256]{2,1,0:T(8,128)}, f32[4,8,256]{2,1,0:T(8,128)S(1)}, u32[]{:S(2)}, u32[]{:S(2)}) collective-permute-start(f32[4,8,256]{2,1,0:T(8,128)} %get-tuple-element.94.refs_0_), channel_id=1, source_target_pairs={{0,2},{1,3},{2,0},{3,1},{4,6},{5,7},{6,4},{7,5},{8,10},{9,11},{10,... | collective-permute-start | bytes 98312 | tf_op jit(solution)/shard_map/ppermute | solution.py:39
  114.9 3.6 %collective-permute-start.22 = (f32[4,8,256]{2,1,0:T(8,128)}, f32[4,8,256]{2,1,0:T(8,128)S(1)}, u32[]{:S(2)}, u32[]{:S(2)}) collective-permute-start(f32[4,8,256]{2,1,0:T(8,128)} %get-tuple-element.94.refs_0_), channel_id=1, source_target_pairs={{0,3},{1,2},{2,1},{3,0},{4,7},{5,6},{6,5},{7,4},{8,11},{9,10},{10,... | collective-permute-start | bytes 98312 | tf_op jit(solution)/shard_map/ppermute | solution.py:39
  165.8 105.4 %copy-start.5 = (bf16[512,1024]{1,0:T(8,128)(2,1)}, bf16[512,1024]{1,0:T(8,128)(2,1)S(1)}, u32[]{:S(2)}) copy-start(bf16[512,1024]{1,0:T(8,128)(2,1)S(1)} %convolution_convert_fusion.1.refs_0_) | copy-start | bytes 3145732
  175.2 11.0 %copy-start.36 = (bf16[256,512]{1,0:T(8,128)(2,1)S(1)}, bf16[256,512]{1,0:T(8,128)(2,1)}, u32[]{:S(2)}) copy-start(bf16[256,512]{1,0:T(8,128)(2,1)} %convolution_convert_fusion.9) | copy-start | bytes 786436
  175.2 4.6 %collective-permute-start.32 = (f32[32,512]{1,0:T(8,128)}, f32[32,512]{1,0:T(8,128)S(1)}, u32[]{:S(2)}, u32[]{:S(2)}) collective-permute-start(f32[32,512]{1,0:T(8,128)} %shard_map.272), channel_id=1, source_target_pairs={{0,4},{4,0},{8,12},{12,8},{16,20},{20,16},{24,28},{28,24},{1,5},{5... | collective-permute-start | bytes 196616 | tf_op jit(solution)/shard_map/ppermute | solution.py:39
  179.9 9.6 %collective-permute-start.33 = (f32[32,512]{1,0:T(8,128)S(1)}, f32[32,512]{1,0:T(8,128)S(1)}, u32[]{:S(2)}, u32[]{:S(2)}) collective-permute-start(f32[32,512]{1,0:T(8,128)S(1)} %add.105), channel_id=1, source_target_pairs={{0,8},{4,12},{8,0},{12,4},{16,24},{20,28},{24,16},{28,20},{1,9},{5... | collective-permute-start | bytes 196616 | tf_op jit(solution)/shard_map/ppermute | solution.py:39
  181.4 9.3 %collective-permute-start.34 = (f32[32,512]{1,0:T(8,128)S(1)}, f32[32,512]{1,0:T(8,128)S(1)}, u32[]{:S(2)}, u32[]{:S(2)}) collective-permute-start(f32[32,512]{1,0:T(8,128)S(1)} %add.105), channel_id=1, source_target_pairs={{0,16},{4,20},{8,24},{12,28},{16,0},{20,4},{24,8},{28,12},{1,17},{... | collective-permute-start | bytes 196616 | tf_op jit(solution)/shard_map/ppermute | solution.py:39
  183.2 9.0 %collective-permute-start.35 = (f32[32,512]{1,0:T(8,128)S(1)}, f32[32,512]{1,0:T(8,128)S(1)}, u32[]{:S(2)}, u32[]{:S(2)}) collective-permute-start(f32[32,512]{1,0:T(8,128)S(1)} %add.105), channel_id=1, source_target_pairs={{0,24},{4,28},{8,16},{12,20},{16,8},{20,12},{24,0},{28,4},{1,25},{... | collective-permute-start | bytes 196616 | tf_op jit(solution)/shard_map/ppermute | solution.py:39
  186.2 12.9 %collective-permute-start.43 = (bf16[256,512]{1,0:T(8,128)(2,1)S(1)}, bf16[256,512]{1,0:T(8,128)(2,1)S(1)}, u32[]{:S(2)}, u32[]{:S(2)}) collective-permute-start(bf16[256,512]{1,0:T(8,128)(2,1)S(1)} %copy-done.36), channel_id=1, source_target_pairs={{0,8},{4,12},{8,0},{12,4},{16,24},{20,28},{24,16},{28,20},{1,9},{5... | collective-permute-start | bytes 786440 | tf_op jit(solution)/shard_map/ppermute | solution.py:39
  186.8 21.3 %collective-permute-start.44 = (bf16[256,512]{1,0:T(8,128)(2,1)S(1)}, bf16[256,512]{1,0:T(8,128)(2,1)S(1)}, u32[]{:S(2)}, u32[]{:S(2)}) collective-permute-start(bf16[256,512]{1,0:T(8,128)(2,1)S(1)} %convolution_convert_fusion.8), channel_id=1, source_target_pairs={{0,16},{4,20},{8,24},{12,28},{16,0},{20,4},{24,8},{28,12},{1,17},{... | collective-permute-start | bytes 786440 | tf_op jit(solution)/shard_map/ppermute | solution.py:39
  189.5 18.6 %collective-permute-start.45 = (bf16[256,512]{1,0:T(8,128)(2,1)S(1)}, bf16[256,512]{1,0:T(8,128)(2,1)S(1)}, u32[]{:S(2)}, u32[]{:S(2)}) collective-permute-start(bf16[256,512]{1,0:T(8,128)(2,1)S(1)} %convolution_convert_fusion.7), channel_id=1, source_target_pairs={{0,24},{4,28},{8,16},{12,20},{16,8},{20,12},{24,0},{28,4},{1,25},{... | collective-permute-start | bytes 786440 | tf_op jit(solution)/shard_map/ppermute | solution.py:39
  190.6 37.7 %collective-permute-start.39 = (bf16[512,512]{1,0:T(8,128)(2,1)}, bf16[512,512]{1,0:T(8,128)(2,1)}, u32[]{:S(2)}, u32[]{:S(2)}) collective-permute-start(bf16[512,512]{1,0:T(8,128)(2,1)} %convolution_convert_fusion.3), channel_id=1, source_target_pairs={{0,4},{4,0},{8,12},{12,8},{16,20},{20,16},{24,28},{28,24},{1,5},{5... | collective-permute-start | bytes 1572872 | tf_op jit(solution)/shard_map/ppermute | solution.py:39
  192.1 35.0 %collective-permute-start.27 = (bf16[256,896]{1,0:T(8,128)(2,1)}, bf16[256,896]{1,0:T(8,128)(2,1)}, u32[]{:S(2)}, u32[]{:S(2)}) collective-permute-start(bf16[256,896]{1,0:T(8,128)(2,1)} %convolution_convert_fusion.6), channel_id=1, source_target_pairs={{0,4},{4,0},{8,12},{12,8},{16,20},{20,16},{24,28},{28,24},{1,5},{5... | collective-permute-start | bytes 1376264 | tf_op jit(solution)/shard_map/ppermute | solution.py:39
  199.1 12.5 %copy-start.17 = (bf16[256,512]{1,0:T(8,128)(2,1)}, bf16[256,512]{1,0:T(8,128)(2,1)S(1)}, u32[]{:S(2)}) copy-start(bf16[256,512]{1,0:T(8,128)(2,1)S(1)} %collective-permute-done.43) | copy-start | bytes 786436
  199.1 29.3 %collective-permute-start.30 = (bf16[256,896]{1,0:T(8,128)(2,1)}, bf16[256,896]{1,0:T(8,128)(2,1)}, u32[]{:S(2)}, u32[]{:S(2)}) collective-permute-start(bf16[256,896]{1,0:T(8,128)(2,1)} %convolution_convert_fusion.5), channel_id=1, source_target_pairs={{0,4},{4,0},{8,12},{12,8},{16,20},{20,16},{24,28},{28,24},{1,5},{5... | collective-permute-start | bytes 1376264 | tf_op jit(solution)/shard_map/ppermute | solution.py:39
  208.1 61.1 %collective-permute-start.25 = (bf16[512,1024]{1,0:T(8,128)(2,1)}, bf16[512,1024]{1,0:T(8,128)(2,1)}, u32[]{:S(2)}, u32[]{:S(2)}) collective-permute-start(bf16[512,1024]{1,0:T(8,128)(2,1)} %get-tuple-element.119), channel_id=1, source_target_pairs={{0,1},{1,0},{2,3},{3,2},{4,5},{5,4},{6,7},{7,6},{8,9},{9,8},{10,11... | collective-permute-start | bytes 3145736 | tf_op jit(solution)/shard_map/ppermute | solution.py:39
  208.2 16.9 %collective-permute-start.46 = (bf16[128,512]{1,0:T(8,128)(2,1)S(1)}, bf16[128,512]{1,0:T(8,128)(2,1)}, u32[]{:S(2)}, u32[]{:S(2)}) collective-permute-start(bf16[128,512]{1,0:T(8,128)(2,1)S(1)} %add_convert_fusion.5), channel_id=1, source_target_pairs={{0,4},{4,0},{8,12},{12,8},{16,20},{20,16},{24,28},{28,24},{1,5},{5... | collective-permute-start | bytes 393224 | tf_op jit(solution)/shard_map/ppermute | solution.py:39
  225.2 46.0 %collective-permute-start.23 = (bf16[512,1024]{1,0:T(8,128)(2,1)}, bf16[512,1024]{1,0:T(8,128)(2,1)S(1)}, u32[]{:S(2)}, u32[]{:S(2)}) collective-permute-start(bf16[512,1024]{1,0:T(8,128)(2,1)} %convolution_convert_fusion), channel_id=1, source_target_pairs={{0,1},{1,0},{2,3},{3,2},{4,5},{5,4},{6,7},{7,6},{8,9},{9,8},{10,11... | collective-permute-start | bytes 3145736 | tf_op jit(solution)/shard_map/ppermute | solution.py:39
  228.3 36.9 %copy-start.28 = (f32[16,256]{1,0:T(8,128)S(1)}, f32[16,256]{1,0:T(8,128)}, u32[]{:S(2)}) copy-start(f32[16,256]{1,0:T(8,128)} %get-tuple-element.157) | copy-start | bytes 49156
  229.7 8.4 %collective-permute-start.40 = (bf16[128,512]{1,0:T(8,128)(2,1)S(1)}, bf16[128,512]{1,0:T(8,128)(2,1)S(1)}, u32[]{:S(2)}, u32[]{:S(2)}) collective-permute-start(bf16[128,512]{1,0:T(8,128)(2,1)S(1)} %get-tuple-element.144), channel_id=1, source_target_pairs={{0,24},{4,28},{8,16},{12,20},{16,8},{20,12},{24,0},{28,4},{1,25},{... | collective-permute-start | bytes 393224 | tf_op jit(solution)/shard_map/ppermute | solution.py:39
  232.5 20.7 %collective-permute-start.41 = (bf16[128,512]{1,0:T(8,128)(2,1)S(1)}, bf16[128,512]{1,0:T(8,128)(2,1)S(1)}, u32[]{:S(2)}, u32[]{:S(2)}) collective-permute-start(bf16[128,512]{1,0:T(8,128)(2,1)S(1)} %get-tuple-element.146), channel_id=1, source_target_pairs={{0,16},{4,20},{8,24},{12,28},{16,0},{20,4},{24,8},{28,12},{1,17},{... | collective-permute-start | bytes 393224 | tf_op jit(solution)/shard_map/ppermute | solution.py:39
  232.5 20.7 %collective-permute-start.42 = (bf16[128,512]{1,0:T(8,128)(2,1)S(1)}, bf16[128,512]{1,0:T(8,128)(2,1)S(1)}, u32[]{:S(2)}, u32[]{:S(2)}) collective-permute-start(bf16[128,512]{1,0:T(8,128)(2,1)S(1)} %get-tuple-element.145), channel_id=1, source_target_pairs={{0,8},{4,12},{8,0},{12,4},{16,24},{20,28},{24,16},{28,20},{1,9},{5... | collective-permute-start | bytes 393224 | tf_op jit(solution)/shard_map/ppermute | solution.py:39
  238.0 26.1 %collective-permute-start.28 = (bf16[128,896]{1,0:T(8,128)(2,1)S(1)}, bf16[128,896]{1,0:T(8,128)(2,1)S(1)}, u32[]{:S(2)}, u32[]{:S(2)}) collective-permute-start(bf16[128,896]{1,0:T(8,128)(2,1)S(1)} %get-tuple-element.143), channel_id=1, source_target_pairs={{0,24},{4,28},{8,16},{12,20},{16,8},{20,12},{24,0},{28,4},{1,25},{... | collective-permute-start | bytes 688136 | tf_op jit(solution)/shard_map/ppermute | solution.py:39
  253.2 11.0 %collective-permute-start.29 = (bf16[128,896]{1,0:T(8,128)(2,1)S(1)}, bf16[128,896]{1,0:T(8,128)(2,1)S(1)}, u32[]{:S(2)}, u32[]{:S(2)}) collective-permute-start(bf16[128,896]{1,0:T(8,128)(2,1)S(1)} %get-tuple-element.142), channel_id=1, source_target_pairs={{0,16},{4,20},{8,24},{12,28},{16,0},{20,4},{24,8},{28,12},{1,17},{... | collective-permute-start | bytes 688136 | tf_op jit(solution)/shard_map/ppermute | solution.py:39
  253.2 10.9 %collective-permute-start.31 = (bf16[128,896]{1,0:T(8,128)(2,1)S(1)}, bf16[128,896]{1,0:T(8,128)(2,1)S(1)}, u32[]{:S(2)}, u32[]{:S(2)}) collective-permute-start(bf16[128,896]{1,0:T(8,128)(2,1)S(1)} %add_convert_fusion.2), channel_id=1, source_target_pairs={{0,8},{4,12},{8,0},{12,4},{16,24},{20,28},{24,16},{28,20},{1,9},{5... | collective-permute-start | bytes 688136 | tf_op jit(solution)/shard_map/ppermute | solution.py:39
  265.3 8.4 %collective-permute-start.36 = (f32[160,256]{1,0:T(8,128)S(1)}, f32[160,256]{1,0:T(8,128)}, u32[]{:S(2)}, u32[]{:S(2)}) collective-permute-start(f32[160,256]{1,0:T(8,128)S(1)} %pad_maximum_fusion.2), channel_id=1, source_target_pairs={{0,1},{1,0},{2,3},{3,2},{4,5},{5,4},{6,7},{7,6},{8,9},{9,8},{10,11... | collective-permute-start | bytes 491528 | tf_op jit(solution)/shard_map/ppermute | solution.py:39
  265.4 8.3 %collective-permute-start.37 = (f32[160,256]{1,0:T(8,128)S(1)}, f32[160,256]{1,0:T(8,128)}, u32[]{:S(2)}, u32[]{:S(2)}) collective-permute-start(f32[160,256]{1,0:T(8,128)S(1)} %pad_maximum_fusion.2), channel_id=1, source_target_pairs={{0,2},{1,3},{2,0},{3,1},{4,6},{5,7},{6,4},{7,5},{8,10},{9,11},{10,... | collective-permute-start | bytes 491528 | tf_op jit(solution)/shard_map/ppermute | solution.py:39
  266.2 8.9 %collective-permute-start.38 = (f32[160,256]{1,0:T(8,128)S(1)}, f32[160,256]{1,0:T(8,128)}, u32[]{:S(2)}, u32[]{:S(2)}) collective-permute-start(f32[160,256]{1,0:T(8,128)S(1)} %pad_maximum_fusion.2), channel_id=1, source_target_pairs={{0,3},{1,2},{2,1},{3,0},{4,7},{5,6},{6,5},{7,4},{8,11},{9,10},{10,... | collective-permute-start | bytes 491528 | tf_op jit(solution)/shard_map/ppermute | solution.py:39
  270.4 17.0 %collective-permute-start.26 = (bf16[256,1024]{1,0:T(8,128)(2,1)S(1)}, bf16[256,1024]{1,0:T(8,128)(2,1)}, u32[]{:S(2)}, u32[]{:S(2)}) collective-permute-start(bf16[256,1024]{1,0:T(8,128)(2,1)S(1)} %add_convert_fusion), channel_id=1, source_target_pairs={{0,2},{1,3},{2,0},{3,1},{4,6},{5,7},{6,4},{7,5},{8,10},{9,11},{10,... | collective-permute-start | bytes 1572872 | tf_op jit(solution)/shard_map/ppermute | solution.py:39
  271.2 19.8 %copy-start.6 = (bf16[512,1024]{1,0:T(8,128)(2,1)}, bf16[512,1024]{1,0:T(8,128)(2,1)S(1)}, u32[]{:S(2)}) copy-start(bf16[512,1024]{1,0:T(8,128)(2,1)S(1)} %collective-permute-done.23.refs_2_) | copy-start | bytes 3145732
  272.4 25.6 %collective-permute-start.24 = (bf16[256,1024]{1,0:T(8,128)(2,1)}, bf16[256,1024]{1,0:T(8,128)(2,1)S(1)}, u32[]{:S(2)}, u32[]{:S(2)}) collective-permute-start(bf16[256,1024]{1,0:T(8,128)(2,1)} %add_convert_fusion.1), channel_id=1, source_target_pairs={{0,2},{1,3},{2,0},{3,1},{4,6},{5,7},{6,4},{7,5},{8,10},{9,11},{10,... | collective-permute-start | bytes 1572872 | tf_op jit(solution)/shard_map/ppermute | solution.py:39
  (21 other events, 50.5 us)

commit v3 on v2

--- a/solution.py
+++ b/solution.py
@@ -5,6 +5,8 @@
 from jax.experimental.pallas import tpu as pltpu
 from jax.sharding import PartitionSpec as P
 
+
+DP, TP = "dp", "tensor"
 
 CHUNK = 128
 ROWS = 256
@@ -172,8 +174,9 @@
     def kernel(place, *refs):
         token_refs, refs = refs[:count], refs[count:]
         weight_refs, refs = refs[:pieces], refs[pieces:]
-        taps_x, taps_bc, per_head, skip, *carried = refs[:7]
-        refs = refs[7 + (0 if start == 0 else 7) :]
+        taps_x, taps_bc, per_head, skip, *refs = refs
+        if start:
+            carried, refs = refs[:3], refs[10:]
         pre_x, pre_bc, raw_x, raw_bc, dt_out, mixed, before, state, halo_x, halo_bc = refs[:10]
         if start == 0:
             weights, refs = refs[10], refs[11:]
@@ -188,10 +191,14 @@
 
         @pl.when(pl.program_id(0) == 0)
         def _():
-            state[...] = carried[0][...]
-            ext_x[0:8, :] = carried[1][...]
-            ext_bc[0:8, :] = carried[2][...]
-            if start == 0:
+            if start:
+                state[...] = carried[0][...]
+                ext_x[0:8, :] = carried[1][...]
+                ext_bc[0:8, :] = carried[2][...]
+            else:
+                state[...] = jnp.zeros(state.shape, f32)
+                ext_x[0:8, :] = jnp.zeros((8, inner), f32)
+                ext_bc[0:8, :] = jnp.zeros((8, twice), f32)
                 join(weights, weight_refs)
 
         raw = mm(normed[...], weights[...])
@@ -258,7 +265,8 @@
     def kernel(place, *refs):
         d_mixed, pre_x, pre_bc, raw_x, raw_bc, dt_in, mixed, before, *refs = refs
         taps_x, taps_bc, per_head, skip, *refs = refs
-        carried, refs = refs[:7], refs[7 + resumed :]
+        if resumed:
+            carried, refs = refs[:7], refs[8:]
         columns, *results, ext_x, ext_bc = refs
         grad_x, grad_bc, grad_head, d_state, after, halo_x, halo_bc = results
         size = d_mixed.shape[0]
@@ -268,8 +276,8 @@
 
         @pl.when(pl.program_id(0) == 0)
         def _():
-            for result, value in zip(results, carried):
-                result[...] = value[...]
+            for k, result in enumerate(results):
+                result[...] = carried[k][...] if resumed else jnp.zeros(result.shape, f32)
             ext_x[size : size + 8, :] = halo_x[...]
             ext_bc[size : size + 8, :] = halo_bc[...]
 
@@ -535,6 +543,19 @@
     grad_gain[...] = jnp.broadcast_to(jnp.sum(total, axis=0, keepdims=True), grad_gain.shape)
 
 
+def product_kernel(bounds):
+    def kernel(place, left, right, *outs):
+        at = pl.program_id(0)
+        value = mm(left[...], right[...], TN).astype(bf16)
+        for i, out in enumerate(outs):
+
+            @pl.when((at >= bounds[i]) & (at < bounds[i + 1]))
+            def _(out=out):
+                out[...] = value
+
+    return kernel
+
+
 def whole(shape):
     return pl.BlockSpec(shape, lambda c, place: (0,) * len(shape))
 
@@ -578,8 +599,8 @@
 ):
     rows_local, seqs, model = block_input.shape
     assert seqs == 1
-    dp = lax.axis_size("dp")
-    tensor = lax.axis_size("tensor")
+    dp = lax.axis_size(DP)
+    tensor = lax.axis_size(TP)
     length = rows_local * tensor
     inner = w_zx.shape[2]
     twice = w_bc.shape[1]
@@ -592,8 +613,8 @@
     chunk = min(CHUNK, rows_local)
     block = min(ROWS, rows_local)
     chunks = length // chunk
-    place_dp = lax.axis_index("dp").astype(jnp.int32).reshape(1)
-    place_tensor = lax.axis_index("tensor").astype(jnp.int32).reshape(1)
+    place_dp = lax.axis_index(DP).astype(jnp.int32).reshape(1)
+    place_tensor = lax.axis_index(TP).astype(jnp.int32).reshape(1)
     narrow = (model // dp) % LANES != 0
     blocks = 1 if narrow else dp
     place_entry = place_dp * 0 if narrow else place_dp
@@ -613,8 +634,8 @@
         [((rows_local, model), bf16)] * 2,
     )(place_entry, tokens_local, upstream_local, gain_in)
     if narrow:
-        normed_local = exchange_blocks(normed_local, "dp", dp)
-        upstream_sent = exchange_blocks(upstream_sent, "dp", dp, ordered=False)
+        normed_local = exchange_blocks(normed_local, DP, dp)
+        upstream_sent = exchange_blocks(upstream_sent, DP, dp, ordered=False)
 
     def stack(rows, cols):
         rows = [r.reshape(-1, r.shape[-1]) for r in rows]
@@ -629,16 +650,15 @@
     forward_shapes = [((states, inner), f32), ((8, inner), f32), ((8, twice), f32)]
     backward_shapes = [((8, inner), f32), ((8, twice), f32), ((8, LANES), f32)]
     backward_shapes += [((states, inner), f32)] * 2 + [((8, inner), f32), ((8, twice), f32)]
-    forward_carry = [jnp.zeros(*one) for one in forward_shapes]
-
-    scan_far = gather_far(w_scan, "dp")
-    scan_far[0], taps_x, taps_bc, per_head, skip, gain, forward_carry = lax.optimization_barrier(
-        (scan_far[0], taps_x, taps_bc, per_head, skip, gain, forward_carry)
+
+    scan_far = gather_far(w_scan, DP)
+    scan_far[0], taps_x, taps_bc, per_head, skip, gain = lax.optimization_barrier(
+        (scan_far[0], taps_x, taps_bc, per_head, skip, gain)
     )
-    scan_pieces = gather_near(scan_far, "dp")
-    normed_pieces = gather(normed_local, "tensor")
-    late_pieces = gather(w_late, "dp")
-    upstream_pieces = gather(upstream_sent, "tensor")
+    scan_pieces = gather_near(scan_far, DP)
+    normed_pieces = gather(normed_local, TP)
+    late_pieces = gather(w_late, DP)
+    upstream_pieces = gather(upstream_sent, TP)
     dp_order, tensor_order = order_of(dp), order_of(tensor)
 
     per = rows_local // chunk
@@ -663,8 +683,7 @@
     calls = 2 if chunks % 2 == 0 else 1
     span = chunks // calls
     first = -(-chunks * 5 // 8)
-    carry = forward_carry
-    saved, weights = [], [scan_pieces[k] for k in dp_order]
+    carry, saved, weights = [], [], [scan_pieces[k] for k in dp_order]
     for start, stop in ((0, first), (first, chunks)):
         results = call(
             forward_kernel(width, head_dim, tensor, len(weights), per, start),
@@ -676,7 +695,7 @@
             + [anywhere] * len(saved),
             [ahead(cols, start) for cols in (inner, twice, inner, twice, LANES, inner)]
             + [pl.BlockSpec((1, states, inner), lambda c, place, start=start: (c + start, 0, 0))]
-            + [whole(one.shape) for one in carry]
+            + [whole(one) for one, _ in forward_shapes]
             + [whole((model, wide_cols))] * (start == 0),
             [
                 ((length, inner), f32), ((length, twice), f32), ((length, inner), bf16),
@@ -726,7 +745,7 @@
         mixed, gain,
     )
 
-    sum_terms = direct_terms(sums, "tensor")
+    sum_terms = direct_terms(sums, TP)
 
     scaled, d_mixed, d_gate, grad_gain = call(
         norm_kernel(inner_total, tensor), length // block,
@@ -739,23 +758,42 @@
         ],
     )(place_tensor, *sum_terms, gate_raw, grad_scaled, mixed, gain)
 
-    def tn(left, right):
-        return lax.dot_general(left, right, TN, preferred_element_type=f32).astype(bf16)
-
     share = model // dp
-    out_pairs = [tn(upstream[:, k * share : (k + 2) * share], scaled) for k in range(0, dp, 2)]
-    even = share * ((dp + 1) // 2)
-    gate_near = tn(normed[:, even:], d_gate)
-    gate_own = tn(normed[:, :even], d_gate)
+    wide_share = share * min(2, dp)
+    steps = model // wide_share
+
+    def products(left, right, bounds):
+        cols = right.shape[1]
+
+        def piece(i):
+            count = bounds[i + 1] - bounds[i]
+            return pl.BlockSpec(
+                (wide_share, cols),
+                lambda c, place: (jnp.clip(c - bounds[i], 0, count - 1), 0),
+            )
+
+        return call(
+            product_kernel(bounds), steps,
+            [pl.BlockSpec((length, wide_share), lambda c, place: (0, c)), whole(right.shape)],
+            [piece(i) for i in range(len(bounds) - 1)],
+            [
+                (((high - low) * wide_share, cols), bf16)
+                for low, high in zip(bounds, bounds[1:])
+            ],
+        )(place_tensor, left, right)
+
+    middle = (steps + 1) // 2
+    out_pairs = products(upstream, scaled, list(range(steps + 1)))
+    gate_own, *gate_near = products(normed, d_gate, sorted({0, middle, steps}))
     stay = rows_local * ((tensor + 1) // 2)
     branch_near = mm(scaled[stay:], full_out, NT).astype(bf16)
     branch_own = mm(scaled[:stay], full_out, NT).astype(bf16)
-    out_terms = far_first(out_pairs, "dp")
-    gate_terms = near_first(gate_own, [gate_near], "dp")
-    branch_terms = near_first(branch_own, [branch_near], "tensor")
+    out_terms = far_first(out_pairs, DP)
+    gate_terms = near_first(gate_own, gate_near, DP)
+    branch_terms = near_first(branch_own, [branch_near], TP)
     if narrow:
         branch_terms = [
-            (exchange_blocks(array, "dp", dp, True, False), k) for array, k in branch_terms
+            (exchange_blocks(array, DP, dp, True, False), k) for array, k in branch_terms
         ]
     slabs = rows_local // slab
     out_block = pl.BlockSpec((slab, 1, model), lambda c, place: (c, 0, 0))
@@ -770,7 +808,7 @@
         [((rows_local, 1, model), f32)],
     )(place_entry, tokens_local, *[array for array, _ in branch_terms])
 
-    carry = [jnp.zeros(*one) for one in backward_shapes]
+    carry = []
     columns = []
     for at in range(calls):
         start = chunks - 1 - at * span
@@ -781,7 +819,7 @@
             + [whole((8, inner)), whole((8, twice)), whole((8, LANES)), whole((1, inner))]
             + [whole(one.shape) for one in carry]
             + [anywhere] * len(columns),
-            [back(wide_cols, start)] + [whole(one.shape) for one in carry],
+            [back(wide_cols, start)] + [whole(one) for one, _ in backward_shapes],
             [((length, wide_cols), bf16), *backward_shapes],
             [pltpu.VMEM((chunk + 8, inner), f32), pltpu.VMEM((chunk + 8, twice), f32)],
             {1 + 8 + 4 + 7: 0} if columns else {},
@@ -793,12 +831,9 @@
     columns = columns[0]
     grad_x, grad_bc, grad_head = carry[:3]
 
-    later = even + (model - even) // 2 if dp % 4 == 0 else even
-    scan_near = [tn(normed[:, later:], columns)]
-    if later > even:
-        scan_near.append(tn(normed[:, even:later], columns))
-    scan_own = tn(normed[:, :even], columns)
-    scan_terms = near_first(scan_own, scan_near, "dp")
+    later = (middle + steps) // 2
+    scan_own, *scan_near = products(normed, columns, sorted({0, middle, later, steps}))
+    scan_terms = near_first(scan_own, scan_near[::-1], DP)
     features = model // 4
     leave = max(length - stay, rows_local)
     normed_own, normed_near, pre_part = call(
@@ -815,9 +850,9 @@
         ],
         [((stay, model), bf16), ((leave, model), bf16), ((8, model), f32)],
     )(place_tensor, normed, d_gate, columns, full_gate, full_scan)
-    normed_terms = near_first(normed_own, [normed_near], "tensor")
+    normed_terms = near_first(normed_own, [normed_near], TP)
     if narrow:
-        normed_terms = [(exchange_blocks(array, "dp", dp, True), k) for array, k in normed_terms]
+        normed_terms = [(exchange_blocks(array, DP, dp, True), k) for array, k in normed_terms]
     (input_grad,) = call(
         input_kernel(blocks, len(normed_terms)), slabs,
         [rows_of(slab, model)] * 2 + [whole((1, model))]
@@ -831,7 +866,7 @@
     cols = max(inner, twice + LANES)
     cols += -cols % 512
     if narrow:
-        pre_part = exchange_blocks(pre_part, "dp", dp, True)
+        pre_part = exchange_blocks(pre_part, DP, dp, True)
     rows = 24 + max(model // cols, 8)
     (packed,) = call(
         pack_kernel(blocks, cols), 1,
@@ -841,14 +876,14 @@
         ],
         [whole((rows, cols))], [((rows, cols), f32)], [pltpu.VMEM((8, model), f32)],
     )(place_entry, grad_x, grad_gain, grad_bc, grad_head, pre_part, gain_in)
-    small = all_sum(packed, "dp")
+    small = all_sum(packed, DP)
 
     assert cols % twice == 0 and model % cols == 0
     across = [small[16:, k : k + twice] for k in range(0, cols, twice)]
     across = jnp.concatenate(across, axis=0)
     keys_rows = grad_w_scan.shape[0]
     across = jnp.concatenate([grad_w_scan[:, inner : inner + twice], across], axis=0)
-    across = total_of(direct_terms(across, "tensor"))
+    across = total_of(direct_terms(across, TP))
     grad_w_bc = across[:keys_rows]
     of_bc = across[keys_rows:]
     count = rows - 16
@@ -880,14 +915,14 @@
 
 def solution(mesh):
     placed = (
-        P("tensor", "dp", None), P(), P("dp", None, "tensor"), P("dp", "tensor"), P("dp", None),
-        P(None, "tensor"), P("tensor"), P(), P(), P("tensor"), P("tensor"), P("tensor"),
-        P("tensor"), P("tensor", "dp"), P("tensor", "dp", None),
+        P(TP, DP, None), P(), P(DP, None, TP), P(DP, TP), P(DP, None),
+        P(None, TP), P(TP), P(), P(), P(TP), P(TP), P(TP),
+        P(TP), P(TP, DP), P(TP, DP, None),
     )
     results = (
-        P("tensor", "dp", None), P("tensor", "dp", None), P(), P("dp", None, "tensor"),
-        P("dp", "tensor"), P("dp", None), P(None, "tensor"), P("tensor"), P(), P(), P("tensor"),
-        P("tensor"), P("tensor"), P("tensor"), P("tensor", "dp"),
+        P(TP, DP, None), P(TP, DP, None), P(), P(DP, None, TP),
+        P(DP, TP), P(DP, None), P(None, TP), P(TP), P(), P(), P(TP),
+        P(TP), P(TP), P(TP), P(TP, DP),
     )
 
     return jax.shard_map(per_device, mesh=mesh, in_specs=placed, out_specs=results, check_vma=False)

time: 303 us -> 296 us (0.977)
  matrix products: 19.4 us -> 2.45 us
  Pallas kernels: 78.5 us -> 93.9 us
  waiting for transfers between devices: 110 us -> 100 us
    dot_general x9 -> x0, matrix products: 16.9 us -> none  [tn(): lax.dot_general(left, right, TN, preferred_element_type=f32).astype(bf16)]
    pallas_call x0 -> x3, Pallas kernels: none -> 16.4 us  [products(): call(product_kernel(bounds), steps, [pl.BlockSpec((length, wide_share), l...]
    ppermute x47, waiting for transfers between devices: 110 us -> 100 us  [swap(): return lax.ppermute(value, axis, [(i, i ^ bits) for i in range(size)])]
    unnamed x82 -> x74, local copies, waits for them, and re-layouts: 6.68 us -> 8.2 us
  transfers between devices with their start and end apart: 47 -> 47, of which waited for: 19 -> 19; matrix products, arithmetic and copies ran while one was open for 8% -> 8% of each run, Pallas kernels for 9% -> 14%
where the time goes in v3:
time: 296 us; the launch traced here: 295 us
  waiting for transfers between devices  100 us (34%)
  Pallas kernels  93.9 us (32%)
  starting transfers between devices  62.8 us (21%)
  local copies, waits for them, and re-layouts  17.2 us (6%)
  other arithmetic  17.2 us (6%)
    ppermute x47, waiting for transfers between devices, swap(): return lax.ppermute(value, axis, [(i, i ^ bits) for i in range(size)])  100 us
    ppermute x47, starting transfers between devices, swap(): return lax.ppermute(value, axis, [(i, i ^ bits) for i in range(size)])  62.8 us
    pallas_call x2, Pallas kernels, per_device(): call(backward_kernel(width, head_dim, len(columns)), span, [back(cols, st...  23.4 us
    pallas_call x2, Pallas kernels, per_device(): call(forward_kernel(width, head_dim, tensor, len(weights), per, start), s...  20.3 us
    pallas_call x3, Pallas kernels, products(): call(product_kernel(bounds), steps, [pl.BlockSpec((length, wide_share), l...  16.4 us
    pallas_call x1, Pallas kernels, per_device(): call(gate_kernel(tensor, dp, parts), length // block, [gate_piece(p) for...  8.98 us
    unnamed x74, local copies, waits for them, and re-layouts  8.2 us
    pallas_call x1, Pallas kernels, per_device(): call(normed_kernel, 4, [pl.BlockSpec((length, features), lambda c, place:...  7.69 us
  transfers between devices with their start and end apart: 47, of which 19 were waited for; matrix products, arithmetic and copies ran while one was open for 8% of the time, Pallas kernels for 14%

profile of v3, /device:TPU:0, one launch (start us, length us, event | category | flops | bytes accessed | tf_op | source)
XLA Modules:
  0.0 294.8 jit_solution(13329506036606144490)
XLA Ops:
  3.5 1.5 fusion.2
  5.1 1.3 select_maximum_fusion.2.refs_14_.refs_7_.refs_10_
  6.4 1.3 select_maximum_fusion.1.refs_13_.refs_6_.refs_9_
  7.7 1.3 select_maximum_fusion.refs_12_.refs_5_.refs_8_
  9.9 3.0 %collective-permute-start.16 = (bf16[128,896]{1,0:T(8,128)(2,1)S(1)}, bf16[128,896]{1,0:T(8,128)(2,1)S(1)}, u32[]{:S(2)}, u32[]{:S(2)}) collective-permute-start(bf16[128,896]{1,0:T(8,128)(2,1)S(1)} %maximum_maximum_fusion.refs_4_), channel_id=1, source_target_pairs={{0,4},{4,0},{8,12},{12,8},{16,20},{20,16},{24,28},{28,24},{1,5},{5... | collective-permute-start | bytes 688136 | tf_op jit(solution)/shard_map/ppermute | solution.py:41
  13.0 3.6 %collective-permute-start.15 = (bf16[128,896]{1,0:T(8,128)(2,1)S(1)}, bf16[128,896]{1,0:T(8,128)(2,1)S(1)}, u32[]{:S(2)}, u32[]{:S(2)}) collective-permute-start(bf16[128,896]{1,0:T(8,128)(2,1)S(1)} %maximum_maximum_fusion.refs_4_), channel_id=1, source_target_pairs={{0,24},{4,28},{8,16},{12,20},{16,8},{20,12},{24,0},{28,4},{1,25},{... | collective-permute-start | bytes 688136 | tf_op jit(solution)/shard_map/ppermute | solution.py:41
  16.6 2.5 shard_map.262
  19.1 1.5 collective-permute-start
  20.8 2.0 collective-permute-start.11
  22.8 1.6 collective-permute-start.13
  24.3 15.1 %collective-permute-start.9 = (bf16[128,1024]{1,0:T(8,128)(2,1)S(1)}, bf16[128,1024]{1,0:T(8,128)(2,1)}, u32[]{:S(2)}, u32[]{:S(2)}) collective-permute-start(bf16[128,1024]{1,0:T(8,128)(2,1)S(1)} %pad_maximum_fusion.1.refs_8_), channel_id=1, source_target_pairs={{0,16},{4,20},{8,24},{12,28},{16,0},{20,4},{24,8},{28,12},{1,17},{... | collective-permute-start | bytes 786440 | tf_op jit(solution)/shard_map/ppermute | solution.py:41
  39.5 8.5 %collective-permute-done.14.refs_6_ = bf16[128,896]{1,0:T(8,128)(2,1)S(1)} collective-permute-done((bf16[128,896]{1,0:T(8,128)(2,1)S(1)}, bf16[128,896]{1,0:T(8,128)(2,1)S(1)}, u32[]{:S(2)}, u32[]{:S(2)}) %collective-permute-start.14) | collective-permute-done | bytes 229408 | tf_op jit(solution)/shard_map/ppermute | solution.py:41
  48.0 1.5 collective-permute-start.3
  50.2 8.2 %collective-permute-done.9.refs_12_ = bf16[128,1024]{1,0:T(8,128)(2,1)} collective-permute-done((bf16[128,1024]{1,0:T(8,128)(2,1)S(1)}, bf16[128,1024]{1,0:T(8,128)(2,1)}, u32[]{:S(2)}, u32[]{:S(2)}) %collective-permute-start.9) | collective-permute-done | bytes 262176 | tf_op jit(solution)/shard_map/ppermute | solution.py:41
  59.0 2.4 collective-permute-done.7.refs_10_
  61.9 1.5 collective-permute-start.18
  63.4 5.7 %collective-permute-done.19.refs_11_ = bf16[128,896]{1,0:T(8,128)(2,1)S(1)} collective-permute-done((bf16[128,896]{1,0:T(8,128)(2,1)S(1)}, bf16[128,896]{1,0:T(8,128)(2,1)S(1)}, u32[]{:S(2)}, u32[]{:S(2)}) %collective-permute-start.19) | collective-permute-done | bytes 229408 | tf_op jit(solution)/shard_map/ppermute | solution.py:41
  69.6 1.9 collective-permute-done.18.refs_10_
  72.1 5.9 %collective-permute-done.17.refs_9_ = bf16[128,896]{1,0:T(8,128)(2,1)S(1)} collective-permute-done((bf16[128,896]{1,0:T(8,128)(2,1)S(1)}, bf16[128,896]{1,0:T(8,128)(2,1)S(1)}, u32[]{:S(2)}, u32[]{:S(2)}) %collective-permute-start.17) | collective-permute-done | bytes 229408 | tf_op jit(solution)/shard_map/ppermute | solution.py:41
  78.5 1.5 collective-permute-start.10
  80.8 12.0 %shard_map.263 = (f32[1024,512]{1,0:T(8,128)}, f32[1024,256]{1,0:T(8,128)}, bf16[1024,512]{1,0:T(8,128)(2,1)}, bf16[1024,256]{1,0:T(8,128)(2,1)}, f32[1024,128]{...) custom-call(s32[1]{0:T(128)} %bitcast.2.place, ...), custom_call_target="tpu_custom_call" | custom-call | tf_op jit(solution)/shard_map/pallas_call | solution.py:688
  92.8 8.3 %shard_map.264 = (f32[1024,512]{1,0:T(8,128)}, f32[1024,256]{1,0:T(8,128)}, bf16[1024,512]{1,0:T(8,128)(2,1)}, bf16[1024,256]{1,0:T(8,128)(2,1)}, f32[1024,128]{...) custom-call(s32[1]{0:T(128)} %bitcast.2.place, ...), custom_call_target="tpu_custom_call", output_to_operand_aliasing={{0}: (13, {}), {1}: (14, {}), {2}: (15, {}), {3}: (16, {}),... | custom-call | tf_op jit(solution)/shard_map/pallas_call | solution.py:688
  102.0 9.0 %shard_map.265 = (f32[1024,512]{1,0:T(8,128)}, f32[1024,512]{1,0:T(8,128)}, f32[4,8,256]{2,1,0:T(8,128)}, bf16[1024,1024]{1,0:T(8,128)(2,1)}, bf16[1024,1024]{1,...) custom-call(s32[1]{0:T(128)} %bitcast.2.place, bf16[256,1024]{1,0:T(8,128)(2,1)} %get-tuple-element.77.refs_0_, ...), custom_call_target="tpu_custom_call" | custom-call | tf_op jit(solution)/shard_map/pallas_call | solution.py:728
  111.0 1.6 collective-permute-start.21
  112.9 1.9 collective-permute-done.22.refs_3_
  115.9 6.4 %shard_map.266 = (bf16[1024,512]{1,0:T(8,128)(2,1)}, f32[1024,512]{1,0:T(8,128)}, bf16[1024,512]{1,0:T(8,128)(2,1)}, f32[8,512]{1,0:T(8,128)}) custom-call(s32[1]{0:T(128)} %bitcast.2.place, f32[4,8,256]{2,1,0:T(8,128)} %get-tuple-element.97.refs_0_, f32[4,8,256]{2,1,0:T(8,128)} %copy-done.31, f32[4,8,256]{2,1,0:T(8,128)} %copy-done.30, ...), custom_call_target="tpu_custom_call" | custom-call | tf_op jit(solution)/shard_map/pallas_call | solution.py:750
  122.3 11.6 %shard_map.268 = (bf16[1024,896]{1,0:T(8,128)(2,1)}, f32[8,512]{1,0:T(8,128)}, f32[8,256]{1,0:T(8,128)}, f32[8,128]{1,0:T(8,128)}, f32[128,512]{1,0:T(8,128)}, /...) custom-call(s32[1]{0:T(128)} %bitcast.2.place, f32[1024,512]{1,0:T(8,128)} %get-tuple-element.104.refs_0_, ...), custom_call_target="tpu_custom_call" | custom-call | tf_op jit(solution)/shard_map/pallas_call | solution.py:815
  133.8 11.9 %shard_map.269 = (bf16[1024,896]{1,0:T(8,128)(2,1)}, f32[8,512]{1,0:T(8,128)}, f32[8,256]{1,0:T(8,128)}, f32[8,128]{1,0:T(8,128)}, f32[128,512]{1,0:T(8,128)}, /...) custom-call(s32[1]{0:T(128)} %bitcast.2.place, ...), custom_call_target="tpu_custom_call", output_to_operand_aliasing={{0}: (20, {})} | custom-call | tf_op jit(solution)/shard_map/pallas_call | solution.py:815
  145.8 7.7 %shard_map.270 = (bf16[512,1024]{1,0:T(8,128)(2,1)}, bf16[512,1024]{1,0:T(8,128)(2,1)}, f32[8,1024]{1,0:T(8,128)}) custom-call(s32[1]{0:T(128)} %bitcast.2.place, bf16[1024,1024]{1,0:T(8,128)(2,1)} %get-tuple-element.102.tokens.left, bf16[1024,512]{1,0:T(8,128)(2,1)} %get-tuple-element.103.d_gate.right, bf16[1024,896]{1,0:T(8,128)(2,1)} %get-tuple-element.119.columns.right, ...), custom_call_target="tpu_custom_call" | custom-call | tf_op jit(solution)/shard_map/pallas_call | solution.py:839
  153.4 1.5 shard_map.273
  154.9 1.4 collective-permute-start.32
  157.1 2.6 collective-permute-done.32
  159.7 2.5 collective-permute-start.35
  162.2 1.9 collective-permute-start.33
  164.1 1.7 convolution_convert_fusion
  165.8 4.9 %shard_map.274 = (bf16[512,512]{1,0:T(8,128)(2,1)}, bf16[512,512]{1,0:T(8,128)(2,1)}) custom-call(s32[1]{0:T(128)} %bitcast.2.place, bf16[1024,1024]{1,0:T(8,128)(2,1)} %get-tuple-element.102.tokens.left, bf16[1024,512]{1,0:T(8,128)(2,1)} %get-tuple-element.103.d_gate.right), custom_call_target="tpu_custom_call" | custom-call | tf_op jit(solution)/shard_map/pallas_call | solution.py:775
  170.8 6.4 %shard_map.272 = (bf16[512,896]{1,0:T(8,128)(2,1)}, bf16[256,896]{1,0:T(8,128)(2,1)}, bf16[256,896]{1,0:T(8,128)(2,1)}) custom-call(s32[1]{0:T(128)} %bitcast.2.place, bf16[1024,1024]{1,0:T(8,128)(2,1)} %get-tuple-element.102.tokens.left, bf16[1024,896]{1,0:T(8,128)(2,1)} %get-tuple-element.119.columns.right), custom_call_target="tpu_custom_call" | custom-call | tf_op jit(solution)/shard_map/pallas_call | solution.py:775
  177.2 5.1 %shard_map.275 = (bf16[256,512]{1,0:T(8,128)(2,1)}, bf16[256,512]{1,0:T(8,128)(2,1)}, bf16[256,512]{1,0:T(8,128)(2,1)}, bf16[256,512]{1,0:T(8,128)(2,1)}) custom-call(s32[1]{0:T(128)} %bitcast.2.place, bf16[1024,1024]{1,0:T(8,128)(2,1)} %get-tuple-element.134.left, bf16[1024,512]{1,0:T(8,128)(2,1)} %get-tuple-element.100.right), custom_call_target="tpu_custom_call" | custom-call | tf_op jit(solution)/shard_map/pallas_call | solution.py:775
  182.3 2.9 collective-permute-start.44
  185.3 1.3 collective-permute-start.45
  186.6 1.4 collective-permute-start.39
  189.8 4.2 %collective-permute-done.43 = bf16[256,512]{1,0:T(8,128)(2,1)S(1)} collective-permute-done((bf16[256,512]{1,0:T(8,128)(2,1)}, bf16[256,512]{1,0:T(8,128)(2,1)S(1)}, u32[]{:S(2)}, u32[]{:S(2)}) %collective-permute-start.43) | collective-permute-done | bytes 262176 | tf_op jit(solution)/shard_map/ppermute | solution.py:41
  193.9 1.4 collective-permute-start.27
  195.3 8.6 %collective-permute-done.44 = bf16[256,512]{1,0:T(8,128)(2,1)S(1)} collective-permute-done((bf16[256,512]{1,0:T(8,128)(2,1)}, bf16[256,512]{1,0:T(8,128)(2,1)S(1)}, u32[]{:S(2)}, u32[]{:S(2)}) %collective-permute-start.44) | collective-permute-done | bytes 262176 | tf_op jit(solution)/shard_map/ppermute | solution.py:41
  203.9 1.4 collective-permute-start.30
  208.2 1.3 reshape_squeeze.3
  209.5 1.3 reduce_sum.9
  210.8 10.2 %collective-permute-done.46 = bf16[128,512]{1,0:T(8,128)(2,1)S(1)} collective-permute-done((bf16[128,512]{1,0:T(8,128)(2,1)S(1)}, bf16[128,512]{1,0:T(8,128)(2,1)S(1)}, u32[]{:S(2)}, u32[]{:S(2)}) %collective-permute-start.46) | collective-permute-done | bytes 131104 | tf_op jit(solution)/shard_map/ppermute | solution.py:41
  224.9 1.3 add_convert_fusion.8
  226.3 2.6 collective-permute-start.40
  228.9 1.8 collective-permute-start.41
  231.7 2.8 collective-permute-done.40
  234.6 5.2 %collective-permute-done.42 = bf16[128,512]{1,0:T(8,128)(2,1)S(1)} collective-permute-done((bf16[128,512]{1,0:T(8,128)(2,1)S(1)}, bf16[128,512]{1,0:T(8,128)(2,1)S(1)}, u32[]{:S(2)}, u32[]{:S(2)}) %collective-permute-start.42) | collective-permute-done | bytes 131104 | tf_op jit(solution)/shard_map/ppermute | solution.py:41
  239.7 1.8 collective-permute-start.28
  241.5 7.8 %collective-permute-done.41 = bf16[128,512]{1,0:T(8,128)(2,1)S(1)} collective-permute-done((bf16[128,512]{1,0:T(8,128)(2,1)S(1)}, bf16[128,512]{1,0:T(8,128)(2,1)S(1)}, u32[]{:S(2)}, u32[]{:S(2)}) %collective-permute-start.41) | collective-permute-done | bytes 131104 | tf_op jit(solution)/shard_map/ppermute | solution.py:41
  250.4 4.2 %collective-permute-done.29 = bf16[128,896]{1,0:T(8,128)(2,1)S(1)} collective-permute-done((bf16[128,896]{1,0:T(8,128)(2,1)S(1)}, bf16[128,896]{1,0:T(8,128)(2,1)S(1)}, u32[]{:S(2)}, u32[]{:S(2)}) %collective-permute-start.29) | collective-permute-done | bytes 229408 | tf_op jit(solution)/shard_map/ppermute | solution.py:41
  254.6 3.4 %collective-permute-done.31 = bf16[128,896]{1,0:T(8,128)(2,1)S(1)} collective-permute-done((bf16[128,896]{1,0:T(8,128)(2,1)S(1)}, bf16[128,896]{1,0:T(8,128)(2,1)S(1)}, u32[]{:S(2)}, u32[]{:S(2)}) %collective-permute-start.31) | collective-permute-done | bytes 229408 | tf_op jit(solution)/shard_map/ppermute | solution.py:41
  259.7 1.7 collective-permute-start.36
  264.0 1.2 add_convert_fusion
  265.3 1.7 collective-permute-start.26
  270.4 10.5 %collective-permute-done.24.refs_1_ = bf16[256,1024]{1,0:T(8,128)(2,1)S(1)} collective-permute-done((bf16[256,1024]{1,0:T(8,128)(2,1)S(1)}, bf16[256,1024]{1,0:T(8,128)(2,1)S(1)}, u32[]{:S(2)}, u32[]{:S(2)}) %collective-permute-start.24) | collective-permute-done | bytes 524320 | tf_op jit(solution)/shard_map/ppermute | solution.py:41
  281.7 3.2 %shard_map.267 = f32[256,1,1024]{2,1,0:T(1,128)} custom-call(s32[1]{0:T(128)} %bitcast.place, bf16[256,1024]{1,0:T(8,128)(2,1)} %bitcast.37, bf16[512,1024]{1,0:T(8,128)(2,1)} %copy-done.3, bf16[256,1024]{1,0:T(8,128)(2,1)} %copy-done.12, bf16[512,1024]{1,0:T(8,128)(2,1)} %copy-done.4), custom_call_target="tpu_custom_call" | custom-call | tf_op jit(solution)/shard_map/pallas_call | solution.py:804
  284.9 5.5 %collective-permute-done.26.refs_1_ = bf16[256,1024]{1,0:T(8,128)(2,1)S(1)} collective-permute-done((bf16[256,1024]{1,0:T(8,128)(2,1)S(1)}, bf16[256,1024]{1,0:T(8,128)(2,1)S(1)}, u32[]{:S(2)}, u32[]{:S(2)}) %collective-permute-start.26) | collective-permute-done | bytes 524320 | tf_op jit(solution)/shard_map/ppermute | solution.py:41
  291.2 3.6 %shard_map.271 = f32[256,1,1024]{2,1,0:T(1,128)} custom-call(s32[1]{0:T(128)} %bitcast.place, bf16[256,1024]{1,0:T(8,128)(2,1)} %bitcast.38, bf16[256,1024]{1,0:T(8,128)(2,1)} %bitcast.40, f32[1,1024]{1,0:T(1,128)} %bitcast.46, bf16[512,1024]{1,0:T(8,128)(2,1)} %get-tuple-element.121.refs_0_, bf16[256,1024]{1,0:T(8,128)(2,1)} %copy-done.13, ...), custom_call_target="tpu_custom_call" | custom-call | tf_op jit(solution)/shard_map/pallas_call | solution.py:856
  (159 shorter events, 31.2 us)
Async XLA Ops:
  0.6 19.9 %copy-start.28 = (bf16[512,128]{1,0:T(8,128)(2,1)S(1)}, bf16[512,128]{1,0:T(8,128)(2,1)}, u32[]{:S(2)}) copy-start(bf16[512,128]{1,0:T(8,128)(2,1)} %param.28) | copy-start | bytes 393220
  9.9 70.7 %copy-start.8 = (bf16[128,896]{1,0:T(8,128)(2,1)}, bf16[128,896]{1,0:T(8,128)(2,1)S(1)}, u32[]{:S(2)}) copy-start(bf16[128,896]{1,0:T(8,128)(2,1)S(1)} %maximum_maximum_fusion.refs_4_) | copy-start | bytes 688132
  9.9 12.8 %collective-permute-start.16 = (bf16[128,896]{1,0:T(8,128)(2,1)S(1)}, bf16[128,896]{1,0:T(8,128)(2,1)S(1)}, u32[]{:S(2)}, u32[]{:S(2)}) collective-permute-start(bf16[128,896]{1,0:T(8,128)(2,1)S(1)} %maximum_maximum_fusion.refs_4_), channel_id=1, source_target_pairs={{0,4},{4,0},{8,12},{12,8},{16,20},{20,16},{24,28},{28,24},{1,5},{5... | collective-permute-start | bytes 688136 | tf_op jit(solution)/shard_map/ppermute | solution.py:41
  13.0 11.4 %collective-permute-start.15 = (bf16[128,896]{1,0:T(8,128)(2,1)S(1)}, bf16[128,896]{1,0:T(8,128)(2,1)S(1)}, u32[]{:S(2)}, u32[]{:S(2)}) collective-permute-start(bf16[128,896]{1,0:T(8,128)(2,1)S(1)} %maximum_maximum_fusion.refs_4_), channel_id=1, source_target_pairs={{0,24},{4,28},{8,16},{12,20},{16,8},{20,12},{24,0},{28,4},{1,25},{... | collective-permute-start | bytes 688136 | tf_op jit(solution)/shard_map/ppermute | solution.py:41
  16.6 31.4 %collective-permute-start.14 = (bf16[128,896]{1,0:T(8,128)(2,1)S(1)}, bf16[128,896]{1,0:T(8,128)(2,1)S(1)}, u32[]{:S(2)}, u32[]{:S(2)}) collective-permute-start(bf16[128,896]{1,0:T(8,128)(2,1)S(1)} %maximum_maximum_fusion.refs_4_), channel_id=1, source_target_pairs={{0,16},{4,20},{8,24},{12,28},{16,0},{20,4},{24,8},{28,12},{1,17},{... | collective-permute-start | bytes 688136 | tf_op jit(solution)/shard_map/ppermute | solution.py:41
  19.1 39.4 %collective-permute-start = (bf16[256,1024]{1,0:T(8,128)(2,1)}, bf16[256,1024]{1,0:T(8,128)(2,1)S(1)}, u32[]{:S(2)}, u32[]{:S(2)}) collective-permute-start(bf16[256,1024]{1,0:T(8,128)(2,1)} %get-tuple-element.77.refs_0_), channel_id=1, source_target_pairs={{0,2},{1,3},{2,0},{3,1},{4,6},{5,7},{6,4},{7,5},{8,10},{9,11},{10,... | collective-permute-start | bytes 1572872 | tf_op jit(solution)/shard_map/ppermute | solution.py:41
  20.8 80.3 %copy-start.6 = (bf16[128,1024]{1,0:T(8,128)(2,1)}, bf16[128,1024]{1,0:T(8,128)(2,1)S(1)}, u32[]{:S(2)}) copy-start(bf16[128,1024]{1,0:T(8,128)(2,1)S(1)} %pad_maximum_fusion.1.refs_8_) | copy-start | bytes 786436
  20.8 28.8 %collective-permute-start.11 = (bf16[128,1024]{1,0:T(8,128)(2,1)S(1)}, bf16[128,1024]{1,0:T(8,128)(2,1)S(1)}, u32[]{:S(2)}, u32[]{:S(2)}) collective-permute-start(bf16[128,1024]{1,0:T(8,128)(2,1)S(1)} %pad_maximum_fusion.1.refs_8_), channel_id=1, source_target_pairs={{0,24},{4,28},{8,16},{12,20},{16,8},{20,12},{24,0},{28,4},{1,25},{... | collective-permute-start | bytes 786440 | tf_op jit(solution)/shard_map/ppermute | solution.py:41
  22.8 25.2 %copy-start.19 = (bf16[128,896]{1,0:T(8,128)(2,1)}, bf16[128,896]{1,0:T(8,128)(2,1)S(1)}, u32[]{:S(2)}) copy-start(bf16[128,896]{1,0:T(8,128)(2,1)S(1)} %collective-permute-done.16.refs_8_) | copy-start | bytes 688132
  22.8 26.7 %collective-permute-start.13 = (bf16[128,896]{1,0:T(8,128)(2,1)S(1)}, bf16[128,896]{1,0:T(8,128)(2,1)S(1)}, u32[]{:S(2)}, u32[]{:S(2)}) collective-permute-start(bf16[128,896]{1,0:T(8,128)(2,1)S(1)} %maximum_maximum_fusion.refs_4_), channel_id=1, source_target_pairs={{0,8},{4,12},{8,0},{12,4},{16,24},{20,28},{24,16},{28,20},{1,9},{5... | collective-permute-start | bytes 688136 | tf_op jit(solution)/shard_map/ppermute | solution.py:41
  24.3 39.1 %copy-start.20 = (bf16[128,896]{1,0:T(8,128)(2,1)}, bf16[128,896]{1,0:T(8,128)(2,1)S(1)}, u32[]{:S(2)}) copy-start(bf16[128,896]{1,0:T(8,128)(2,1)S(1)} %collective-permute-done.15.refs_7_) | copy-start | bytes 688132
  24.3 34.1 %collective-permute-start.9 = (bf16[128,1024]{1,0:T(8,128)(2,1)S(1)}, bf16[128,1024]{1,0:T(8,128)(2,1)}, u32[]{:S(2)}, u32[]{:S(2)}) collective-permute-start(bf16[128,1024]{1,0:T(8,128)(2,1)S(1)} %pad_maximum_fusion.1.refs_8_), channel_id=1, source_target_pairs={{0,16},{4,20},{8,24},{12,28},{16,0},{20,4},{24,8},{28,12},{1,17},{... | collective-permute-start | bytes 786440 | tf_op jit(solution)/shard_map/ppermute | solution.py:41
  48.0 21.1 %collective-permute-start.3 = (bf16[256,1024]{1,0:T(8,128)(2,1)}, bf16[256,1024]{1,0:T(8,128)(2,1)S(1)}, u32[]{:S(2)}, u32[]{:S(2)}) collective-permute-start(bf16[256,1024]{1,0:T(8,128)(2,1)} %get-tuple-element.78.refs_4_), channel_id=1, source_target_pairs={{0,2},{1,3},{2,0},{3,1},{4,6},{5,7},{6,4},{7,5},{8,10},{9,11},{10,... | collective-permute-start | bytes 1572872 | tf_op jit(solution)/shard_map/ppermute | solution.py:41
  49.5 30.5 %copy-start.22 = (bf16[128,896]{1,0:T(8,128)(2,1)}, bf16[128,896]{1,0:T(8,128)(2,1)S(1)}, u32[]{:S(2)}) copy-start(bf16[128,896]{1,0:T(8,128)(2,1)S(1)} %collective-permute-done.13.refs_5_) | copy-start | bytes 688132
  49.5 11.9 %collective-permute-start.7 = (bf16[128,1024]{1,0:T(8,128)(2,1)S(1)}, bf16[128,1024]{1,0:T(8,128)(2,1)}, u32[]{:S(2)}, u32[]{:S(2)}) collective-permute-start(bf16[128,1024]{1,0:T(8,128)(2,1)S(1)} %pad_maximum_fusion.1.refs_8_), channel_id=1, source_target_pairs={{0,8},{4,12},{8,0},{12,4},{16,24},{20,28},{24,16},{28,20},{1,9},{5... | collective-permute-start | bytes 786440 | tf_op jit(solution)/shard_map/ppermute | solution.py:41
  49.6 51.5 %copy-start.14 = (bf16[128,1024]{1,0:T(8,128)(2,1)}, bf16[128,1024]{1,0:T(8,128)(2,1)S(1)}, u32[]{:S(2)}) copy-start(bf16[128,1024]{1,0:T(8,128)(2,1)S(1)} %collective-permute-done.11.refs_14_) | copy-start | bytes 786436
  49.6 12.3 %collective-permute-start.6 = (bf16[128,1024]{1,0:T(8,128)(2,1)S(1)}, bf16[128,1024]{1,0:T(8,128)(2,1)S(1)}, u32[]{:S(2)}, u32[]{:S(2)}) collective-permute-start(bf16[128,1024]{1,0:T(8,128)(2,1)S(1)} %pad_maximum_fusion.1.refs_8_), channel_id=1, source_target_pairs={{0,4},{4,0},{8,12},{12,8},{16,20},{20,16},{24,28},{28,24},{1,5},{5... | collective-permute-start | bytes 786440 | tf_op jit(solution)/shard_map/ppermute | solution.py:41
  58.5 20.1 %collective-permute-start.1 = (bf16[256,1024]{1,0:T(8,128)(2,1)}, bf16[256,1024]{1,0:T(8,128)(2,1)S(1)}, u32[]{:S(2)}, u32[]{:S(2)}) collective-permute-start(bf16[256,1024]{1,0:T(8,128)(2,1)} %get-tuple-element.77.refs_0_), channel_id=1, source_target_pairs={{0,1},{1,0},{2,3},{3,2},{4,5},{5,4},{6,7},{7,6},{8,9},{9,8},{10,11... | collective-permute-start | bytes 1572872 | tf_op jit(solution)/shard_map/ppermute | solution.py:41
  58.5 22.2 %copy-start = (bf16[256,1024]{1,0:T(8,128)(2,1)}, bf16[256,1024]{1,0:T(8,128)(2,1)S(1)}, u32[]{:S(2)}) copy-start(bf16[256,1024]{1,0:T(8,128)(2,1)S(1)} %collective-permute-done.refs_2_.refs_1_) | copy-start | bytes 1572868
  58.5 21.6 %collective-permute-start.2 = (bf16[256,1024]{1,0:T(8,128)(2,1)S(1)}, bf16[256,1024]{1,0:T(8,128)(2,1)S(1)}, u32[]{:S(2)}, u32[]{:S(2)}) collective-permute-start(bf16[256,1024]{1,0:T(8,128)(2,1)S(1)} %collective-permute-done.refs_2_.refs_1_), channel_id=1, source_target_pairs={{0,1},{1,0},{2,3},{3,2},{4,5},{5,4},{6,7},{7,6},{8,9},{9,8},{10,11... | collective-permute-start | bytes 1572872 | tf_op jit(solution)/shard_map/ppermute | solution.py:41
  61.4 7.7 %collective-permute-start.19 = (bf16[128,896]{1,0:T(8,128)(2,1)S(1)}, bf16[128,896]{1,0:T(8,128)(2,1)S(1)}, u32[]{:S(2)}, u32[]{:S(2)}) collective-permute-start(bf16[128,896]{1,0:T(8,128)(2,1)S(1)} %collective-permute-done.15.refs_7_), channel_id=1, source_target_pairs={{0,4},{4,0},{8,12},{12,8},{16,20},{20,16},{24,28},{28,24},{1,5},{5... | collective-permute-start | bytes 688136 | tf_op jit(solution)/shard_map/ppermute | solution.py:41
  61.9 9.7 %collective-permute-start.18 = (bf16[128,896]{1,0:T(8,128)(2,1)}, bf16[128,896]{1,0:T(8,128)(2,1)S(1)}, u32[]{:S(2)}, u32[]{:S(2)}) collective-permute-start(bf16[128,896]{1,0:T(8,128)(2,1)} %copy-done.21), channel_id=1, source_target_pairs={{0,4},{4,0},{8,12},{12,8},{16,20},{20,16},{24,28},{28,24},{1,5},{5... | collective-permute-start | bytes 688136 | tf_op jit(solution)/shard_map/ppermute | solution.py:41
  69.1 10.9 %copy-start.23 = (bf16[128,896]{1,0:T(8,128)(2,1)}, bf16[128,896]{1,0:T(8,128)(2,1)S(1)}, u32[]{:S(2)}) copy-start(bf16[128,896]{1,0:T(8,128)(2,1)S(1)} %collective-permute-done.19.refs_11_) | copy-start | bytes 688132
  69.1 32.1 %collective-permute-start.4 = (bf16[256,1024]{1,0:T(8,128)(2,1)}, bf16[256,1024]{1,0:T(8,128)(2,1)S(1)}, u32[]{:S(2)}, u32[]{:S(2)}) collective-permute-start(bf16[256,1024]{1,0:T(8,128)(2,1)} %get-tuple-element.78.refs_4_), channel_id=1, source_target_pairs={{0,1},{1,0},{2,3},{3,2},{4,5},{5,4},{6,7},{7,6},{8,9},{9,8},{10,11... | collective-permute-start | bytes 1572872 | tf_op jit(solution)/shard_map/ppermute | solution.py:41
  69.1 32.0 %copy-start.10 = (bf16[256,1024]{1,0:T(8,128)(2,1)}, bf16[256,1024]{1,0:T(8,128)(2,1)S(1)}, u32[]{:S(2)}) copy-start(bf16[256,1024]{1,0:T(8,128)(2,1)S(1)} %collective-permute-done.3.refs_5_) | copy-start | bytes 1572868
  69.1 32.1 %collective-permute-start.5 = (bf16[256,1024]{1,0:T(8,128)(2,1)S(1)}, bf16[256,1024]{1,0:T(8,128)(2,1)}, u32[]{:S(2)}, u32[]{:S(2)}) collective-permute-start(bf16[256,1024]{1,0:T(8,128)(2,1)S(1)} %collective-permute-done.3.refs_5_), channel_id=1, source_target_pairs={{0,1},{1,0},{2,3},{3,2},{4,5},{5,4},{6,7},{7,6},{8,9},{9,8},{10,11... | collective-permute-start | bytes 1572872 | tf_op jit(solution)/shard_map/ppermute | solution.py:41
  71.6 8.5 %copy-start.24 = (bf16[128,896]{1,0:T(8,128)(2,1)}, bf16[128,896]{1,0:T(8,128)(2,1)S(1)}, u32[]{:S(2)}) copy-start(bf16[128,896]{1,0:T(8,128)(2,1)S(1)} %collective-permute-done.18.refs_10_) | copy-start | bytes 688132
  71.6 6.4 %collective-permute-start.17 = (bf16[128,896]{1,0:T(8,128)(2,1)S(1)}, bf16[128,896]{1,0:T(8,128)(2,1)S(1)}, u32[]{:S(2)}, u32[]{:S(2)}) collective-permute-start(bf16[128,896]{1,0:T(8,128)(2,1)S(1)} %collective-permute-done.13.refs_5_), channel_id=1, source_target_pairs={{0,4},{4,0},{8,12},{12,8},{16,20},{20,16},{24,28},{28,24},{1,5},{5... | collective-permute-start | bytes 688136 | tf_op jit(solution)/shard_map/ppermute | solution.py:41
  78.0 23.2 %collective-permute-start.12 = (bf16[128,1024]{1,0:T(8,128)(2,1)S(1)}, bf16[128,1024]{1,0:T(8,128)(2,1)}, u32[]{:S(2)}, u32[]{:S(2)}) collective-permute-start(bf16[128,1024]{1,0:T(8,128)(2,1)S(1)} %collective-permute-done.11.refs_14_), channel_id=1, source_target_pairs={{0,4},{4,0},{8,12},{12,8},{16,20},{20,16},{24,28},{28,24},{1,5},{5... | collective-permute-start | bytes 786440 | tf_op jit(solution)/shard_map/ppermute | solution.py:41
  78.5 22.6 %collective-permute-start.10 = (bf16[128,1024]{1,0:T(8,128)(2,1)}, bf16[128,1024]{1,0:T(8,128)(2,1)}, u32[]{:S(2)}, u32[]{:S(2)}) collective-permute-start(bf16[128,1024]{1,0:T(8,128)(2,1)} %collective-permute-done.9.refs_12_), channel_id=1, source_target_pairs={{0,4},{4,0},{8,12},{12,8},{16,20},{20,16},{24,28},{28,24},{1,5},{5... | collective-permute-start | bytes 786440 | tf_op jit(solution)/shard_map/ppermute | solution.py:41
  80.1 21.1 %collective-permute-start.8 = (bf16[128,1024]{1,0:T(8,128)(2,1)}, bf16[128,1024]{1,0:T(8,128)(2,1)}, u32[]{:S(2)}, u32[]{:S(2)}) collective-permute-start(bf16[128,1024]{1,0:T(8,128)(2,1)} %collective-permute-done.7.refs_10_), channel_id=1, source_target_pairs={{0,4},{4,0},{8,12},{12,8},{16,20},{20,16},{24,28},{28,24},{1,5},{5... | collective-permute-start | bytes 786440 | tf_op jit(solution)/shard_map/ppermute | solution.py:41
  111.0 3.8 %collective-permute-start.22 = (f32[4,8,256]{2,1,0:T(8,128)}, f32[4,8,256]{2,1,0:T(8,128)S(1)}, u32[]{:S(2)}, u32[]{:S(2)}) collective-permute-start(f32[4,8,256]{2,1,0:T(8,128)} %get-tuple-element.97.refs_0_), channel_id=1, source_target_pairs={{0,3},{1,2},{2,1},{3,0},{4,7},{5,6},{6,5},{7,4},{8,11},{9,10},{10,... | collective-permute-start | bytes 98312 | tf_op jit(solution)/shard_map/ppermute | solution.py:41
  111.0 4.2 %collective-permute-start.21 = (f32[4,8,256]{2,1,0:T(8,128)}, f32[4,8,256]{2,1,0:T(8,128)S(1)}, u32[]{:S(2)}, u32[]{:S(2)}) collective-permute-start(f32[4,8,256]{2,1,0:T(8,128)} %get-tuple-element.97.refs_0_), channel_id=1, source_target_pairs={{0,2},{1,3},{2,0},{3,1},{4,6},{5,7},{6,4},{7,5},{8,10},{9,11},{10,... | collective-permute-start | bytes 98312 | tf_op jit(solution)/shard_map/ppermute | solution.py:41
  112.7 2.6 collective-permute-start.20
  145.7 10.6 %copy-start.7 = (bf16[1024,512]{1,0:T(8,128)(2,1)S(1)}, bf16[1024,512]{1,0:T(8,128)(2,1)}, u32[]{:S(2)}) copy-start(bf16[1024,512]{1,0:T(8,128)(2,1)} %get-tuple-element.100.right) | copy-start | bytes 3145732
  145.7 10.6 %copy-start.32 = (bf16[1024,512]{1,0:T(8,128)(2,1)S(1)}, bf16[1024,512]{1,0:T(8,128)(2,1)}, u32[]{:S(2)}) copy-start(bf16[1024,512]{1,0:T(8,128)(2,1)} %get-tuple-element.101) | copy-start | bytes 3145732
  154.9 4.7 %collective-permute-start.32 = (f32[32,512]{1,0:T(8,128)}, f32[32,512]{1,0:T(8,128)S(1)}, u32[]{:S(2)}, u32[]{:S(2)}) collective-permute-start(f32[32,512]{1,0:T(8,128)} %shard_map.273), channel_id=1, source_target_pairs={{0,4},{4,0},{8,12},{12,8},{16,20},{20,16},{24,28},{28,24},{1,5},{5... | collective-permute-start | bytes 196616 | tf_op jit(solution)/shard_map/ppermute | solution.py:41
  157.1 106.3 %copy-start.3 = (bf16[512,1024]{1,0:T(8,128)(2,1)}, bf16[512,1024]{1,0:T(8,128)(2,1)S(1)}, u32[]{:S(2)}) copy-start(bf16[512,1024]{1,0:T(8,128)(2,1)S(1)} %convolution_convert_fusion.1.refs_0_) | copy-start | bytes 3145732
  159.7 25.6 %collective-permute-start.35 = (f32[32,512]{1,0:T(8,128)S(1)}, f32[32,512]{1,0:T(8,128)S(1)}, u32[]{:S(2)}, u32[]{:S(2)}) collective-permute-start(f32[32,512]{1,0:T(8,128)S(1)} %add.105), channel_id=1, source_target_pairs={{0,24},{4,28},{8,16},{12,20},{16,8},{20,12},{24,0},{28,4},{1,25},{... | collective-permute-start | bytes 196616 | tf_op jit(solution)/shard_map/ppermute | solution.py:41
  162.2 24.4 %collective-permute-start.34 = (f32[32,512]{1,0:T(8,128)S(1)}, f32[32,512]{1,0:T(8,128)S(1)}, u32[]{:S(2)}, u32[]{:S(2)}) collective-permute-start(f32[32,512]{1,0:T(8,128)S(1)} %add.105), channel_id=1, source_target_pairs={{0,16},{4,20},{8,24},{12,28},{16,0},{20,4},{24,8},{28,12},{1,17},{... | collective-permute-start | bytes 196616 | tf_op jit(solution)/shard_map/ppermute | solution.py:41
  162.2 25.8 %collective-permute-start.33 = (f32[32,512]{1,0:T(8,128)S(1)}, f32[32,512]{1,0:T(8,128)S(1)}, u32[]{:S(2)}, u32[]{:S(2)}) collective-permute-start(f32[32,512]{1,0:T(8,128)S(1)} %add.105), channel_id=1, source_target_pairs={{0,8},{4,12},{8,0},{12,4},{16,24},{20,28},{24,16},{28,20},{1,9},{5... | collective-permute-start | bytes 196616 | tf_op jit(solution)/shard_map/ppermute | solution.py:41
  177.2 46.6 %copy-start.9 = (bf16[512,896]{1,0:T(8,128)(2,1)S(1)}, bf16[512,896]{1,0:T(8,128)(2,1)}, u32[]{:S(2)}) copy-start(bf16[512,896]{1,0:T(8,128)(2,1)} %get-tuple-element.123) | copy-start | bytes 2752516
  182.2 11.7 %collective-permute-start.43 = (bf16[256,512]{1,0:T(8,128)(2,1)}, bf16[256,512]{1,0:T(8,128)(2,1)S(1)}, u32[]{:S(2)}, u32[]{:S(2)}) collective-permute-start(bf16[256,512]{1,0:T(8,128)(2,1)} %get-tuple-element.136), channel_id=1, source_target_pairs={{0,8},{4,12},{8,0},{12,4},{16,24},{20,28},{24,16},{28,20},{1,9},{5... | collective-permute-start | bytes 786440 | tf_op jit(solution)/shard_map/ppermute | solution.py:41
  182.3 21.5 %collective-permute-start.44 = (bf16[256,512]{1,0:T(8,128)(2,1)}, bf16[256,512]{1,0:T(8,128)(2,1)S(1)}, u32[]{:S(2)}, u32[]{:S(2)}) collective-permute-start(bf16[256,512]{1,0:T(8,128)(2,1)} %get-tuple-element.137), channel_id=1, source_target_pairs={{0,16},{4,20},{8,24},{12,28},{16,0},{20,4},{24,8},{28,12},{1,17},{... | collective-permute-start | bytes 786440 | tf_op jit(solution)/shard_map/ppermute | solution.py:41
  185.3 20.0 %collective-permute-start.45 = (bf16[256,512]{1,0:T(8,128)(2,1)}, bf16[256,512]{1,0:T(8,128)(2,1)S(1)}, u32[]{:S(2)}, u32[]{:S(2)}) collective-permute-start(bf16[256,512]{1,0:T(8,128)(2,1)} %get-tuple-element.138), channel_id=1, source_target_pairs={{0,24},{4,28},{8,16},{12,20},{16,8},{20,12},{24,0},{28,4},{1,25},{... | collective-permute-start | bytes 786440 | tf_op jit(solution)/shard_map/ppermute | solution.py:41
  186.6 38.3 %collective-permute-start.39 = (bf16[512,512]{1,0:T(8,128)(2,1)}, bf16[512,512]{1,0:T(8,128)(2,1)}, u32[]{:S(2)}, u32[]{:S(2)}) collective-permute-start(bf16[512,512]{1,0:T(8,128)(2,1)} %get-tuple-element.133), channel_id=1, source_target_pairs={{0,4},{4,0},{8,12},{12,8},{16,20},{20,16},{24,28},{28,24},{1,5},{5... | collective-permute-start | bytes 1572872 | tf_op jit(solution)/shard_map/ppermute | solution.py:41
  188.0 75.4 %collective-permute-start.23 = (bf16[512,1024]{1,0:T(8,128)(2,1)}, bf16[512,1024]{1,0:T(8,128)(2,1)S(1)}, u32[]{:S(2)}, u32[]{:S(2)}) collective-permute-start(bf16[512,1024]{1,0:T(8,128)(2,1)} %convolution_convert_fusion), channel_id=1, source_target_pairs={{0,1},{1,0},{2,3},{3,2},{4,5},{5,4},{6,7},{7,6},{8,9},{9,8},{10,11... | collective-permute-start | bytes 3145736 | tf_op jit(solution)/shard_map/ppermute | solution.py:41
  193.9 29.8 %collective-permute-start.27 = (bf16[256,896]{1,0:T(8,128)(2,1)}, bf16[256,896]{1,0:T(8,128)(2,1)}, u32[]{:S(2)}, u32[]{:S(2)}) collective-permute-start(bf16[256,896]{1,0:T(8,128)(2,1)} %get-tuple-element.124), channel_id=1, source_target_pairs={{0,4},{4,0},{8,12},{12,8},{16,20},{20,16},{24,28},{28,24},{1,5},{5... | collective-permute-start | bytes 1376264 | tf_op jit(solution)/shard_map/ppermute | solution.py:41
  203.9 21.1 %collective-permute-start.30 = (bf16[256,896]{1,0:T(8,128)(2,1)}, bf16[256,896]{1,0:T(8,128)(2,1)}, u32[]{:S(2)}, u32[]{:S(2)}) collective-permute-start(bf16[256,896]{1,0:T(8,128)(2,1)} %get-tuple-element.125), channel_id=1, source_target_pairs={{0,4},{4,0},{8,12},{12,8},{16,20},{20,16},{24,28},{28,24},{1,5},{5... | collective-permute-start | bytes 1376264 | tf_op jit(solution)/shard_map/ppermute | solution.py:41
  206.3 14.8 %collective-permute-start.46 = (bf16[128,512]{1,0:T(8,128)(2,1)S(1)}, bf16[128,512]{1,0:T(8,128)(2,1)S(1)}, u32[]{:S(2)}, u32[]{:S(2)}) collective-permute-start(bf16[128,512]{1,0:T(8,128)(2,1)S(1)} %add_convert_fusion.5), channel_id=1, source_target_pairs={{0,4},{4,0},{8,12},{12,8},{16,20},{20,16},{24,28},{28,24},{1,5},{5... | collective-permute-start | bytes 393224 | tf_op jit(solution)/shard_map/ppermute | solution.py:41
  221.7 42.3 %collective-permute-start.25 = (bf16[512,1024]{1,0:T(8,128)(2,1)}, bf16[512,1024]{1,0:T(8,128)(2,1)}, u32[]{:S(2)}, u32[]{:S(2)}) collective-permute-start(bf16[512,1024]{1,0:T(8,128)(2,1)} %get-tuple-element.122), channel_id=1, source_target_pairs={{0,1},{1,0},{2,3},{3,2},{4,5},{5,4},{6,7},{7,6},{8,9},{9,8},{10,11... | collective-permute-start | bytes 3145736 | tf_op jit(solution)/shard_map/ppermute | solution.py:41
  226.2 32.9 %copy-start.26 = (f32[16,256]{1,0:T(8,128)S(1)}, f32[16,256]{1,0:T(8,128)}, u32[]{:S(2)}) copy-start(f32[16,256]{1,0:T(8,128)} %get-tuple-element.169) | copy-start | bytes 49156
  226.3 8.3 %collective-permute-start.40 = (bf16[128,512]{1,0:T(8,128)(2,1)S(1)}, bf16[128,512]{1,0:T(8,128)(2,1)S(1)}, u32[]{:S(2)}, u32[]{:S(2)}) collective-permute-start(bf16[128,512]{1,0:T(8,128)(2,1)S(1)} %get-tuple-element.156), channel_id=1, source_target_pairs={{0,24},{4,28},{8,16},{12,20},{16,8},{20,12},{24,0},{28,4},{1,25},{... | collective-permute-start | bytes 393224 | tf_op jit(solution)/shard_map/ppermute | solution.py:41
  228.9 10.8 %collective-permute-start.42 = (bf16[128,512]{1,0:T(8,128)(2,1)S(1)}, bf16[128,512]{1,0:T(8,128)(2,1)S(1)}, u32[]{:S(2)}, u32[]{:S(2)}) collective-permute-start(bf16[128,512]{1,0:T(8,128)(2,1)S(1)} %get-tuple-element.157), channel_id=1, source_target_pairs={{0,8},{4,12},{8,0},{12,4},{16,24},{20,28},{24,16},{28,20},{1,9},{5... | collective-permute-start | bytes 393224 | tf_op jit(solution)/shard_map/ppermute | solution.py:41
  228.9 20.5 %collective-permute-start.41 = (bf16[128,512]{1,0:T(8,128)(2,1)S(1)}, bf16[128,512]{1,0:T(8,128)(2,1)S(1)}, u32[]{:S(2)}, u32[]{:S(2)}) collective-permute-start(bf16[128,512]{1,0:T(8,128)(2,1)S(1)} %get-tuple-element.158), channel_id=1, source_target_pairs={{0,16},{4,20},{8,24},{12,28},{16,0},{20,4},{24,8},{28,12},{1,17},{... | collective-permute-start | bytes 393224 | tf_op jit(solution)/shard_map/ppermute | solution.py:41
  234.6 20.0 %collective-permute-start.29 = (bf16[128,896]{1,0:T(8,128)(2,1)S(1)}, bf16[128,896]{1,0:T(8,128)(2,1)S(1)}, u32[]{:S(2)}, u32[]{:S(2)}) collective-permute-start(bf16[128,896]{1,0:T(8,128)(2,1)S(1)} %get-tuple-element.154), channel_id=1, source_target_pairs={{0,16},{4,20},{8,24},{12,28},{16,0},{20,4},{24,8},{28,12},{1,17},{... | collective-permute-start | bytes 688136 | tf_op jit(solution)/shard_map/ppermute | solution.py:41
  239.7 14.9 %collective-permute-start.28 = (bf16[128,896]{1,0:T(8,128)(2,1)S(1)}, bf16[128,896]{1,0:T(8,128)(2,1)S(1)}, u32[]{:S(2)}, u32[]{:S(2)}) collective-permute-start(bf16[128,896]{1,0:T(8,128)(2,1)S(1)} %get-tuple-element.155), channel_id=1, source_target_pairs={{0,24},{4,28},{8,16},{12,20},{16,8},{20,12},{24,0},{28,4},{1,25},{... | collective-permute-start | bytes 688136 | tf_op jit(solution)/shard_map/ppermute | solution.py:41
  249.3 8.6 %collective-permute-start.31 = (bf16[128,896]{1,0:T(8,128)(2,1)S(1)}, bf16[128,896]{1,0:T(8,128)(2,1)S(1)}, u32[]{:S(2)}, u32[]{:S(2)}) collective-permute-start(bf16[128,896]{1,0:T(8,128)(2,1)S(1)} %add_convert_fusion.2), channel_id=1, source_target_pairs={{0,8},{4,12},{8,0},{12,4},{16,24},{20,28},{24,16},{28,20},{1,9},{5... | collective-permute-start | bytes 688136 | tf_op jit(solution)/shard_map/ppermute | solution.py:41
  259.2 7.8 %collective-permute-start.37 = (f32[160,256]{1,0:T(8,128)S(1)}, f32[160,256]{1,0:T(8,128)S(1)}, u32[]{:S(2)}, u32[]{:S(2)}) collective-permute-start(f32[160,256]{1,0:T(8,128)S(1)} %pad_maximum_fusion.2), channel_id=1, source_target_pairs={{0,2},{1,3},{2,0},{3,1},{4,6},{5,7},{6,4},{7,5},{8,10},{9,11},{10,... | collective-permute-start | bytes 491528 | tf_op jit(solution)/shard_map/ppermute | solution.py:41
  259.7 7.3 %collective-permute-start.38 = (f32[160,256]{1,0:T(8,128)S(1)}, f32[160,256]{1,0:T(8,128)S(1)}, u32[]{:S(2)}, u32[]{:S(2)}) collective-permute-start(f32[160,256]{1,0:T(8,128)S(1)} %pad_maximum_fusion.2), channel_id=1, source_target_pairs={{0,3},{1,2},{2,1},{3,0},{4,7},{5,6},{6,5},{7,4},{8,11},{9,10},{10,... | collective-permute-start | bytes 491528 | tf_op jit(solution)/shard_map/ppermute | solution.py:41
  259.7 7.3 %collective-permute-start.36 = (f32[160,256]{1,0:T(8,128)S(1)}, f32[160,256]{1,0:T(8,128)}, u32[]{:S(2)}, u32[]{:S(2)}) collective-permute-start(f32[160,256]{1,0:T(8,128)S(1)} %pad_maximum_fusion.2), channel_id=1, source_target_pairs={{0,1},{1,0},{2,3},{3,2},{4,5},{5,4},{6,7},{7,6},{8,9},{9,8},{10,11... | collective-permute-start | bytes 491528 | tf_op jit(solution)/shard_map/ppermute | solution.py:41
  263.3 6.4 %copy-start.4 = (bf16[512,1024]{1,0:T(8,128)(2,1)}, bf16[512,1024]{1,0:T(8,128)(2,1)S(1)}, u32[]{:S(2)}) copy-start(bf16[512,1024]{1,0:T(8,128)(2,1)S(1)} %collective-permute-done.23.refs_2_) | copy-start | bytes 3145732
  263.5 17.3 %collective-permute-start.24 = (bf16[256,1024]{1,0:T(8,128)(2,1)S(1)}, bf16[256,1024]{1,0:T(8,128)(2,1)S(1)}, u32[]{:S(2)}, u32[]{:S(2)}) collective-permute-start(bf16[256,1024]{1,0:T(8,128)(2,1)S(1)} %add_convert_fusion.1), channel_id=1, source_target_pairs={{0,2},{1,3},{2,0},{3,1},{4,6},{5,7},{6,4},{7,5},{8,10},{9,11},{10,... | collective-permute-start | bytes 1572872 | tf_op jit(solution)/shard_map/ppermute | solution.py:41
  265.3 25.1 %collective-permute-start.26 = (bf16[256,1024]{1,0:T(8,128)(2,1)S(1)}, bf16[256,1024]{1,0:T(8,128)(2,1)S(1)}, u32[]{:S(2)}, u32[]{:S(2)}) collective-permute-start(bf16[256,1024]{1,0:T(8,128)(2,1)S(1)} %add_convert_fusion), channel_id=1, source_target_pairs={{0,2},{1,3},{2,0},{3,1},{4,6},{5,7},{6,4},{7,5},{8,10},{9,11},{10,... | collective-permute-start | bytes 1572872 | tf_op jit(solution)/shard_map/ppermute | solution.py:41
  (16 other events, 22.2 us)

commit v4 on v3

--- a/solution.py
+++ b/solution.py
@@ -107,15 +107,6 @@
         got.append(swap(pairs[i], axis, 2 * i))
     other = sum(both[rows:].astype(f32) for both in got).astype(bf16)
     return [(both, 0) for both in got] + [(swap(other, axis, 1), 0)]
-
-
-def block_of(term, rows):
-    array, index = term
-    return array[index * rows : (index + 1) * rows].astype(f32)
-
-
-def total_of(terms):
-    return sum(term.astype(f32) for term in terms)
 
 
 def direct_terms(value, axis):
@@ -543,15 +534,41 @@
     grad_gain[...] = jnp.broadcast_to(jnp.sum(total, axis=0, keepdims=True), grad_gain.shape)
 
 
-def product_kernel(bounds):
-    def kernel(place, left, right, *outs):
-        at = pl.program_id(0)
-        value = mm(left[...], right[...], TN).astype(bf16)
-        for i, out in enumerate(outs):
-
-            @pl.when((at >= bounds[i]) & (at < bounds[i + 1]))
-            def _(out=out):
-                out[...] = value
+def weights_kernel(counts, inner, twice):
+    def kernel(place, *refs):
+        groups = []
+        for count in counts:
+            groups.append(refs[:count])
+            refs = refs[count:]
+        grad_zx, grad_out, grad_dt, grad_bc = refs
+
+        def total(terms):
+            return sum(term[...].astype(f32) for term in terms)
+
+        scan, gate, out = (total(group) for group in groups)
+        grad_zx[:, 0, :] = gate
+        grad_zx[:, 1, :] = scan[:, :inner]
+        grad_out[...] = out.T
+        grad_bc[...] = scan[:, inner : inner + twice]
+        grad_dt[...] = scan[:, inner + twice : inner + twice + grad_dt.shape[1]]
+
+    return kernel
+
+
+def shared_kernel(count, rows, cols):
+    def kernel(place, *refs):
+        grad_w, of_conv, of_pre = refs[count:]
+        total = refs[0][...]
+        for term in refs[1:count]:
+            total = total + term[...]
+        share, twice = grad_w.shape
+        grad_w[...] = total[:share]
+        of_conv[...] = total[share : share + 8]
+        for r in range(of_pre.shape[1] // cols):
+            for k in range(cols // twice):
+                at = share + k * rows + 8 + r
+                start = r * cols + k * twice
+                of_pre[:, start : start + twice] = total[at : at + 1]
 
     return kernel
 
@@ -759,35 +776,18 @@
     )(place_tensor, *sum_terms, gate_raw, grad_scaled, mixed, gain)
 
     share = model // dp
-    wide_share = share * min(2, dp)
-    steps = model // wide_share
-
-    def products(left, right, bounds):
-        cols = right.shape[1]
-
-        def piece(i):
-            count = bounds[i + 1] - bounds[i]
-            return pl.BlockSpec(
-                (wide_share, cols),
-                lambda c, place: (jnp.clip(c - bounds[i], 0, count - 1), 0),
-            )
-
-        return call(
-            product_kernel(bounds), steps,
-            [pl.BlockSpec((length, wide_share), lambda c, place: (0, c)), whole(right.shape)],
-            [piece(i) for i in range(len(bounds) - 1)],
-            [
-                (((high - low) * wide_share, cols), bf16)
-                for low, high in zip(bounds, bounds[1:])
-            ],
-        )(place_tensor, left, right)
-
-    middle = (steps + 1) // 2
-    out_pairs = products(upstream, scaled, list(range(steps + 1)))
-    gate_own, *gate_near = products(normed, d_gate, sorted({0, middle, steps}))
+
+    def tn(left, right):
+        return lax.dot_general(left, right, TN, preferred_element_type=f32).astype(bf16)
+
+    out_part = lax.optimization_barrier(tn(upstream, scaled))
+    out_pairs = [out_part[k * share : (k + 2) * share] for k in range(0, dp, 2)]
+    even = share * ((dp + 1) // 2)
+    gate_part = lax.optimization_barrier(tn(normed, d_gate))
+    gate_own, gate_near = gate_part[:even], [gate_part[even:]]
     stay = rows_local * ((tensor + 1) // 2)
-    branch_near = mm(scaled[stay:], full_out, NT).astype(bf16)
-    branch_own = mm(scaled[:stay], full_out, NT).astype(bf16)
+    branch_part = lax.optimization_barrier(mm(scaled, full_out, NT).astype(bf16))
+    branch_own, branch_near = branch_part[:stay], branch_part[stay:]
     out_terms = far_first(out_pairs, DP)
     gate_terms = near_first(gate_own, gate_near, DP)
     branch_terms = near_first(branch_own, [branch_near], TP)
@@ -831,9 +831,12 @@
     columns = columns[0]
     grad_x, grad_bc, grad_head = carry[:3]
 
-    later = (middle + steps) // 2
-    scan_own, *scan_near = products(normed, columns, sorted({0, middle, later, steps}))
-    scan_terms = near_first(scan_own, scan_near[::-1], DP)
+    later = even + (model - even) // 2 if dp % 4 == 0 else even
+    scan_near = [tn(normed[:, later:], columns)]
+    if later > even:
+        scan_near.append(tn(normed[:, even:later], columns))
+    scan_own = tn(normed[:, :even], columns)
+    scan_terms = near_first(scan_own, scan_near, DP)
     features = model // 4
     leave = max(length - stay, rows_local)
     normed_own, normed_near, pre_part = call(
@@ -860,9 +863,19 @@
         [out_block], [((rows_local, 1, model), f32)], [pltpu.VMEM((slab, model), f32)],
     )(place_entry, tokens_local, upstream_local, gain_in, *[array for array, _ in normed_terms])
 
-    grad_w_scan = sum(block_of(term, share) for term in scan_terms)
-    grad_w_out = sum(block_of(term, share) for term in out_terms).T
-    grad_w_gate = sum(block_of(term, share) for term in gate_terms)
+    groups = (scan_terms, gate_terms, out_terms)
+    grad_w_zx, grad_w_out, grad_w_dt, grad_bc_part = call(
+        weights_kernel([len(terms) for terms in groups], inner, twice), 1,
+        [
+            pl.BlockSpec((share, array.shape[1]), lambda c, place, k=k: (k, 0))
+            for terms in groups for array, k in terms
+        ],
+        [whole((share, 2, inner)), whole((inner, share)), whole((share, heads)), whole((share, twice))],
+        [
+            ((share, 2, inner), f32), ((inner, share), f32), ((share, heads), f32),
+            ((share, twice), f32),
+        ],
+    )(place_entry, *[array for terms in groups for array, _ in terms])
     cols = max(inner, twice + LANES)
     cols += -cols % 512
     if narrow:
@@ -881,23 +894,20 @@
     assert cols % twice == 0 and model % cols == 0
     across = [small[16:, k : k + twice] for k in range(0, cols, twice)]
     across = jnp.concatenate(across, axis=0)
-    keys_rows = grad_w_scan.shape[0]
-    across = jnp.concatenate([grad_w_scan[:, inner : inner + twice], across], axis=0)
-    across = total_of(direct_terms(across, TP))
-    grad_w_bc = across[:keys_rows]
-    of_bc = across[keys_rows:]
-    count = rows - 16
-    pre_rows = [of_bc[k * count + 8 : k * count + 8 + model // cols] for k in range(cols // twice)]
-    sum_pre = jnp.concatenate(pre_rows, axis=1).reshape(-1)
-    grad_w_dt = grad_w_scan[:, inner + twice : inner + twice + heads]
-    grad_w_zx = jnp.stack([grad_w_gate, grad_w_scan[:, :inner]], axis=1)
+    across = direct_terms(jnp.concatenate([grad_bc_part, across], axis=0), TP)
+    grad_w_bc, of_bc, sum_pre = call(
+        shared_kernel(tensor, rows - 16, cols), 1,
+        [whole(across[0].shape)] * tensor,
+        [whole((share, twice)), whole((8, twice)), whole((1, model))],
+        [((share, twice), f32), ((8, twice), f32), ((1, model), f32)],
+    )(place_entry, *across)
     of_x = small[:8, :inner]
     sum_gain = small[8, :inner]
     of_head = small[16:24, twice : twice + LANES]
     return (
         block_output,
         input_grad,
-        sum_pre,
+        sum_pre.reshape(model),
         grad_w_zx,
         grad_w_dt,
         grad_w_bc,

time: 296 us -> 300 us (1.014)
  Pallas kernels: 93.9 us -> 82.5 us
  matrix products: 2.45 us -> 11.9 us
  other arithmetic: 17.2 us -> 11.9 us
  starting transfers between devices: 62.8 us -> 67.7 us
  waiting for transfers between devices: 100 us -> 103 us
    pallas_call x3 -> x2, Pallas kernels: 16.4 us -> 4.81 us  [the longest x1 2.98 us: per_device(): call(weights_kernel([len(terms) for terms in groups], inner, twice), 1, [...]
    dot_general x0 -> x5, matrix products: none -> 10.6 us  [tn(): lax.dot_general(left, right, TN, preferred_element_type=f32).astype(bf16)]
    ppermute x47, starting transfers between devices: 62.8 us -> 67.7 us  [swap(): return lax.ppermute(value, axis, [(i, i ^ bits) for i in range(size)])]
    ppermute x47, waiting for transfers between devices: 100 us -> 103 us  [swap(): return lax.ppermute(value, axis, [(i, i ^ bits) for i in range(size)])]
    unnamed x74 -> x111, local copies, waits for them, and re-layouts: 8.2 us -> 8.6 us
  transfers between devices with their start and end apart: 47 -> 47, of which waited for: 19 -> 18; matrix products, arithmetic and copies ran while one was open for 8% -> 6% of each run, Pallas kernels for 14% -> 14%
where the time goes in v4:
time: 300 us; the launch traced here: 299 us
  waiting for transfers between devices  103 us (34%)
  Pallas kernels  82.5 us (28%)
  starting transfers between devices  67.7 us (23%)
  local copies, waits for them, and re-layouts  20.1 us (7%)
  other arithmetic  11.9 us (4%)
  matrix products  11.9 us (4%)
    ppermute x47, waiting for transfers between devices, swap(): return lax.ppermute(value, axis, [(i, i ^ bits) for i in range(size)])  103 us
    ppermute x47, starting transfers between devices, swap(): return lax.ppermute(value, axis, [(i, i ^ bits) for i in range(size)])  67.7 us
    pallas_call x2, Pallas kernels, per_device(): call(backward_kernel(width, head_dim, len(columns)), span, [back(cols, st...  23.6 us
    pallas_call x2, Pallas kernels, per_device(): call(forward_kernel(width, head_dim, tensor, len(weights), per, start), s...  20.2 us
    dot_general x5, matrix products, tn(): lax.dot_general(left, right, TN, preferred_element_type=f32).astype(bf16)  10.6 us
    pallas_call x1, Pallas kernels, per_device(): call(gate_kernel(tensor, dp, parts), length // block, [gate_piece(p) for...  9.01 us
    unnamed x111, local copies, waits for them, and re-layouts  8.6 us
    pallas_call x1, Pallas kernels, per_device(): call(normed_kernel, 4, [pl.BlockSpec((length, features), lambda c, place:...  7.65 us
  transfers between devices with their start and end apart: 47, of which 18 were waited for; matrix products, arithmetic and copies ran while one was open for 6% of the time, Pallas kernels for 14%

profile of v4, /device:TPU:0, one launch (start us, length us, event | category | flops | bytes accessed | tf_op | source)
XLA Modules:
  0.0 298.7 jit_solution(15683344756291638486)
XLA Ops:
  3.5 1.5 fusion.6
  5.1 1.3 select_maximum_fusion.2.refs_14_.refs_7_.refs_10_
  6.4 1.3 select_maximum_fusion.1.refs_13_.refs_6_.refs_9_
  7.7 1.3 select_maximum_fusion.refs_12_.refs_5_.refs_8_
  9.9 3.0 %collective-permute-start.16 = (bf16[128,896]{1,0:T(8,128)(2,1)S(1)}, bf16[128,896]{1,0:T(8,128)(2,1)S(1)}, u32[]{:S(2)}, u32[]{:S(2)}) collective-permute-start(bf16[128,896]{1,0:T(8,128)(2,1)S(1)} %maximum_maximum_fusion.refs_4_), channel_id=1, source_target_pairs={{0,4},{4,0},{8,12},{12,8},{16,20},{20,16},{24,28},{28,24},{1,5},{5... | collective-permute-start | bytes 688136 | tf_op jit(solution)/shard_map/ppermute | solution.py:41
  12.9 3.6 %collective-permute-start.15 = (bf16[128,896]{1,0:T(8,128)(2,1)S(1)}, bf16[128,896]{1,0:T(8,128)(2,1)S(1)}, u32[]{:S(2)}, u32[]{:S(2)}) collective-permute-start(bf16[128,896]{1,0:T(8,128)(2,1)S(1)} %maximum_maximum_fusion.refs_4_), channel_id=1, source_target_pairs={{0,24},{4,28},{8,16},{12,20},{16,8},{20,12},{24,0},{28,4},{1,25},{... | collective-permute-start | bytes 688136 | tf_op jit(solution)/shard_map/ppermute | solution.py:41
  16.6 2.5 shard_map.262
  19.1 1.5 collective-permute-start
  20.8 2.0 collective-permute-start.11
  22.8 1.6 collective-permute-start.13
  24.3 15.1 %collective-permute-start.9 = (bf16[128,1024]{1,0:T(8,128)(2,1)S(1)}, bf16[128,1024]{1,0:T(8,128)(2,1)}, u32[]{:S(2)}, u32[]{:S(2)}) collective-permute-start(bf16[128,1024]{1,0:T(8,128)(2,1)S(1)} %pad_maximum_fusion.refs_8_), channel_id=1, source_target_pairs={{0,16},{4,20},{8,24},{12,28},{16,0},{20,4},{24,8},{28,12},{1,17},{... | collective-permute-start | bytes 786440 | tf_op jit(solution)/shard_map/ppermute | solution.py:41
  39.5 8.5 %collective-permute-done.14.refs_6_ = bf16[128,896]{1,0:T(8,128)(2,1)S(1)} collective-permute-done((bf16[128,896]{1,0:T(8,128)(2,1)S(1)}, bf16[128,896]{1,0:T(8,128)(2,1)S(1)}, u32[]{:S(2)}, u32[]{:S(2)}) %collective-permute-start.14) | collective-permute-done | bytes 229408 | tf_op jit(solution)/shard_map/ppermute | solution.py:41
  48.0 1.5 collective-permute-start.3
  50.2 8.2 %collective-permute-done.9.refs_12_ = bf16[128,1024]{1,0:T(8,128)(2,1)} collective-permute-done((bf16[128,1024]{1,0:T(8,128)(2,1)S(1)}, bf16[128,1024]{1,0:T(8,128)(2,1)}, u32[]{:S(2)}, u32[]{:S(2)}) %collective-permute-start.9) | collective-permute-done | bytes 262176 | tf_op jit(solution)/shard_map/ppermute | solution.py:41
  59.0 2.4 collective-permute-done.7.refs_10_
  61.9 1.5 collective-permute-start.18
  63.4 5.7 %collective-permute-done.19.refs_11_ = bf16[128,896]{1,0:T(8,128)(2,1)S(1)} collective-permute-done((bf16[128,896]{1,0:T(8,128)(2,1)S(1)}, bf16[128,896]{1,0:T(8,128)(2,1)S(1)}, u32[]{:S(2)}, u32[]{:S(2)}) %collective-permute-start.19) | collective-permute-done | bytes 229408 | tf_op jit(solution)/shard_map/ppermute | solution.py:41
  69.6 1.9 collective-permute-done.18.refs_10_
  72.1 5.9 %collective-permute-done.17.refs_9_ = bf16[128,896]{1,0:T(8,128)(2,1)S(1)} collective-permute-done((bf16[128,896]{1,0:T(8,128)(2,1)S(1)}, bf16[128,896]{1,0:T(8,128)(2,1)S(1)}, u32[]{:S(2)}, u32[]{:S(2)}) %collective-permute-start.17) | collective-permute-done | bytes 229408 | tf_op jit(solution)/shard_map/ppermute | solution.py:41
  78.5 1.5 collective-permute-start.10
  80.8 12.0 %shard_map.263 = (f32[1024,512]{1,0:T(8,128)}, f32[1024,256]{1,0:T(8,128)}, bf16[1024,512]{1,0:T(8,128)(2,1)}, bf16[1024,256]{1,0:T(8,128)(2,1)}, f32[1024,128]{...) custom-call(s32[1]{0:T(128)} %bitcast.2.place, ...), custom_call_target="tpu_custom_call" | custom-call | tf_op jit(solution)/shard_map/pallas_call | solution.py:705
  92.8 8.3 %shard_map.264 = (f32[1024,512]{1,0:T(8,128)}, f32[1024,256]{1,0:T(8,128)}, bf16[1024,512]{1,0:T(8,128)(2,1)}, bf16[1024,256]{1,0:T(8,128)(2,1)}, f32[1024,128]{...) custom-call(s32[1]{0:T(128)} %bitcast.2.place, ...), custom_call_target="tpu_custom_call", output_to_operand_aliasing={{0}: (13, {}), {1}: (14, {}), {2}: (15, {}), {3}: (16, {}),... | custom-call | tf_op jit(solution)/shard_map/pallas_call | solution.py:705
  102.0 9.0 %shard_map.265 = (f32[1024,512]{1,0:T(8,128)}, f32[1024,512]{1,0:T(8,128)}, f32[4,8,256]{2,1,0:T(8,128)}, bf16[1024,1024]{1,0:T(8,128)(2,1)}, bf16[1024,1024]{1,...) custom-call(s32[1]{0:T(128)} %bitcast.2.place, bf16[256,1024]{1,0:T(8,128)(2,1)} %get-tuple-element.75.refs_0_, ...), custom_call_target="tpu_custom_call" | custom-call | tf_op jit(solution)/shard_map/pallas_call | solution.py:745
  111.1 1.7 collective-permute-start.21
  112.9 1.9 collective-permute-done.22.refs_3_
  115.9 6.4 %shard_map.266 = (bf16[1024,512]{1,0:T(8,128)(2,1)}, f32[1024,512]{1,0:T(8,128)}, bf16[1024,512]{1,0:T(8,128)(2,1)}, f32[8,512]{1,0:T(8,128)}) custom-call(s32[1]{0:T(128)} %bitcast.2.place, f32[4,8,256]{2,1,0:T(8,128)} %get-tuple-element.95.refs_0_, f32[4,8,256]{2,1,0:T(8,128)} %copy-done.49, f32[4,8,256]{2,1,0:T(8,128)} %copy-done.48, ...), custom_call_target="tpu_custom_call" | custom-call | tf_op jit(solution)/shard_map/pallas_call | solution.py:767
  122.3 11.6 %shard_map.268 = (bf16[1024,896]{1,0:T(8,128)(2,1)}, f32[8,512]{1,0:T(8,128)}, f32[8,256]{1,0:T(8,128)}, f32[8,128]{1,0:T(8,128)}, f32[128,512]{1,0:T(8,128)}, /...) custom-call(s32[1]{0:T(128)} %bitcast.2.place, f32[1024,512]{1,0:T(8,128)} %get-tuple-element.102.refs_0_, ...), custom_call_target="tpu_custom_call" | custom-call | tf_op jit(solution)/shard_map/pallas_call | solution.py:815
  133.9 12.0 %shard_map.269 = (bf16[1024,896]{1,0:T(8,128)(2,1)}, f32[8,512]{1,0:T(8,128)}, f32[8,256]{1,0:T(8,128)}, f32[8,128]{1,0:T(8,128)}, f32[128,512]{1,0:T(8,128)}, /...) custom-call(s32[1]{0:T(128)} %bitcast.2.place, ...), custom_call_target="tpu_custom_call", output_to_operand_aliasing={{0}: (20, {})} | custom-call | tf_op jit(solution)/shard_map/pallas_call | solution.py:815
  145.9 3.1 %convolution_convert_fusion.5 = bf16[256,896]{1,0:T(8,128)(2,1)} fusion(bf16[1024,896]{1,0:T(8,128)(2,1)} %get-tuple-element.117.columns, bf16[1024,1024]{1,0:T(8,128)(2,1)S(1)} %copy-done.5), kind=kOutput, calls=%fused_computation.5 | convolution fusion | flops 469991424 | bytes 2818048 | tf_op jit(solution)/shard_map/dot_general | solution.py:781
  149.1 1.3 convolution_convert_fusion.3.refs_0_
  150.9 1.3 convolution_convert_fusion.1
  152.3 1.3 convolution_convert_fusion
  153.9 2.3 convolution_convert_fusion.2
  157.1 2.4 collective-permute-start.38
  159.5 1.6 fusion.3
  161.1 7.7 %shard_map.270 = (bf16[512,1024]{1,0:T(8,128)(2,1)}, bf16[512,1024]{1,0:T(8,128)(2,1)}, f32[8,1024]{1,0:T(8,128)}) custom-call(s32[1]{0:T(128)} %bitcast.2.place, bf16[1024,1024]{1,0:T(8,128)(2,1)} %get-tuple-element.100.tokens, bf16[1024,512]{1,0:T(8,128)(2,1)} %get-tuple-element.101.d_gate, bf16[1024,896]{1,0:T(8,128)(2,1)} %get-tuple-element.117.columns, ...), custom_call_target="tpu_custom_call" | custom-call | tf_op jit(solution)/shard_map/pallas_call | solution.py:842
  168.8 1.5 shard_map.273
  170.3 1.4 collective-permute-start.40
  171.6 2.6 convolution_convert_fusion.4
  174.8 1.5 collective-permute-start.43
  176.3 2.0 collective-permute-start.42
  180.1 1.6 collective-permute-done.43
  181.7 5.3 %collective-permute-start.36 = (bf16[256,512]{1,0:T(8,128)(2,1)}, bf16[256,512]{1,0:T(8,128)(2,1)}, u32[]{:S(2)}, u32[]{:S(2)}) collective-permute-start(bf16[256,512]{1,0:T(8,128)(2,1)} %get-tuple-element.159), channel_id=1, source_target_pairs={{0,8},{4,12},{8,0},{12,4},{16,24},{20,28},{24,16},{28,20},{1,9},{5... | collective-permute-start | bytes 786440 | tf_op jit(solution)/shard_map/ppermute | solution.py:41
  187.4 1.4 collective-permute-start.27
  191.4 1.4 collective-permute-start.30
  194.2 6.9 %collective-permute-done.27 = bf16[256,896]{1,0:T(8,128)(2,1)} collective-permute-done((bf16[256,896]{1,0:T(8,128)(2,1)}, bf16[256,896]{1,0:T(8,128)(2,1)}, u32[]{:S(2)}, u32[]{:S(2)}) %collective-permute-start.27) | collective-permute-done | bytes 458784 | tf_op jit(solution)/shard_map/ppermute | solution.py:41
  201.1 1.4 collective-permute-start.39
  203.6 18.4 %collective-permute-done.30.refs_4_ = bf16[256,896]{1,0:T(8,128)(2,1)S(1)} collective-permute-done((bf16[256,896]{1,0:T(8,128)(2,1)S(1)}, bf16[256,896]{1,0:T(8,128)(2,1)S(1)}, u32[]{:S(2)}, u32[]{:S(2)}) %collective-permute-start.30) | collective-permute-done | bytes 458784 | tf_op jit(solution)/shard_map/ppermute | solution.py:41
  222.7 1.7 collective-permute-start.28
  225.6 1.3 collective-permute-start.35
  229.1 2.0 collective-permute-start.34
  231.1 10.0 %collective-permute-done.35.refs_8_ = bf16[128,512]{1,0:T(8,128)(2,1)S(1)} collective-permute-done((bf16[128,512]{1,0:T(8,128)(2,1)S(1)}, bf16[128,512]{1,0:T(8,128)(2,1)S(1)}, u32[]{:S(2)}, u32[]{:S(2)}) %collective-permute-start.35) | collective-permute-done | bytes 131104 | tf_op jit(solution)/shard_map/ppermute | solution.py:41
  241.1 1.7 collective-permute-start.33
  243.1 9.5 %collective-permute-done.34.refs_7_ = bf16[128,512]{1,0:T(8,128)(2,1)S(1)} collective-permute-done((bf16[128,512]{1,0:T(8,128)(2,1)S(1)}, bf16[128,512]{1,0:T(8,128)(2,1)S(1)}, u32[]{:S(2)}, u32[]{:S(2)}) %collective-permute-start.34) | collective-permute-done | bytes 131104 | tf_op jit(solution)/shard_map/ppermute | solution.py:41
  255.3 3.0 shard_map.272
  261.2 1.3 slice_bitcast_fusion
  262.4 1.5 copy.42
  263.9 16.8 %collective-permute-done.46.refs_3_ = f32[160,256]{1,0:T(8,128)S(1)} collective-permute-done((f32[160,256]{1,0:T(8,128)S(1)}, f32[160,256]{1,0:T(8,128)S(1)}, u32[]{:S(2)}, u32[]{:S(2)}) %collective-permute-start.46) | collective-permute-done | bytes 163872 | tf_op jit(solution)/shard_map/ppermute | solution.py:41
  280.7 3.9 %collective-permute-done.45.refs_2_ = f32[160,256]{1,0:T(8,128)S(1)} collective-permute-done((f32[160,256]{1,0:T(8,128)S(1)}, f32[160,256]{1,0:T(8,128)S(1)}, u32[]{:S(2)}, u32[]{:S(2)}) %collective-permute-start.45) | collective-permute-done | bytes 163872 | tf_op jit(solution)/shard_map/ppermute | solution.py:41
  285.9 1.8 shard_map.274
  287.7 1.3 slice.179
  289.0 1.3 slice.178
  291.1 3.6 %shard_map.271 = f32[256,1,1024]{2,1,0:T(1,128)} custom-call(s32[1]{0:T(128)} %bitcast.place, bf16[256,1024]{1,0:T(8,128)(2,1)} %bitcast.36, bf16[256,1024]{1,0:T(8,128)(2,1)} %bitcast.39, f32[1,1024]{1,0:T(1,128)} %bitcast.45, bf16[512,1024]{1,0:T(8,128)(2,1)} %get-tuple-element.119.refs_0_, bf16[256,1024]{1,0:T(8,128)(2,1)} %copy-done.24, ...), custom_call_target="tpu_custom_call" | custom-call | tf_op jit(solution)/shard_map/pallas_call | solution.py:859
  295.5 3.2 %shard_map.267 = f32[256,1,1024]{2,1,0:T(1,128)} custom-call(s32[1]{0:T(128)} %bitcast.place, bf16[256,1024]{1,0:T(8,128)(2,1)} %bitcast.37, bf16[512,1024]{1,0:T(8,128)(2,1)} %get-tuple-element.151.refs_0_, bf16[256,1024]{1,0:T(8,128)(2,1)} %copy-done.23, bf16[512,1024]{1,0:T(8,128)(2,1)} %copy-done.8), custom_call_target="tpu_custom_call" | custom-call | tf_op jit(solution)/shard_map/pallas_call | solution.py:804
  (191 shorter events, 32.6 us)
Async XLA Ops:
  9.9 70.7 %copy-start.17 = (bf16[128,896]{1,0:T(8,128)(2,1)}, bf16[128,896]{1,0:T(8,128)(2,1)S(1)}, u32[]{:S(2)}) copy-start(bf16[128,896]{1,0:T(8,128)(2,1)S(1)} %maximum_maximum_fusion.refs_4_) | copy-start | bytes 688132
  9.9 12.8 %collective-permute-start.16 = (bf16[128,896]{1,0:T(8,128)(2,1)S(1)}, bf16[128,896]{1,0:T(8,128)(2,1)S(1)}, u32[]{:S(2)}, u32[]{:S(2)}) collective-permute-start(bf16[128,896]{1,0:T(8,128)(2,1)S(1)} %maximum_maximum_fusion.refs_4_), channel_id=1, source_target_pairs={{0,4},{4,0},{8,12},{12,8},{16,20},{20,16},{24,28},{28,24},{1,5},{5... | collective-permute-start | bytes 688136 | tf_op jit(solution)/shard_map/ppermute | solution.py:41
  12.9 11.4 %collective-permute-start.15 = (bf16[128,896]{1,0:T(8,128)(2,1)S(1)}, bf16[128,896]{1,0:T(8,128)(2,1)S(1)}, u32[]{:S(2)}, u32[]{:S(2)}) collective-permute-start(bf16[128,896]{1,0:T(8,128)(2,1)S(1)} %maximum_maximum_fusion.refs_4_), channel_id=1, source_target_pairs={{0,24},{4,28},{8,16},{12,20},{16,8},{20,12},{24,0},{28,4},{1,25},{... | collective-permute-start | bytes 688136 | tf_op jit(solution)/shard_map/ppermute | solution.py:41
  16.6 31.4 %collective-permute-start.14 = (bf16[128,896]{1,0:T(8,128)(2,1)S(1)}, bf16[128,896]{1,0:T(8,128)(2,1)S(1)}, u32[]{:S(2)}, u32[]{:S(2)}) collective-permute-start(bf16[128,896]{1,0:T(8,128)(2,1)S(1)} %maximum_maximum_fusion.refs_4_), channel_id=1, source_target_pairs={{0,16},{4,20},{8,24},{12,28},{16,0},{20,4},{24,8},{28,12},{1,17},{... | collective-permute-start | bytes 688136 | tf_op jit(solution)/shard_map/ppermute | solution.py:41
  19.1 39.4 %collective-permute-start = (bf16[256,1024]{1,0:T(8,128)(2,1)}, bf16[256,1024]{1,0:T(8,128)(2,1)S(1)}, u32[]{:S(2)}, u32[]{:S(2)}) collective-permute-start(bf16[256,1024]{1,0:T(8,128)(2,1)} %get-tuple-element.75.refs_0_), channel_id=1, source_target_pairs={{0,2},{1,3},{2,0},{3,1},{4,6},{5,7},{6,4},{7,5},{8,10},{9,11},{10,... | collective-permute-start | bytes 1572872 | tf_op jit(solution)/shard_map/ppermute | solution.py:41
  20.8 80.3 %copy-start.15 = (bf16[128,1024]{1,0:T(8,128)(2,1)}, bf16[128,1024]{1,0:T(8,128)(2,1)S(1)}, u32[]{:S(2)}) copy-start(bf16[128,1024]{1,0:T(8,128)(2,1)S(1)} %pad_maximum_fusion.refs_8_) | copy-start | bytes 786436
  20.8 28.8 %collective-permute-start.11 = (bf16[128,1024]{1,0:T(8,128)(2,1)S(1)}, bf16[128,1024]{1,0:T(8,128)(2,1)S(1)}, u32[]{:S(2)}, u32[]{:S(2)}) collective-permute-start(bf16[128,1024]{1,0:T(8,128)(2,1)S(1)} %pad_maximum_fusion.refs_8_), channel_id=1, source_target_pairs={{0,24},{4,28},{8,16},{12,20},{16,8},{20,12},{24,0},{28,4},{1,25},{... | collective-permute-start | bytes 786440 | tf_op jit(solution)/shard_map/ppermute | solution.py:41
  22.8 25.2 %copy-start.29 = (bf16[128,896]{1,0:T(8,128)(2,1)}, bf16[128,896]{1,0:T(8,128)(2,1)S(1)}, u32[]{:S(2)}) copy-start(bf16[128,896]{1,0:T(8,128)(2,1)S(1)} %collective-permute-done.16.refs_8_) | copy-start | bytes 688132
  22.8 26.7 %collective-permute-start.13 = (bf16[128,896]{1,0:T(8,128)(2,1)S(1)}, bf16[128,896]{1,0:T(8,128)(2,1)S(1)}, u32[]{:S(2)}, u32[]{:S(2)}) collective-permute-start(bf16[128,896]{1,0:T(8,128)(2,1)S(1)} %maximum_maximum_fusion.refs_4_), channel_id=1, source_target_pairs={{0,8},{4,12},{8,0},{12,4},{16,24},{20,28},{24,16},{28,20},{1,9},{5... | collective-permute-start | bytes 688136 | tf_op jit(solution)/shard_map/ppermute | solution.py:41
  24.3 39.1 %copy-start.30 = (bf16[128,896]{1,0:T(8,128)(2,1)}, bf16[128,896]{1,0:T(8,128)(2,1)S(1)}, u32[]{:S(2)}) copy-start(bf16[128,896]{1,0:T(8,128)(2,1)S(1)} %collective-permute-done.15.refs_7_) | copy-start | bytes 688132
  24.3 34.1 %collective-permute-start.9 = (bf16[128,1024]{1,0:T(8,128)(2,1)S(1)}, bf16[128,1024]{1,0:T(8,128)(2,1)}, u32[]{:S(2)}, u32[]{:S(2)}) collective-permute-start(bf16[128,1024]{1,0:T(8,128)(2,1)S(1)} %pad_maximum_fusion.refs_8_), channel_id=1, source_target_pairs={{0,16},{4,20},{8,24},{12,28},{16,0},{20,4},{24,8},{28,12},{1,17},{... | collective-permute-start | bytes 786440 | tf_op jit(solution)/shard_map/ppermute | solution.py:41
  48.0 21.1 %collective-permute-start.3 = (bf16[256,1024]{1,0:T(8,128)(2,1)}, bf16[256,1024]{1,0:T(8,128)(2,1)S(1)}, u32[]{:S(2)}, u32[]{:S(2)}) collective-permute-start(bf16[256,1024]{1,0:T(8,128)(2,1)} %get-tuple-element.76.refs_4_), channel_id=1, source_target_pairs={{0,2},{1,3},{2,0},{3,1},{4,6},{5,7},{6,4},{7,5},{8,10},{9,11},{10,... | collective-permute-start | bytes 1572872 | tf_op jit(solution)/shard_map/ppermute | solution.py:41
  49.5 30.5 %copy-start.32 = (bf16[128,896]{1,0:T(8,128)(2,1)}, bf16[128,896]{1,0:T(8,128)(2,1)S(1)}, u32[]{:S(2)}) copy-start(bf16[128,896]{1,0:T(8,128)(2,1)S(1)} %collective-permute-done.13.refs_5_) | copy-start | bytes 688132
  49.5 11.9 %collective-permute-start.7 = (bf16[128,1024]{1,0:T(8,128)(2,1)S(1)}, bf16[128,1024]{1,0:T(8,128)(2,1)}, u32[]{:S(2)}, u32[]{:S(2)}) collective-permute-start(bf16[128,1024]{1,0:T(8,128)(2,1)S(1)} %pad_maximum_fusion.refs_8_), channel_id=1, source_target_pairs={{0,8},{4,12},{8,0},{12,4},{16,24},{20,28},{24,16},{28,20},{1,9},{5... | collective-permute-start | bytes 786440 | tf_op jit(solution)/shard_map/ppermute | solution.py:41
  49.6 51.5 %copy-start.26 = (bf16[128,1024]{1,0:T(8,128)(2,1)}, bf16[128,1024]{1,0:T(8,128)(2,1)S(1)}, u32[]{:S(2)}) copy-start(bf16[128,1024]{1,0:T(8,128)(2,1)S(1)} %collective-permute-done.11.refs_14_) | copy-start | bytes 786436
  49.6 12.3 %collective-permute-start.6 = (bf16[128,1024]{1,0:T(8,128)(2,1)S(1)}, bf16[128,1024]{1,0:T(8,128)(2,1)S(1)}, u32[]{:S(2)}, u32[]{:S(2)}) collective-permute-start(bf16[128,1024]{1,0:T(8,128)(2,1)S(1)} %pad_maximum_fusion.refs_8_), channel_id=1, source_target_pairs={{0,4},{4,0},{8,12},{12,8},{16,20},{20,16},{24,28},{28,24},{1,5},{5... | collective-permute-start | bytes 786440 | tf_op jit(solution)/shard_map/ppermute | solution.py:41
  58.5 20.1 %collective-permute-start.1 = (bf16[256,1024]{1,0:T(8,128)(2,1)}, bf16[256,1024]{1,0:T(8,128)(2,1)S(1)}, u32[]{:S(2)}, u32[]{:S(2)}) collective-permute-start(bf16[256,1024]{1,0:T(8,128)(2,1)} %get-tuple-element.75.refs_0_), channel_id=1, source_target_pairs={{0,1},{1,0},{2,3},{3,2},{4,5},{5,4},{6,7},{7,6},{8,9},{9,8},{10,11... | collective-permute-start | bytes 1572872 | tf_op jit(solution)/shard_map/ppermute | solution.py:41
  58.5 22.2 %copy-start.2 = (bf16[256,1024]{1,0:T(8,128)(2,1)}, bf16[256,1024]{1,0:T(8,128)(2,1)S(1)}, u32[]{:S(2)}) copy-start(bf16[256,1024]{1,0:T(8,128)(2,1)S(1)} %collective-permute-done.refs_2_.refs_1_) | copy-start | bytes 1572868
  58.5 21.6 %collective-permute-start.2 = (bf16[256,1024]{1,0:T(8,128)(2,1)S(1)}, bf16[256,1024]{1,0:T(8,128)(2,1)S(1)}, u32[]{:S(2)}, u32[]{:S(2)}) collective-permute-start(bf16[256,1024]{1,0:T(8,128)(2,1)S(1)} %collective-permute-done.refs_2_.refs_1_), channel_id=1, source_target_pairs={{0,1},{1,0},{2,3},{3,2},{4,5},{5,4},{6,7},{7,6},{8,9},{9,8},{10,11... | collective-permute-start | bytes 1572872 | tf_op jit(solution)/shard_map/ppermute | solution.py:41
  61.4 7.7 %collective-permute-start.19 = (bf16[128,896]{1,0:T(8,128)(2,1)S(1)}, bf16[128,896]{1,0:T(8,128)(2,1)S(1)}, u32[]{:S(2)}, u32[]{:S(2)}) collective-permute-start(bf16[128,896]{1,0:T(8,128)(2,1)S(1)} %collective-permute-done.15.refs_7_), channel_id=1, source_target_pairs={{0,4},{4,0},{8,12},{12,8},{16,20},{20,16},{24,28},{28,24},{1,5},{5... | collective-permute-start | bytes 688136 | tf_op jit(solution)/shard_map/ppermute | solution.py:41
  61.9 9.7 %collective-permute-start.18 = (bf16[128,896]{1,0:T(8,128)(2,1)}, bf16[128,896]{1,0:T(8,128)(2,1)S(1)}, u32[]{:S(2)}, u32[]{:S(2)}) collective-permute-start(bf16[128,896]{1,0:T(8,128)(2,1)} %copy-done.31), channel_id=1, source_target_pairs={{0,4},{4,0},{8,12},{12,8},{16,20},{20,16},{24,28},{28,24},{1,5},{5... | collective-permute-start | bytes 688136 | tf_op jit(solution)/shard_map/ppermute | solution.py:41
  69.1 32.1 %collective-permute-start.4 = (bf16[256,1024]{1,0:T(8,128)(2,1)}, bf16[256,1024]{1,0:T(8,128)(2,1)S(1)}, u32[]{:S(2)}, u32[]{:S(2)}) collective-permute-start(bf16[256,1024]{1,0:T(8,128)(2,1)} %get-tuple-element.76.refs_4_), channel_id=1, source_target_pairs={{0,1},{1,0},{2,3},{3,2},{4,5},{5,4},{6,7},{7,6},{8,9},{9,8},{10,11... | collective-permute-start | bytes 1572872 | tf_op jit(solution)/shard_map/ppermute | solution.py:41
  69.1 32.0 %copy-start.21 = (bf16[256,1024]{1,0:T(8,128)(2,1)}, bf16[256,1024]{1,0:T(8,128)(2,1)S(1)}, u32[]{:S(2)}) copy-start(bf16[256,1024]{1,0:T(8,128)(2,1)S(1)} %collective-permute-done.3.refs_5_) | copy-start | bytes 1572868
  69.1 32.1 %collective-permute-start.5 = (bf16[256,1024]{1,0:T(8,128)(2,1)S(1)}, bf16[256,1024]{1,0:T(8,128)(2,1)}, u32[]{:S(2)}, u32[]{:S(2)}) collective-permute-start(bf16[256,1024]{1,0:T(8,128)(2,1)S(1)} %collective-permute-done.3.refs_5_), channel_id=1, source_target_pairs={{0,1},{1,0},{2,3},{3,2},{4,5},{5,4},{6,7},{7,6},{8,9},{9,8},{10,11... | collective-permute-start | bytes 1572872 | tf_op jit(solution)/shard_map/ppermute | solution.py:41
  71.6 6.4 %collective-permute-start.17 = (bf16[128,896]{1,0:T(8,128)(2,1)S(1)}, bf16[128,896]{1,0:T(8,128)(2,1)S(1)}, u32[]{:S(2)}, u32[]{:S(2)}) collective-permute-start(bf16[128,896]{1,0:T(8,128)(2,1)S(1)} %collective-permute-done.13.refs_5_), channel_id=1, source_target_pairs={{0,4},{4,0},{8,12},{12,8},{16,20},{20,16},{24,28},{28,24},{1,5},{5... | collective-permute-start | bytes 688136 | tf_op jit(solution)/shard_map/ppermute | solution.py:41
  78.0 23.1 %collective-permute-start.12 = (bf16[128,1024]{1,0:T(8,128)(2,1)S(1)}, bf16[128,1024]{1,0:T(8,128)(2,1)}, u32[]{:S(2)}, u32[]{:S(2)}) collective-permute-start(bf16[128,1024]{1,0:T(8,128)(2,1)S(1)} %collective-permute-done.11.refs_14_), channel_id=1, source_target_pairs={{0,4},{4,0},{8,12},{12,8},{16,20},{20,16},{24,28},{28,24},{1,5},{5... | collective-permute-start | bytes 786440 | tf_op jit(solution)/shard_map/ppermute | solution.py:41
  78.5 22.6 %collective-permute-start.10 = (bf16[128,1024]{1,0:T(8,128)(2,1)}, bf16[128,1024]{1,0:T(8,128)(2,1)}, u32[]{:S(2)}, u32[]{:S(2)}) collective-permute-start(bf16[128,1024]{1,0:T(8,128)(2,1)} %collective-permute-done.9.refs_12_), channel_id=1, source_target_pairs={{0,4},{4,0},{8,12},{12,8},{16,20},{20,16},{24,28},{28,24},{1,5},{5... | collective-permute-start | bytes 786440 | tf_op jit(solution)/shard_map/ppermute | solution.py:41
  80.1 21.1 %collective-permute-start.8 = (bf16[128,1024]{1,0:T(8,128)(2,1)}, bf16[128,1024]{1,0:T(8,128)(2,1)}, u32[]{:S(2)}, u32[]{:S(2)}) collective-permute-start(bf16[128,1024]{1,0:T(8,128)(2,1)} %collective-permute-done.7.refs_10_), channel_id=1, source_target_pairs={{0,4},{4,0},{8,12},{12,8},{16,20},{20,16},{24,28},{28,24},{1,5},{5... | collective-permute-start | bytes 786440 | tf_op jit(solution)/shard_map/ppermute | solution.py:41
  111.0 3.8 %collective-permute-start.22 = (f32[4,8,256]{2,1,0:T(8,128)}, f32[4,8,256]{2,1,0:T(8,128)S(1)}, u32[]{:S(2)}, u32[]{:S(2)}) collective-permute-start(f32[4,8,256]{2,1,0:T(8,128)} %get-tuple-element.95.refs_0_), channel_id=1, source_target_pairs={{0,3},{1,2},{2,1},{3,0},{4,7},{5,6},{6,5},{7,4},{8,11},{9,10},{10,... | collective-permute-start | bytes 98312 | tf_op jit(solution)/shard_map/ppermute | solution.py:41
  111.1 4.2 %collective-permute-start.21 = (f32[4,8,256]{2,1,0:T(8,128)}, f32[4,8,256]{2,1,0:T(8,128)S(1)}, u32[]{:S(2)}, u32[]{:S(2)}) collective-permute-start(f32[4,8,256]{2,1,0:T(8,128)} %get-tuple-element.95.refs_0_), channel_id=1, source_target_pairs={{0,2},{1,3},{2,0},{3,1},{4,6},{5,7},{6,4},{7,5},{8,10},{9,11},{10,... | collective-permute-start | bytes 98312 | tf_op jit(solution)/shard_map/ppermute | solution.py:41
  112.7 2.6 collective-permute-start.20
  150.4 72.3 %copy-start.7 = (bf16[512,896]{1,0:T(8,128)(2,1)}, bf16[512,896]{1,0:T(8,128)(2,1)S(1)}, u32[]{:S(2)}) copy-start(bf16[512,896]{1,0:T(8,128)(2,1)S(1)} %convolution_convert_fusion.3.refs_0_) | copy-start | bytes 2752516
  157.1 33.6 %collective-permute-start.38 = (bf16[256,512]{1,0:T(8,128)(2,1)}, bf16[256,512]{1,0:T(8,128)(2,1)S(1)}, u32[]{:S(2)}, u32[]{:S(2)}) collective-permute-start(bf16[256,512]{1,0:T(8,128)(2,1)} %get-tuple-element.157), channel_id=1, source_target_pairs={{0,24},{4,28},{8,16},{12,20},{16,8},{20,12},{24,0},{28,4},{1,25},{... | collective-permute-start | bytes 786440 | tf_op jit(solution)/shard_map/ppermute | solution.py:41
  159.5 31.9 %collective-permute-start.37 = (bf16[256,512]{1,0:T(8,128)(2,1)}, bf16[256,512]{1,0:T(8,128)(2,1)S(1)}, u32[]{:S(2)}, u32[]{:S(2)}) collective-permute-start(bf16[256,512]{1,0:T(8,128)(2,1)} %get-tuple-element.158), channel_id=1, source_target_pairs={{0,16},{4,20},{8,24},{12,28},{16,0},{20,4},{24,8},{28,12},{1,17},{... | collective-permute-start | bytes 786440 | tf_op jit(solution)/shard_map/ppermute | solution.py:41
  170.3 4.5 %collective-permute-start.40 = (f32[32,512]{1,0:T(8,128)}, f32[32,512]{1,0:T(8,128)S(1)}, u32[]{:S(2)}, u32[]{:S(2)}) collective-permute-start(f32[32,512]{1,0:T(8,128)} %shard_map.273), channel_id=1, source_target_pairs={{0,4},{4,0},{8,12},{12,8},{16,20},{20,16},{24,28},{28,24},{1,5},{5... | collective-permute-start | bytes 196616 | tf_op jit(solution)/shard_map/ppermute | solution.py:41
  174.8 6.9 %collective-permute-start.43 = (f32[32,512]{1,0:T(8,128)S(1)}, f32[32,512]{1,0:T(8,128)S(1)}, u32[]{:S(2)}, u32[]{:S(2)}) collective-permute-start(f32[32,512]{1,0:T(8,128)S(1)} %add.62), channel_id=1, source_target_pairs={{0,24},{4,28},{8,16},{12,20},{16,8},{20,12},{24,0},{28,4},{1,25},{... | collective-permute-start | bytes 196616 | tf_op jit(solution)/shard_map/ppermute | solution.py:41
  176.3 11.1 %collective-permute-start.42 = (f32[32,512]{1,0:T(8,128)S(1)}, f32[32,512]{1,0:T(8,128)S(1)}, u32[]{:S(2)}, u32[]{:S(2)}) collective-permute-start(f32[32,512]{1,0:T(8,128)S(1)} %add.62), channel_id=1, source_target_pairs={{0,16},{4,20},{8,24},{12,28},{16,0},{20,4},{24,8},{28,12},{1,17},{... | collective-permute-start | bytes 196616 | tf_op jit(solution)/shard_map/ppermute | solution.py:41
  178.3 9.1 %collective-permute-start.41 = (f32[32,512]{1,0:T(8,128)S(1)}, f32[32,512]{1,0:T(8,128)S(1)}, u32[]{:S(2)}, u32[]{:S(2)}) collective-permute-start(f32[32,512]{1,0:T(8,128)S(1)} %add.62), channel_id=1, source_target_pairs={{0,8},{4,12},{8,0},{12,4},{16,24},{20,28},{24,16},{28,20},{1,9},{5... | collective-permute-start | bytes 196616 | tf_op jit(solution)/shard_map/ppermute | solution.py:41
  181.7 11.5 %collective-permute-start.36 = (bf16[256,512]{1,0:T(8,128)(2,1)}, bf16[256,512]{1,0:T(8,128)(2,1)}, u32[]{:S(2)}, u32[]{:S(2)}) collective-permute-start(bf16[256,512]{1,0:T(8,128)(2,1)} %get-tuple-element.159), channel_id=1, source_target_pairs={{0,8},{4,12},{8,0},{12,4},{16,24},{20,28},{24,16},{28,20},{1,9},{5... | collective-permute-start | bytes 786440 | tf_op jit(solution)/shard_map/ppermute | solution.py:41
  187.4 38.2 %collective-permute-start.23 = (bf16[512,1024]{1,0:T(8,128)(2,1)}, bf16[512,1024]{1,0:T(8,128)(2,1)S(1)}, u32[]{:S(2)}, u32[]{:S(2)}) collective-permute-start(bf16[512,1024]{1,0:T(8,128)(2,1)} %get-tuple-element.150), channel_id=1, source_target_pairs={{0,1},{1,0},{2,3},{3,2},{4,5},{5,4},{6,7},{7,6},{8,9},{9,8},{10,11... | collective-permute-start | bytes 3145736 | tf_op jit(solution)/shard_map/ppermute | solution.py:41
  187.4 13.7 %collective-permute-start.27 = (bf16[256,896]{1,0:T(8,128)(2,1)}, bf16[256,896]{1,0:T(8,128)(2,1)}, u32[]{:S(2)}, u32[]{:S(2)}) collective-permute-start(bf16[256,896]{1,0:T(8,128)(2,1)} %convolution_convert_fusion.5), channel_id=1, source_target_pairs={{0,4},{4,0},{8,12},{12,8},{16,20},{20,16},{24,28},{28,24},{1,5},{5... | collective-permute-start | bytes 1376264 | tf_op jit(solution)/shard_map/ppermute | solution.py:41
  190.7 37.5 %copy-start.19 = (bf16[256,512]{1,0:T(8,128)(2,1)}, bf16[256,512]{1,0:T(8,128)(2,1)S(1)}, u32[]{:S(2)}) copy-start(bf16[256,512]{1,0:T(8,128)(2,1)S(1)} %collective-permute-done.38.refs_13_) | copy-start | bytes 786436
  190.7 32.0 %collective-permute-start.32 = (bf16[512,512]{1,0:T(8,128)(2,1)S(1)}, bf16[512,512]{1,0:T(8,128)(2,1)S(1)}, u32[]{:S(2)}, u32[]{:S(2)}) collective-permute-start(bf16[512,512]{1,0:T(8,128)(2,1)S(1)} %get-tuple-element.161), channel_id=1, source_target_pairs={{0,4},{4,0},{8,12},{12,8},{16,20},{20,16},{24,28},{28,24},{1,5},{5... | collective-permute-start | bytes 1572872 | tf_op jit(solution)/shard_map/ppermute | solution.py:41
  191.4 36.8 %copy-start.20 = (bf16[256,512]{1,0:T(8,128)(2,1)}, bf16[256,512]{1,0:T(8,128)(2,1)S(1)}, u32[]{:S(2)}) copy-start(bf16[256,512]{1,0:T(8,128)(2,1)S(1)} %collective-permute-done.37.refs_12_) | copy-start | bytes 786436
  191.4 30.7 %collective-permute-start.30 = (bf16[256,896]{1,0:T(8,128)(2,1)S(1)}, bf16[256,896]{1,0:T(8,128)(2,1)S(1)}, u32[]{:S(2)}, u32[]{:S(2)}) collective-permute-start(bf16[256,896]{1,0:T(8,128)(2,1)S(1)} %copy-done.25), channel_id=1, source_target_pairs={{0,4},{4,0},{8,12},{12,8},{16,20},{20,16},{24,28},{28,24},{1,5},{5... | collective-permute-start | bytes 1376264 | tf_op jit(solution)/shard_map/ppermute | solution.py:41
  193.1 35.1 %collective-permute-start.25 = (bf16[512,1024]{1,0:T(8,128)(2,1)}, bf16[512,1024]{1,0:T(8,128)(2,1)S(1)}, u32[]{:S(2)}, u32[]{:S(2)}) collective-permute-start(bf16[512,1024]{1,0:T(8,128)(2,1)} %get-tuple-element.120), channel_id=1, source_target_pairs={{0,1},{1,0},{2,3},{3,2},{4,5},{5,4},{6,7},{7,6},{8,9},{9,8},{10,11... | collective-permute-start | bytes 3145736 | tf_op jit(solution)/shard_map/ppermute | solution.py:41
  194.2 48.7 %copy-start.9 = (bf16[512,1024]{1,0:T(8,128)(2,1)S(1)}, bf16[512,1024]{1,0:T(8,128)(2,1)}, u32[]{:S(2)}) copy-start(bf16[512,1024]{1,0:T(8,128)(2,1)} %get-tuple-element.119.refs_0_) | copy-start | bytes 3145732
  201.1 27.9 %collective-permute-start.39 = (bf16[128,512]{1,0:T(8,128)(2,1)S(1)}, bf16[128,512]{1,0:T(8,128)(2,1)S(1)}, u32[]{:S(2)}, u32[]{:S(2)}) collective-permute-start(bf16[128,512]{1,0:T(8,128)(2,1)S(1)} %add_convert_fusion.5), channel_id=1, source_target_pairs={{0,4},{4,0},{8,12},{12,8},{16,20},{20,16},{24,28},{28,24},{1,5},{5... | collective-permute-start | bytes 393224 | tf_op jit(solution)/shard_map/ppermute | solution.py:41
  222.1 20.9 %copy-start.16 = (bf16[256,896]{1,0:T(8,128)(2,1)}, bf16[256,896]{1,0:T(8,128)(2,1)S(1)}, u32[]{:S(2)}) copy-start(bf16[256,896]{1,0:T(8,128)(2,1)S(1)} %collective-permute-done.30.refs_4_) | copy-start | bytes 1376260
  222.1 32.5 %collective-permute-start.29 = (bf16[128,896]{1,0:T(8,128)(2,1)S(1)}, bf16[128,896]{1,0:T(8,128)(2,1)}, u32[]{:S(2)}, u32[]{:S(2)}) collective-permute-start(bf16[128,896]{1,0:T(8,128)(2,1)S(1)} %get-tuple-element.155), channel_id=1, source_target_pairs={{0,16},{4,20},{8,24},{12,28},{16,0},{20,4},{24,8},{28,12},{1,17},{... | collective-permute-start | bytes 688136 | tf_op jit(solution)/shard_map/ppermute | solution.py:41
  222.7 31.9 %copy-start.38 = (f32[32,512]{1,0:T(8,128)S(1)}, f32[32,512]{1,0:T(8,128)}, u32[]{:S(2)}) copy-start(f32[32,512]{1,0:T(8,128)} %copy-done.37) | copy-start | bytes 196612
  222.7 31.9 %collective-permute-start.28 = (bf16[128,896]{1,0:T(8,128)(2,1)S(1)}, bf16[128,896]{1,0:T(8,128)(2,1)}, u32[]{:S(2)}, u32[]{:S(2)}) collective-permute-start(bf16[128,896]{1,0:T(8,128)(2,1)S(1)} %get-tuple-element.156), channel_id=1, source_target_pairs={{0,24},{4,28},{8,16},{12,20},{16,8},{20,12},{24,0},{28,4},{1,25},{... | collective-permute-start | bytes 688136 | tf_op jit(solution)/shard_map/ppermute | solution.py:41
  225.6 32.7 %copy-start.8 = (bf16[512,1024]{1,0:T(8,128)(2,1)}, bf16[512,1024]{1,0:T(8,128)(2,1)S(1)}, u32[]{:S(2)}) copy-start(bf16[512,1024]{1,0:T(8,128)(2,1)S(1)} %collective-permute-done.23.refs_2_) | copy-start | bytes 3145732
  225.6 15.5 %collective-permute-start.35 = (bf16[128,512]{1,0:T(8,128)(2,1)S(1)}, bf16[128,512]{1,0:T(8,128)(2,1)S(1)}, u32[]{:S(2)}, u32[]{:S(2)}) collective-permute-start(bf16[128,512]{1,0:T(8,128)(2,1)S(1)} %get-tuple-element.152), channel_id=1, source_target_pairs={{0,8},{4,12},{8,0},{12,4},{16,24},{20,28},{24,16},{28,20},{1,9},{5... | collective-permute-start | bytes 393224 | tf_op jit(solution)/shard_map/ppermute | solution.py:41
  228.2 26.4 %collective-permute-start.31 = (bf16[128,896]{1,0:T(8,128)(2,1)S(1)}, bf16[128,896]{1,0:T(8,128)(2,1)S(1)}, u32[]{:S(2)}, u32[]{:S(2)}) collective-permute-start(bf16[128,896]{1,0:T(8,128)(2,1)S(1)} %add_convert_fusion.2), channel_id=1, source_target_pairs={{0,8},{4,12},{8,0},{12,4},{16,24},{20,28},{24,16},{28,20},{1,9},{5... | collective-permute-start | bytes 688136 | tf_op jit(solution)/shard_map/ppermute | solution.py:41
  229.1 25.6 %copy-start.42 = (bf16[128,512]{1,0:T(8,128)(2,1)}, bf16[128,512]{1,0:T(8,128)(2,1)S(1)}, u32[]{:S(2)}) copy-start(bf16[128,512]{1,0:T(8,128)(2,1)S(1)} %collective-permute-done.39.refs_14_) | copy-start | bytes 393220
  229.1 23.5 %collective-permute-start.34 = (bf16[128,512]{1,0:T(8,128)(2,1)S(1)}, bf16[128,512]{1,0:T(8,128)(2,1)S(1)}, u32[]{:S(2)}, u32[]{:S(2)}) collective-permute-start(bf16[128,512]{1,0:T(8,128)(2,1)S(1)} %get-tuple-element.153), channel_id=1, source_target_pairs={{0,16},{4,20},{8,24},{12,28},{16,0},{20,4},{24,8},{28,12},{1,17},{... | collective-permute-start | bytes 393224 | tf_op jit(solution)/shard_map/ppermute | solution.py:41
  241.1 12.6 %collective-permute-start.33 = (bf16[128,512]{1,0:T(8,128)(2,1)S(1)}, bf16[128,512]{1,0:T(8,128)(2,1)S(1)}, u32[]{:S(2)}, u32[]{:S(2)}) collective-permute-start(bf16[128,512]{1,0:T(8,128)(2,1)S(1)} %get-tuple-element.154), channel_id=1, source_target_pairs={{0,24},{4,28},{8,16},{12,20},{16,8},{20,12},{24,0},{28,4},{1,25},{... | collective-permute-start | bytes 393224 | tf_op jit(solution)/shard_map/ppermute | solution.py:41
  252.6 42.1 %collective-permute-start.24 = (bf16[256,1024]{1,0:T(8,128)(2,1)S(1)}, bf16[256,1024]{1,0:T(8,128)(2,1)S(1)}, u32[]{:S(2)}, u32[]{:S(2)}) collective-permute-start(bf16[256,1024]{1,0:T(8,128)(2,1)S(1)} %add_convert_fusion.1), channel_id=1, source_target_pairs={{0,2},{1,3},{2,0},{3,1},{4,6},{5,7},{6,4},{7,5},{8,10},{9,11},{10,... | collective-permute-start | bytes 1572872 | tf_op jit(solution)/shard_map/ppermute | solution.py:41
  253.6 36.6 %collective-permute-start.26 = (bf16[256,1024]{1,0:T(8,128)(2,1)S(1)}, bf16[256,1024]{1,0:T(8,128)(2,1)S(1)}, u32[]{:S(2)}, u32[]{:S(2)}) collective-permute-start(bf16[256,1024]{1,0:T(8,128)(2,1)S(1)} %add_convert_fusion), channel_id=1, source_target_pairs={{0,2},{1,3},{2,0},{3,1},{4,6},{5,7},{6,4},{7,5},{8,10},{9,11},{10,... | collective-permute-start | bytes 1572872 | tf_op jit(solution)/shard_map/ppermute | solution.py:41
  259.2 25.4 %copy-start.18 = (f32[160,256]{1,0:T(8,128)}, f32[160,256]{1,0:T(8,128)S(1)}, u32[]{:S(2)}) copy-start(f32[160,256]{1,0:T(8,128)S(1)} %pad_maximum_fusion.1.refs_0_) | copy-start | bytes 491524
  259.2 21.5 %collective-permute-start.46 = (f32[160,256]{1,0:T(8,128)S(1)}, f32[160,256]{1,0:T(8,128)S(1)}, u32[]{:S(2)}, u32[]{:S(2)}) collective-permute-start(f32[160,256]{1,0:T(8,128)S(1)} %pad_maximum_fusion.1.refs_0_), channel_id=1, source_target_pairs={{0,3},{1,2},{2,1},{3,0},{4,7},{5,6},{6,5},{7,4},{8,11},{9,10},{10,... | collective-permute-start | bytes 491528 | tf_op jit(solution)/shard_map/ppermute | solution.py:41
  259.3 25.2 %collective-permute-start.45 = (f32[160,256]{1,0:T(8,128)S(1)}, f32[160,256]{1,0:T(8,128)S(1)}, u32[]{:S(2)}, u32[]{:S(2)}) collective-permute-start(f32[160,256]{1,0:T(8,128)S(1)} %pad_maximum_fusion.1.refs_0_), channel_id=1, source_target_pairs={{0,2},{1,3},{2,0},{3,1},{4,6},{5,7},{6,4},{7,5},{8,10},{9,11},{10,... | collective-permute-start | bytes 491528 | tf_op jit(solution)/shard_map/ppermute | solution.py:41
  260.5 24.1 %collective-permute-start.44 = (f32[160,256]{1,0:T(8,128)S(1)}, f32[160,256]{1,0:T(8,128)S(1)}, u32[]{:S(2)}, u32[]{:S(2)}) collective-permute-start(f32[160,256]{1,0:T(8,128)S(1)} %pad_maximum_fusion.1.refs_0_), channel_id=1, source_target_pairs={{0,1},{1,0},{2,3},{3,2},{4,5},{5,4},{6,7},{7,6},{8,9},{9,8},{10,11... | collective-permute-start | bytes 491528 | tf_op jit(solution)/shard_map/ppermute | solution.py:41
  (36 other events, 171.0 us)

commit v5 on v4

--- a/solution.py
+++ b/solution.py
@@ -557,13 +557,15 @@
 
 def shared_kernel(count, rows, cols):
     def kernel(place, *refs):
-        grad_w, of_conv, of_pre = refs[count:]
+        grad_w, of_taps, of_bias, of_pre = refs[count:]
+        width = of_taps.shape[0]
         total = refs[0][...]
         for term in refs[1:count]:
             total = total + term[...]
         share, twice = grad_w.shape
         grad_w[...] = total[:share]
-        of_conv[...] = total[share : share + 8]
+        of_taps[...] = total[share : share + width]
+        of_bias[...] = total[share + width : share + width + 1]
         for r in range(of_pre.shape[1] // cols):
             for k in range(cols // twice):
                 at = share + k * rows + 8 + r
@@ -831,7 +833,7 @@
     columns = columns[0]
     grad_x, grad_bc, grad_head = carry[:3]
 
-    later = even + (model - even) // 2 if dp % 4 == 0 else even
+    later = model - share if model - share > even else even
     scan_near = [tn(normed[:, later:], columns)]
     if later > even:
         scan_near.append(tn(normed[:, even:later], columns))
@@ -895,11 +897,11 @@
     across = [small[16:, k : k + twice] for k in range(0, cols, twice)]
     across = jnp.concatenate(across, axis=0)
     across = direct_terms(jnp.concatenate([grad_bc_part, across], axis=0), TP)
-    grad_w_bc, of_bc, sum_pre = call(
+    grad_w_bc, sum_taps, sum_bias, sum_pre = call(
         shared_kernel(tensor, rows - 16, cols), 1,
         [whole(across[0].shape)] * tensor,
-        [whole((share, twice)), whole((8, twice)), whole((1, model))],
-        [((share, twice), f32), ((8, twice), f32), ((1, model), f32)],
+        [whole((share, twice)), whole((width, twice)), whole((1, twice)), whole((1, model))],
+        [((share, twice), f32), ((width, twice), f32), ((1, twice), f32), ((1, model), f32)],
     )(place_entry, *across)
     of_x = small[:8, :inner]
     sum_gain = small[8, :inner]
@@ -913,8 +915,8 @@
         grad_w_bc,
         of_x[:width],
         of_x[width],
-        of_bc[:width],
-        of_bc[width],
+        sum_taps,
+        sum_bias.reshape(twice),
         of_head[0, :heads],
         of_head[1, :heads],
         of_x[width + 1].reshape(heads, head_dim).sum(axis=1),

time: 300 us -> 292 us (0.973)
  waiting for transfers between devices: 103 us -> 91.4 us
  starting transfers between devices: 67.7 us -> 74.2 us
    ppermute x47, waiting for transfers between devices: 103 us -> 91.4 us  [swap(): return lax.ppermute(value, axis, [(i, i ^ bits) for i in range(size)])]
    ppermute x47, starting transfers between devices: 67.7 us -> 74.2 us  [swap(): return lax.ppermute(value, axis, [(i, i ^ bits) for i in range(size)])]
    unnamed x111 -> x109, local copies, waits for them, and re-layouts: 8.6 us -> 9.79 us
  transfers between devices with their start and end apart: 47 -> 47, of which waited for: 18 -> 16; matrix products, arithmetic and copies ran while one was open for 6% -> 4% of each run, Pallas kernels for 14% -> 11%
where the time goes in v5:
time: 292 us
  waiting for transfers between devices  91.4 us (31%)
  Pallas kernels  82.5 us (28%)
  starting transfers between devices  74.2 us (25%)
  local copies, waits for them, and re-layouts  19.5 us (7%)
  matrix products  11.9 us (4%)
  other arithmetic  10.9 us (4%)
    ppermute x47, waiting for transfers between devices, swap(): return lax.ppermute(value, axis, [(i, i ^ bits) for i in range(size)])  91.4 us
    ppermute x47, starting transfers between devices, swap(): return lax.ppermute(value, axis, [(i, i ^ bits) for i in range(size)])  74.2 us
    pallas_call x2, Pallas kernels, per_device(): call(backward_kernel(width, head_dim, len(columns)), span, [back(cols, st...  23.5 us
    pallas_call x2, Pallas kernels, per_device(): call(forward_kernel(width, head_dim, tensor, len(weights), per, start), s...  20.3 us
    dot_general x5, matrix products, tn(): lax.dot_general(left, right, TN, preferred_element_type=f32).astype(bf16)  10.6 us
    unnamed x109, local copies, waits for them, and re-layouts  9.79 us
    pallas_call x1, Pallas kernels, per_device(): call(gate_kernel(tensor, dp, parts), length // block, [gate_piece(p) for...  8.98 us
    pallas_call x1, Pallas kernels, per_device(): call(normed_kernel, 4, [pl.BlockSpec((length, features), lambda c, place:...  7.61 us
  transfers between devices with their start and end apart: 47, of which 16 were waited for; matrix products, arithmetic and copies ran while one was open for 4% of the time, Pallas kernels for 11%

profile of v5, /device:TPU:0, one launch (start us, length us, event | category | flops | bytes accessed | tf_op | source)
XLA Modules:
  0.0 291.6 jit_solution(18124074756390894084)
XLA Ops:
  3.5 1.5 fusion.6
  5.1 1.3 select_maximum_fusion.2.refs_14_.refs_7_.refs_10_
  6.4 1.3 select_maximum_fusion.1.refs_13_.refs_6_.refs_9_
  7.7 1.3 select_maximum_fusion.refs_12_.refs_5_.refs_8_
  9.9 3.0 %collective-permute-start.16 = (bf16[128,896]{1,0:T(8,128)(2,1)S(1)}, bf16[128,896]{1,0:T(8,128)(2,1)S(1)}, u32[]{:S(2)}, u32[]{:S(2)}) collective-permute-start(bf16[128,896]{1,0:T(8,128)(2,1)S(1)} %maximum_maximum_fusion.refs_4_), channel_id=1, source_target_pairs={{0,4},{4,0},{8,12},{12,8},{16,20},{20,16},{24,28},{28,24},{1,5},{5... | collective-permute-start | bytes 688136 | tf_op jit(solution)/shard_map/ppermute | solution.py:41
  13.0 3.6 %collective-permute-start.15 = (bf16[128,896]{1,0:T(8,128)(2,1)S(1)}, bf16[128,896]{1,0:T(8,128)(2,1)S(1)}, u32[]{:S(2)}, u32[]{:S(2)}) collective-permute-start(bf16[128,896]{1,0:T(8,128)(2,1)S(1)} %maximum_maximum_fusion.refs_4_), channel_id=1, source_target_pairs={{0,24},{4,28},{8,16},{12,20},{16,8},{20,12},{24,0},{28,4},{1,25},{... | collective-permute-start | bytes 688136 | tf_op jit(solution)/shard_map/ppermute | solution.py:41
  16.6 2.5 shard_map.262
  19.1 1.5 collective-permute-start
  20.8 2.0 collective-permute-start.11
  22.8 1.6 collective-permute-start.13
  24.3 15.1 %collective-permute-start.9 = (bf16[128,1024]{1,0:T(8,128)(2,1)S(1)}, bf16[128,1024]{1,0:T(8,128)(2,1)}, u32[]{:S(2)}, u32[]{:S(2)}) collective-permute-start(bf16[128,1024]{1,0:T(8,128)(2,1)S(1)} %pad_maximum_fusion.refs_8_), channel_id=1, source_target_pairs={{0,16},{4,20},{8,24},{12,28},{16,0},{20,4},{24,8},{28,12},{1,17},{... | collective-permute-start | bytes 786440 | tf_op jit(solution)/shard_map/ppermute | solution.py:41
  39.5 8.5 %collective-permute-done.14.refs_6_ = bf16[128,896]{1,0:T(8,128)(2,1)S(1)} collective-permute-done((bf16[128,896]{1,0:T(8,128)(2,1)S(1)}, bf16[128,896]{1,0:T(8,128)(2,1)S(1)}, u32[]{:S(2)}, u32[]{:S(2)}) %collective-permute-start.14) | collective-permute-done | bytes 229408 | tf_op jit(solution)/shard_map/ppermute | solution.py:41
  48.0 1.5 collective-permute-start.3
  50.2 8.3 %collective-permute-done.9.refs_12_ = bf16[128,1024]{1,0:T(8,128)(2,1)} collective-permute-done((bf16[128,1024]{1,0:T(8,128)(2,1)S(1)}, bf16[128,1024]{1,0:T(8,128)(2,1)}, u32[]{:S(2)}, u32[]{:S(2)}) %collective-permute-start.9) | collective-permute-done | bytes 262176 | tf_op jit(solution)/shard_map/ppermute | solution.py:41
  59.0 2.4 collective-permute-done.7.refs_10_
  61.9 1.5 collective-permute-start.18
  63.4 5.7 %collective-permute-done.19.refs_11_ = bf16[128,896]{1,0:T(8,128)(2,1)S(1)} collective-permute-done((bf16[128,896]{1,0:T(8,128)(2,1)S(1)}, bf16[128,896]{1,0:T(8,128)(2,1)S(1)}, u32[]{:S(2)}, u32[]{:S(2)}) %collective-permute-start.19) | collective-permute-done | bytes 229408 | tf_op jit(solution)/shard_map/ppermute | solution.py:41
  69.6 1.9 collective-permute-done.18.refs_10_
  72.1 5.9 %collective-permute-done.17.refs_9_ = bf16[128,896]{1,0:T(8,128)(2,1)S(1)} collective-permute-done((bf16[128,896]{1,0:T(8,128)(2,1)S(1)}, bf16[128,896]{1,0:T(8,128)(2,1)S(1)}, u32[]{:S(2)}, u32[]{:S(2)}) %collective-permute-start.17) | collective-permute-done | bytes 229408 | tf_op jit(solution)/shard_map/ppermute | solution.py:41
  78.5 1.5 collective-permute-start.10
  80.8 12.0 %shard_map.263 = (f32[1024,512]{1,0:T(8,128)}, f32[1024,256]{1,0:T(8,128)}, bf16[1024,512]{1,0:T(8,128)(2,1)}, bf16[1024,256]{1,0:T(8,128)(2,1)}, f32[1024,128]{...) custom-call(s32[1]{0:T(128)} %bitcast.2.place, ...), custom_call_target="tpu_custom_call" | custom-call | tf_op jit(solution)/shard_map/pallas_call | solution.py:707
  92.8 8.3 %shard_map.264 = (f32[1024,512]{1,0:T(8,128)}, f32[1024,256]{1,0:T(8,128)}, bf16[1024,512]{1,0:T(8,128)(2,1)}, bf16[1024,256]{1,0:T(8,128)(2,1)}, f32[1024,128]{...) custom-call(s32[1]{0:T(128)} %bitcast.2.place, ...), custom_call_target="tpu_custom_call", output_to_operand_aliasing={{0}: (13, {}), {1}: (14, {}), {2}: (15, {}), {3}: (16, {}),... | custom-call | tf_op jit(solution)/shard_map/pallas_call | solution.py:707
  102.0 9.0 %shard_map.265 = (f32[1024,512]{1,0:T(8,128)}, f32[1024,512]{1,0:T(8,128)}, f32[4,8,256]{2,1,0:T(8,128)}, bf16[1024,1024]{1,0:T(8,128)(2,1)}, bf16[1024,1024]{1,...) custom-call(s32[1]{0:T(128)} %bitcast.2.place, bf16[256,1024]{1,0:T(8,128)(2,1)} %get-tuple-element.76.refs_0_, ...), custom_call_target="tpu_custom_call" | custom-call | tf_op jit(solution)/shard_map/pallas_call | solution.py:747
  111.1 1.7 collective-permute-start.21
  112.9 1.9 collective-permute-done.22.refs_3_
  115.9 6.4 %shard_map.266 = (bf16[1024,512]{1,0:T(8,128)(2,1)}, f32[1024,512]{1,0:T(8,128)}, bf16[1024,512]{1,0:T(8,128)(2,1)}, f32[8,512]{1,0:T(8,128)}) custom-call(s32[1]{0:T(128)} %bitcast.2.place, f32[4,8,256]{2,1,0:T(8,128)} %get-tuple-element.96.refs_0_, f32[4,8,256]{2,1,0:T(8,128)} %copy-done.48, f32[4,8,256]{2,1,0:T(8,128)} %copy-done.47, ...), custom_call_target="tpu_custom_call" | custom-call | tf_op jit(solution)/shard_map/pallas_call | solution.py:769
  122.3 11.6 %shard_map.268 = (bf16[1024,896]{1,0:T(8,128)(2,1)}, f32[8,512]{1,0:T(8,128)}, f32[8,256]{1,0:T(8,128)}, f32[8,128]{1,0:T(8,128)}, f32[128,512]{1,0:T(8,128)}, /...) custom-call(s32[1]{0:T(128)} %bitcast.2.place, f32[1024,512]{1,0:T(8,128)} %get-tuple-element.103.refs_0_, ...), custom_call_target="tpu_custom_call" | custom-call | tf_op jit(solution)/shard_map/pallas_call | solution.py:817
  133.9 12.0 %shard_map.269 = (bf16[1024,896]{1,0:T(8,128)(2,1)}, f32[8,512]{1,0:T(8,128)}, f32[8,256]{1,0:T(8,128)}, f32[8,128]{1,0:T(8,128)}, f32[128,512]{1,0:T(8,128)}, /...) custom-call(s32[1]{0:T(128)} %bitcast.2.place, ...), custom_call_target="tpu_custom_call", output_to_operand_aliasing={{0}: (20, {})} | custom-call | tf_op jit(solution)/shard_map/pallas_call | solution.py:817
  145.9 2.8 convolution_convert_fusion.5
  148.7 1.9 convolution_convert_fusion.4
  150.6 1.3 convolution_convert_fusion.3.refs_0_
  152.4 2.3 convolution_convert_fusion.1
  154.8 1.3 convolution_convert_fusion
  156.1 2.3 convolution_convert_fusion.2
  158.4 1.6 fusion.3
  160.0 7.6 %shard_map.270 = (bf16[512,1024]{1,0:T(8,128)(2,1)}, bf16[512,1024]{1,0:T(8,128)(2,1)}, f32[8,1024]{1,0:T(8,128)}) custom-call(s32[1]{0:T(128)} %bitcast.2.place, bf16[1024,1024]{1,0:T(8,128)(2,1)} %get-tuple-element.101.tokens, bf16[1024,512]{1,0:T(8,128)(2,1)} %get-tuple-element.102.d_gate, bf16[1024,896]{1,0:T(8,128)(2,1)} %get-tuple-element.118.columns, ...), custom_call_target="tpu_custom_call" | custom-call | tf_op jit(solution)/shard_map/pallas_call | solution.py:844
  167.6 1.6 shard_map.273
  169.2 1.3 collective-permute-start.40
  171.5 2.4 collective-permute-start.38
  173.9 2.4 collective-permute-start.43
  176.3 1.1 collective-permute-start.42
  179.4 10.4 %collective-permute-done.43 = f32[32,512]{1,0:T(8,128)S(1)} collective-permute-done((f32[32,512]{1,0:T(8,128)S(1)}, f32[32,512]{1,0:T(8,128)S(1)}, u32[]{:S(2)}, u32[]{:S(2)}) %collective-permute-start.43) | collective-permute-done | bytes 65568 | tf_op jit(solution)/shard_map/ppermute | solution.py:41
  189.8 11.6 %collective-permute-start.36 = (bf16[256,512]{1,0:T(8,128)(2,1)}, bf16[256,512]{1,0:T(8,128)(2,1)}, u32[]{:S(2)}, u32[]{:S(2)}) collective-permute-start(bf16[256,512]{1,0:T(8,128)(2,1)} %get-tuple-element.161), channel_id=1, source_target_pairs={{0,8},{4,12},{8,0},{12,4},{16,24},{20,28},{24,16},{28,20},{1,9},{5... | collective-permute-start | bytes 786440 | tf_op jit(solution)/shard_map/ppermute | solution.py:41
  202.3 1.3 collective-permute-start.27
  203.7 15.9 %collective-permute-done.27 = bf16[128,896]{1,0:T(8,128)(2,1)S(1)} collective-permute-done((bf16[128,896]{1,0:T(8,128)(2,1)S(1)}, bf16[128,896]{1,0:T(8,128)(2,1)S(1)}, u32[]{:S(2)}, u32[]{:S(2)}) %collective-permute-start.27) | collective-permute-done | bytes 229408 | tf_op jit(solution)/shard_map/ppermute | solution.py:41
  224.1 2.1 collective-permute-start.28
  226.2 1.2 add_convert_fusion.5
  227.4 1.4 collective-permute-start.39
  228.9 11.8 %collective-permute-done.29.refs_4_ = bf16[384,896]{1,0:T(8,128)(2,1)S(1)} collective-permute-done((bf16[384,896]{1,0:T(8,128)(2,1)}, bf16[384,896]{1,0:T(8,128)(2,1)S(1)}, u32[]{:S(2)}, u32[]{:S(2)}) %collective-permute-start.29) | collective-permute-done | bytes 688160 | tf_op jit(solution)/shard_map/ppermute | solution.py:41
  240.9 2.6 collective-permute-start.34
  243.5 1.2 add_convert_fusion.1
  245.6 2.3 collective-permute-start.30
  248.1 2.0 collective-permute-start.33
  251.0 1.2 collective-permute-start.26
  252.8 8.4 %collective-permute-done.33.refs_6_ = bf16[128,512]{1,0:T(8,128)(2,1)S(1)} collective-permute-done((bf16[128,512]{1,0:T(8,128)(2,1)S(1)}, bf16[128,512]{1,0:T(8,128)(2,1)S(1)}, u32[]{:S(2)}, u32[]{:S(2)}) %collective-permute-start.33) | collective-permute-done | bytes 131104 | tf_op jit(solution)/shard_map/ppermute | solution.py:41
  261.2 1.5 collective-permute-done.30.refs_2_
  263.4 3.0 %shard_map.272 = (f32[128,2,512]{2,1,0:T(2,128)}, f32[512,128]{1,0:T(8,128)}, f32[128,8]{1,0:T(8,128)}, f32[128,256]{1,0:T(8,128)}) custom-call(s32[1]{0:T(128)} %bitcast.place, bf16[512,896]{1,0:T(8,128)(2,1)} %copy-done.6, bf16[128,896]{1,0:T(8,128)(2,1)} %copy-done.30, bf16[128,896]{1,0:T(8,128)(2,1)} %copy-done.34, bf16[128,896]{1,0:T(8,128)(2,1)} %copy-done.32, ...), custom_call_target="tpu_custom_call" | custom-call | tf_op jit(solution)/shard_map/pallas_call | solution.py:869
  269.3 1.3 slice_bitcast_fusion
  270.6 1.5 copy.42
  272.1 4.5 %collective-permute-done.46.refs_3_ = f32[160,256]{1,0:T(8,128)S(1)} collective-permute-done((f32[160,256]{1,0:T(8,128)S(1)}, f32[160,256]{1,0:T(8,128)S(1)}, u32[]{:S(2)}, u32[]{:S(2)}) %collective-permute-start.46) | collective-permute-done | bytes 163872 | tf_op jit(solution)/shard_map/ppermute | solution.py:41
  276.6 3.4 %collective-permute-done.45.refs_2_ = f32[160,256]{1,0:T(8,128)S(1)} collective-permute-done((f32[160,256]{1,0:T(8,128)S(1)}, f32[160,256]{1,0:T(8,128)S(1)}, u32[]{:S(2)}, u32[]{:S(2)}) %collective-permute-start.45) | collective-permute-done | bytes 163872 | tf_op jit(solution)/shard_map/ppermute | solution.py:41
  281.4 1.8 shard_map.274
  284.0 3.6 %shard_map.271 = f32[256,1,1024]{2,1,0:T(1,128)} custom-call(s32[1]{0:T(128)} %bitcast.place, bf16[256,1024]{1,0:T(8,128)(2,1)} %bitcast.36, bf16[256,1024]{1,0:T(8,128)(2,1)} %bitcast.39, f32[1,1024]{1,0:T(1,128)} %bitcast.45, bf16[512,1024]{1,0:T(8,128)(2,1)} %get-tuple-element.120.refs_0_, bf16[256,1024]{1,0:T(8,128)(2,1)} %copy-done.21, ...), custom_call_target="tpu_custom_call" | custom-call | tf_op jit(solution)/shard_map/pallas_call | solution.py:861
  288.4 3.2 %shard_map.267 = f32[256,1,1024]{2,1,0:T(1,128)} custom-call(s32[1]{0:T(128)} %bitcast.place, bf16[256,1024]{1,0:T(8,128)(2,1)} %bitcast.37, bf16[512,1024]{1,0:T(8,128)(2,1)} %get-tuple-element.153.refs_0_, bf16[256,1024]{1,0:T(8,128)(2,1)} %copy-done.20, bf16[512,1024]{1,0:T(8,128)(2,1)} %copy-done.7), custom_call_target="tpu_custom_call" | custom-call | tf_op jit(solution)/shard_map/pallas_call | solution.py:806
  (187 shorter events, 28.5 us)
Async XLA Ops:
  0.6 19.9 %copy-start.45 = (bf16[512,128]{1,0:T(8,128)(2,1)S(1)}, bf16[512,128]{1,0:T(8,128)(2,1)}, u32[]{:S(2)}) copy-start(bf16[512,128]{1,0:T(8,128)(2,1)} %param.28) | copy-start | bytes 393220
  9.9 70.7 %copy-start.16 = (bf16[128,896]{1,0:T(8,128)(2,1)}, bf16[128,896]{1,0:T(8,128)(2,1)S(1)}, u32[]{:S(2)}) copy-start(bf16[128,896]{1,0:T(8,128)(2,1)S(1)} %maximum_maximum_fusion.refs_4_) | copy-start | bytes 688132
  9.9 12.8 %collective-permute-start.16 = (bf16[128,896]{1,0:T(8,128)(2,1)S(1)}, bf16[128,896]{1,0:T(8,128)(2,1)S(1)}, u32[]{:S(2)}, u32[]{:S(2)}) collective-permute-start(bf16[128,896]{1,0:T(8,128)(2,1)S(1)} %maximum_maximum_fusion.refs_4_), channel_id=1, source_target_pairs={{0,4},{4,0},{8,12},{12,8},{16,20},{20,16},{24,28},{28,24},{1,5},{5... | collective-permute-start | bytes 688136 | tf_op jit(solution)/shard_map/ppermute | solution.py:41
  13.0 11.4 %collective-permute-start.15 = (bf16[128,896]{1,0:T(8,128)(2,1)S(1)}, bf16[128,896]{1,0:T(8,128)(2,1)S(1)}, u32[]{:S(2)}, u32[]{:S(2)}) collective-permute-start(bf16[128,896]{1,0:T(8,128)(2,1)S(1)} %maximum_maximum_fusion.refs_4_), channel_id=1, source_target_pairs={{0,24},{4,28},{8,16},{12,20},{16,8},{20,12},{24,0},{28,4},{1,25},{... | collective-permute-start | bytes 688136 | tf_op jit(solution)/shard_map/ppermute | solution.py:41
  16.6 31.4 %collective-permute-start.14 = (bf16[128,896]{1,0:T(8,128)(2,1)S(1)}, bf16[128,896]{1,0:T(8,128)(2,1)S(1)}, u32[]{:S(2)}, u32[]{:S(2)}) collective-permute-start(bf16[128,896]{1,0:T(8,128)(2,1)S(1)} %maximum_maximum_fusion.refs_4_), channel_id=1, source_target_pairs={{0,16},{4,20},{8,24},{12,28},{16,0},{20,4},{24,8},{28,12},{1,17},{... | collective-permute-start | bytes 688136 | tf_op jit(solution)/shard_map/ppermute | solution.py:41
  19.1 39.4 %collective-permute-start = (bf16[256,1024]{1,0:T(8,128)(2,1)}, bf16[256,1024]{1,0:T(8,128)(2,1)S(1)}, u32[]{:S(2)}, u32[]{:S(2)}) collective-permute-start(bf16[256,1024]{1,0:T(8,128)(2,1)} %get-tuple-element.76.refs_0_), channel_id=1, source_target_pairs={{0,2},{1,3},{2,0},{3,1},{4,6},{5,7},{6,4},{7,5},{8,10},{9,11},{10,... | collective-permute-start | bytes 1572872 | tf_op jit(solution)/shard_map/ppermute | solution.py:41
  20.8 80.3 %copy-start.15 = (bf16[128,1024]{1,0:T(8,128)(2,1)}, bf16[128,1024]{1,0:T(8,128)(2,1)S(1)}, u32[]{:S(2)}) copy-start(bf16[128,1024]{1,0:T(8,128)(2,1)S(1)} %pad_maximum_fusion.refs_8_) | copy-start | bytes 786436
  20.8 28.8 %collective-permute-start.11 = (bf16[128,1024]{1,0:T(8,128)(2,1)S(1)}, bf16[128,1024]{1,0:T(8,128)(2,1)S(1)}, u32[]{:S(2)}, u32[]{:S(2)}) collective-permute-start(bf16[128,1024]{1,0:T(8,128)(2,1)S(1)} %pad_maximum_fusion.refs_8_), channel_id=1, source_target_pairs={{0,24},{4,28},{8,16},{12,20},{16,8},{20,12},{24,0},{28,4},{1,25},{... | collective-permute-start | bytes 786440 | tf_op jit(solution)/shard_map/ppermute | solution.py:41
  22.8 27.4 %copy-start.26 = (bf16[128,896]{1,0:T(8,128)(2,1)}, bf16[128,896]{1,0:T(8,128)(2,1)S(1)}, u32[]{:S(2)}) copy-start(bf16[128,896]{1,0:T(8,128)(2,1)S(1)} %collective-permute-done.16.refs_8_) | copy-start | bytes 688132
  22.8 26.7 %collective-permute-start.13 = (bf16[128,896]{1,0:T(8,128)(2,1)S(1)}, bf16[128,896]{1,0:T(8,128)(2,1)S(1)}, u32[]{:S(2)}, u32[]{:S(2)}) collective-permute-start(bf16[128,896]{1,0:T(8,128)(2,1)S(1)} %maximum_maximum_fusion.refs_4_), channel_id=1, source_target_pairs={{0,8},{4,12},{8,0},{12,4},{16,24},{20,28},{24,16},{28,20},{1,9},{5... | collective-permute-start | bytes 688136 | tf_op jit(solution)/shard_map/ppermute | solution.py:41
  24.3 39.1 %copy-start.27 = (bf16[128,896]{1,0:T(8,128)(2,1)}, bf16[128,896]{1,0:T(8,128)(2,1)S(1)}, u32[]{:S(2)}) copy-start(bf16[128,896]{1,0:T(8,128)(2,1)S(1)} %collective-permute-done.15.refs_7_) | copy-start | bytes 688132
  24.3 34.1 %collective-permute-start.9 = (bf16[128,1024]{1,0:T(8,128)(2,1)S(1)}, bf16[128,1024]{1,0:T(8,128)(2,1)}, u32[]{:S(2)}, u32[]{:S(2)}) collective-permute-start(bf16[128,1024]{1,0:T(8,128)(2,1)S(1)} %pad_maximum_fusion.refs_8_), channel_id=1, source_target_pairs={{0,16},{4,20},{8,24},{12,28},{16,0},{20,4},{24,8},{28,12},{1,17},{... | collective-permute-start | bytes 786440 | tf_op jit(solution)/shard_map/ppermute | solution.py:41
  48.0 21.1 %collective-permute-start.3 = (bf16[256,1024]{1,0:T(8,128)(2,1)}, bf16[256,1024]{1,0:T(8,128)(2,1)S(1)}, u32[]{:S(2)}, u32[]{:S(2)}) collective-permute-start(bf16[256,1024]{1,0:T(8,128)(2,1)} %get-tuple-element.77.refs_4_), channel_id=1, source_target_pairs={{0,2},{1,3},{2,0},{3,1},{4,6},{5,7},{6,4},{7,5},{8,10},{9,11},{10,... | collective-permute-start | bytes 1572872 | tf_op jit(solution)/shard_map/ppermute | solution.py:41
  49.5 30.5 %copy-start.29 = (bf16[128,896]{1,0:T(8,128)(2,1)}, bf16[128,896]{1,0:T(8,128)(2,1)S(1)}, u32[]{:S(2)}) copy-start(bf16[128,896]{1,0:T(8,128)(2,1)S(1)} %collective-permute-done.13.refs_5_) | copy-start | bytes 688132
  49.5 11.9 %collective-permute-start.7 = (bf16[128,1024]{1,0:T(8,128)(2,1)S(1)}, bf16[128,1024]{1,0:T(8,128)(2,1)}, u32[]{:S(2)}, u32[]{:S(2)}) collective-permute-start(bf16[128,1024]{1,0:T(8,128)(2,1)S(1)} %pad_maximum_fusion.refs_8_), channel_id=1, source_target_pairs={{0,8},{4,12},{8,0},{12,4},{16,24},{20,28},{24,16},{28,20},{1,9},{5... | collective-permute-start | bytes 786440 | tf_op jit(solution)/shard_map/ppermute | solution.py:41
  49.6 51.5 %copy-start.22 = (bf16[128,1024]{1,0:T(8,128)(2,1)}, bf16[128,1024]{1,0:T(8,128)(2,1)S(1)}, u32[]{:S(2)}) copy-start(bf16[128,1024]{1,0:T(8,128)(2,1)S(1)} %collective-permute-done.11.refs_14_) | copy-start | bytes 786436
  49.6 12.3 %collective-permute-start.6 = (bf16[128,1024]{1,0:T(8,128)(2,1)S(1)}, bf16[128,1024]{1,0:T(8,128)(2,1)S(1)}, u32[]{:S(2)}, u32[]{:S(2)}) collective-permute-start(bf16[128,1024]{1,0:T(8,128)(2,1)S(1)} %pad_maximum_fusion.refs_8_), channel_id=1, source_target_pairs={{0,4},{4,0},{8,12},{12,8},{16,20},{20,16},{24,28},{28,24},{1,5},{5... | collective-permute-start | bytes 786440 | tf_op jit(solution)/shard_map/ppermute | solution.py:41
  58.5 20.1 %collective-permute-start.1 = (bf16[256,1024]{1,0:T(8,128)(2,1)}, bf16[256,1024]{1,0:T(8,128)(2,1)S(1)}, u32[]{:S(2)}, u32[]{:S(2)}) collective-permute-start(bf16[256,1024]{1,0:T(8,128)(2,1)} %get-tuple-element.76.refs_0_), channel_id=1, source_target_pairs={{0,1},{1,0},{2,3},{3,2},{4,5},{5,4},{6,7},{7,6},{8,9},{9,8},{10,11... | collective-permute-start | bytes 1572872 | tf_op jit(solution)/shard_map/ppermute | solution.py:41
  58.5 22.2 %copy-start.1 = (bf16[256,1024]{1,0:T(8,128)(2,1)}, bf16[256,1024]{1,0:T(8,128)(2,1)S(1)}, u32[]{:S(2)}) copy-start(bf16[256,1024]{1,0:T(8,128)(2,1)S(1)} %collective-permute-done.refs_2_.refs_1_) | copy-start | bytes 1572868
  58.5 21.6 %collective-permute-start.2 = (bf16[256,1024]{1,0:T(8,128)(2,1)S(1)}, bf16[256,1024]{1,0:T(8,128)(2,1)S(1)}, u32[]{:S(2)}, u32[]{:S(2)}) collective-permute-start(bf16[256,1024]{1,0:T(8,128)(2,1)S(1)} %collective-permute-done.refs_2_.refs_1_), channel_id=1, source_target_pairs={{0,1},{1,0},{2,3},{3,2},{4,5},{5,4},{6,7},{7,6},{8,9},{9,8},{10,11... | collective-permute-start | bytes 1572872 | tf_op jit(solution)/shard_map/ppermute | solution.py:41
  61.4 7.7 %collective-permute-start.19 = (bf16[128,896]{1,0:T(8,128)(2,1)S(1)}, bf16[128,896]{1,0:T(8,128)(2,1)S(1)}, u32[]{:S(2)}, u32[]{:S(2)}) collective-permute-start(bf16[128,896]{1,0:T(8,128)(2,1)S(1)} %collective-permute-done.15.refs_7_), channel_id=1, source_target_pairs={{0,4},{4,0},{8,12},{12,8},{16,20},{20,16},{24,28},{28,24},{1,5},{5... | collective-permute-start | bytes 688136 | tf_op jit(solution)/shard_map/ppermute | solution.py:41
  61.9 9.7 %collective-permute-start.18 = (bf16[128,896]{1,0:T(8,128)(2,1)}, bf16[128,896]{1,0:T(8,128)(2,1)S(1)}, u32[]{:S(2)}, u32[]{:S(2)}) collective-permute-start(bf16[128,896]{1,0:T(8,128)(2,1)} %copy-done.28), channel_id=1, source_target_pairs={{0,4},{4,0},{8,12},{12,8},{16,20},{20,16},{24,28},{28,24},{1,5},{5... | collective-permute-start | bytes 688136 | tf_op jit(solution)/shard_map/ppermute | solution.py:41
  69.1 32.1 %collective-permute-start.4 = (bf16[256,1024]{1,0:T(8,128)(2,1)}, bf16[256,1024]{1,0:T(8,128)(2,1)S(1)}, u32[]{:S(2)}, u32[]{:S(2)}) collective-permute-start(bf16[256,1024]{1,0:T(8,128)(2,1)} %get-tuple-element.77.refs_4_), channel_id=1, source_target_pairs={{0,1},{1,0},{2,3},{3,2},{4,5},{5,4},{6,7},{7,6},{8,9},{9,8},{10,11... | collective-permute-start | bytes 1572872 | tf_op jit(solution)/shard_map/ppermute | solution.py:41
  69.1 32.0 %copy-start.18 = (bf16[256,1024]{1,0:T(8,128)(2,1)}, bf16[256,1024]{1,0:T(8,128)(2,1)S(1)}, u32[]{:S(2)}) copy-start(bf16[256,1024]{1,0:T(8,128)(2,1)S(1)} %collective-permute-done.3.refs_5_) | copy-start | bytes 1572868
  69.1 32.1 %collective-permute-start.5 = (bf16[256,1024]{1,0:T(8,128)(2,1)S(1)}, bf16[256,1024]{1,0:T(8,128)(2,1)}, u32[]{:S(2)}, u32[]{:S(2)}) collective-permute-start(bf16[256,1024]{1,0:T(8,128)(2,1)S(1)} %collective-permute-done.3.refs_5_), channel_id=1, source_target_pairs={{0,1},{1,0},{2,3},{3,2},{4,5},{5,4},{6,7},{7,6},{8,9},{9,8},{10,11... | collective-permute-start | bytes 1572872 | tf_op jit(solution)/shard_map/ppermute | solution.py:41
  71.6 6.4 %collective-permute-start.17 = (bf16[128,896]{1,0:T(8,128)(2,1)S(1)}, bf16[128,896]{1,0:T(8,128)(2,1)S(1)}, u32[]{:S(2)}, u32[]{:S(2)}) collective-permute-start(bf16[128,896]{1,0:T(8,128)(2,1)S(1)} %collective-permute-done.13.refs_5_), channel_id=1, source_target_pairs={{0,4},{4,0},{8,12},{12,8},{16,20},{20,16},{24,28},{28,24},{1,5},{5... | collective-permute-start | bytes 688136 | tf_op jit(solution)/shard_map/ppermute | solution.py:41
  78.0 23.2 %collective-permute-start.12 = (bf16[128,1024]{1,0:T(8,128)(2,1)S(1)}, bf16[128,1024]{1,0:T(8,128)(2,1)}, u32[]{:S(2)}, u32[]{:S(2)}) collective-permute-start(bf16[128,1024]{1,0:T(8,128)(2,1)S(1)} %collective-permute-done.11.refs_14_), channel_id=1, source_target_pairs={{0,4},{4,0},{8,12},{12,8},{16,20},{20,16},{24,28},{28,24},{1,5},{5... | collective-permute-start | bytes 786440 | tf_op jit(solution)/shard_map/ppermute | solution.py:41
  78.5 22.6 %collective-permute-start.10 = (bf16[128,1024]{1,0:T(8,128)(2,1)}, bf16[128,1024]{1,0:T(8,128)(2,1)}, u32[]{:S(2)}, u32[]{:S(2)}) collective-permute-start(bf16[128,1024]{1,0:T(8,128)(2,1)} %collective-permute-done.9.refs_12_), channel_id=1, source_target_pairs={{0,4},{4,0},{8,12},{12,8},{16,20},{20,16},{24,28},{28,24},{1,5},{5... | collective-permute-start | bytes 786440 | tf_op jit(solution)/shard_map/ppermute | solution.py:41
  80.1 21.1 %collective-permute-start.8 = (bf16[128,1024]{1,0:T(8,128)(2,1)}, bf16[128,1024]{1,0:T(8,128)(2,1)}, u32[]{:S(2)}, u32[]{:S(2)}) collective-permute-start(bf16[128,1024]{1,0:T(8,128)(2,1)} %collective-permute-done.7.refs_10_), channel_id=1, source_target_pairs={{0,4},{4,0},{8,12},{12,8},{16,20},{20,16},{24,28},{28,24},{1,5},{5... | collective-permute-start | bytes 786440 | tf_op jit(solution)/shard_map/ppermute | solution.py:41
  111.0 3.8 %collective-permute-start.22 = (f32[4,8,256]{2,1,0:T(8,128)}, f32[4,8,256]{2,1,0:T(8,128)S(1)}, u32[]{:S(2)}, u32[]{:S(2)}) collective-permute-start(f32[4,8,256]{2,1,0:T(8,128)} %get-tuple-element.96.refs_0_), channel_id=1, source_target_pairs={{0,3},{1,2},{2,1},{3,0},{4,7},{5,6},{6,5},{7,4},{8,11},{9,10},{10,... | collective-permute-start | bytes 98312 | tf_op jit(solution)/shard_map/ppermute | solution.py:41
  111.1 4.2 %collective-permute-start.21 = (f32[4,8,256]{2,1,0:T(8,128)}, f32[4,8,256]{2,1,0:T(8,128)S(1)}, u32[]{:S(2)}, u32[]{:S(2)}) collective-permute-start(f32[4,8,256]{2,1,0:T(8,128)} %get-tuple-element.96.refs_0_), channel_id=1, source_target_pairs={{0,2},{1,3},{2,0},{3,1},{4,6},{5,7},{6,4},{7,5},{8,10},{9,11},{10,... | collective-permute-start | bytes 98312 | tf_op jit(solution)/shard_map/ppermute | solution.py:41
  112.7 2.6 collective-permute-start.20
  151.9 88.8 %copy-start.6 = (bf16[512,896]{1,0:T(8,128)(2,1)}, bf16[512,896]{1,0:T(8,128)(2,1)S(1)}, u32[]{:S(2)}) copy-start(bf16[512,896]{1,0:T(8,128)(2,1)S(1)} %convolution_convert_fusion.3.refs_0_) | copy-start | bytes 2752516
  169.2 33.1 %copy-start.25 = (bf16[128,896]{1,0:T(8,128)(2,1)S(1)}, bf16[128,896]{1,0:T(8,128)(2,1)}, u32[]{:S(2)}) copy-start(bf16[128,896]{1,0:T(8,128)(2,1)} %convolution_convert_fusion.5) | copy-start | bytes 688132
  169.2 4.7 %collective-permute-start.40 = (f32[32,512]{1,0:T(8,128)}, f32[32,512]{1,0:T(8,128)S(1)}, u32[]{:S(2)}, u32[]{:S(2)}) collective-permute-start(f32[32,512]{1,0:T(8,128)} %shard_map.273), channel_id=1, source_target_pairs={{0,4},{4,0},{8,12},{12,8},{16,20},{20,16},{24,28},{28,24},{1,5},{5... | collective-permute-start | bytes 196616 | tf_op jit(solution)/shard_map/ppermute | solution.py:41
  171.5 50.7 %collective-permute-start.38 = (bf16[256,512]{1,0:T(8,128)(2,1)}, bf16[256,512]{1,0:T(8,128)(2,1)}, u32[]{:S(2)}, u32[]{:S(2)}) collective-permute-start(bf16[256,512]{1,0:T(8,128)(2,1)} %get-tuple-element.159), channel_id=1, source_target_pairs={{0,24},{4,28},{8,16},{12,20},{16,8},{20,12},{24,0},{28,4},{1,25},{... | collective-permute-start | bytes 786440 | tf_op jit(solution)/shard_map/ppermute | solution.py:41
  173.9 49.0 %collective-permute-start.37 = (bf16[256,512]{1,0:T(8,128)(2,1)}, bf16[256,512]{1,0:T(8,128)(2,1)}, u32[]{:S(2)}, u32[]{:S(2)}) collective-permute-start(bf16[256,512]{1,0:T(8,128)(2,1)} %get-tuple-element.160), channel_id=1, source_target_pairs={{0,16},{4,20},{8,24},{12,28},{16,0},{20,4},{24,8},{28,12},{1,17},{... | collective-permute-start | bytes 786440 | tf_op jit(solution)/shard_map/ppermute | solution.py:41
  173.9 15.9 %collective-permute-start.43 = (f32[32,512]{1,0:T(8,128)S(1)}, f32[32,512]{1,0:T(8,128)S(1)}, u32[]{:S(2)}, u32[]{:S(2)}) collective-permute-start(f32[32,512]{1,0:T(8,128)S(1)} %add.62), channel_id=1, source_target_pairs={{0,24},{4,28},{8,16},{12,20},{16,8},{20,12},{24,0},{28,4},{1,25},{... | collective-permute-start | bytes 196616 | tf_op jit(solution)/shard_map/ppermute | solution.py:41
  176.3 25.2 %collective-permute-start.42 = (f32[32,512]{1,0:T(8,128)S(1)}, f32[32,512]{1,0:T(8,128)S(1)}, u32[]{:S(2)}, u32[]{:S(2)}) collective-permute-start(f32[32,512]{1,0:T(8,128)S(1)} %add.62), channel_id=1, source_target_pairs={{0,16},{4,20},{8,24},{12,28},{16,0},{20,4},{24,8},{28,12},{1,17},{... | collective-permute-start | bytes 196616 | tf_op jit(solution)/shard_map/ppermute | solution.py:41
  177.4 24.8 %collective-permute-start.41 = (f32[32,512]{1,0:T(8,128)S(1)}, f32[32,512]{1,0:T(8,128)S(1)}, u32[]{:S(2)}, u32[]{:S(2)}) collective-permute-start(f32[32,512]{1,0:T(8,128)S(1)} %add.62), channel_id=1, source_target_pairs={{0,8},{4,12},{8,0},{12,4},{16,24},{20,28},{24,16},{28,20},{1,9},{5... | collective-permute-start | bytes 196616 | tf_op jit(solution)/shard_map/ppermute | solution.py:41
  189.8 34.3 %collective-permute-start.36 = (bf16[256,512]{1,0:T(8,128)(2,1)}, bf16[256,512]{1,0:T(8,128)(2,1)}, u32[]{:S(2)}, u32[]{:S(2)}) collective-permute-start(bf16[256,512]{1,0:T(8,128)(2,1)} %get-tuple-element.161), channel_id=1, source_target_pairs={{0,8},{4,12},{8,0},{12,4},{16,24},{20,28},{24,16},{28,20},{1,9},{5... | collective-permute-start | bytes 786440 | tf_op jit(solution)/shard_map/ppermute | solution.py:41
  201.6 25.8 %collective-permute-start.32 = (bf16[512,512]{1,0:T(8,128)(2,1)}, bf16[512,512]{1,0:T(8,128)(2,1)S(1)}, u32[]{:S(2)}, u32[]{:S(2)}) collective-permute-start(bf16[512,512]{1,0:T(8,128)(2,1)} %get-tuple-element.163), channel_id=1, source_target_pairs={{0,4},{4,0},{8,12},{12,8},{16,20},{20,16},{24,28},{28,24},{1,5},{5... | collective-permute-start | bytes 1572872 | tf_op jit(solution)/shard_map/ppermute | solution.py:41
  202.3 17.3 %collective-permute-start.27 = (bf16[128,896]{1,0:T(8,128)(2,1)S(1)}, bf16[128,896]{1,0:T(8,128)(2,1)S(1)}, u32[]{:S(2)}, u32[]{:S(2)}) collective-permute-start(bf16[128,896]{1,0:T(8,128)(2,1)S(1)} %copy-done.25), channel_id=1, source_target_pairs={{0,4},{4,0},{8,12},{12,8},{16,20},{20,16},{24,28},{28,24},{1,5},{5... | collective-permute-start | bytes 688136 | tf_op jit(solution)/shard_map/ppermute | solution.py:41
  203.6 17.2 %copy-start.37 = (f32[32,512]{1,0:T(8,128)}, f32[32,512]{1,0:T(8,128)S(1)}, u32[]{:S(2)}) copy-start(f32[32,512]{1,0:T(8,128)S(1)} %add_add_fusion) | copy-start | bytes 196612
  220.3 20.6 %collective-permute-start.23 = (bf16[512,1024]{1,0:T(8,128)(2,1)}, bf16[512,1024]{1,0:T(8,128)(2,1)S(1)}, u32[]{:S(2)}, u32[]{:S(2)}) collective-permute-start(bf16[512,1024]{1,0:T(8,128)(2,1)} %get-tuple-element.152), channel_id=1, source_target_pairs={{0,1},{1,0},{2,3},{3,2},{4,5},{5,4},{6,7},{7,6},{8,9},{9,8},{10,11... | collective-permute-start | bytes 3145736 | tf_op jit(solution)/shard_map/ppermute | solution.py:41
  222.2 18.5 %collective-permute-start.29 = (bf16[384,896]{1,0:T(8,128)(2,1)}, bf16[384,896]{1,0:T(8,128)(2,1)S(1)}, u32[]{:S(2)}, u32[]{:S(2)}) collective-permute-start(bf16[384,896]{1,0:T(8,128)(2,1)} %convolution_convert_fusion.4), channel_id=1, source_target_pairs={{0,4},{4,0},{8,12},{12,8},{16,20},{20,16},{24,28},{28,24},{1,5},{5... | collective-permute-start | bytes 2064392 | tf_op jit(solution)/shard_map/ppermute | solution.py:41
  222.9 21.8 %collective-permute-start.25 = (bf16[512,1024]{1,0:T(8,128)(2,1)}, bf16[512,1024]{1,0:T(8,128)(2,1)S(1)}, u32[]{:S(2)}, u32[]{:S(2)}) collective-permute-start(bf16[512,1024]{1,0:T(8,128)(2,1)} %get-tuple-element.121), channel_id=1, source_target_pairs={{0,1},{1,0},{2,3},{3,2},{4,5},{5,4},{6,7},{7,6},{8,9},{9,8},{10,11... | collective-permute-start | bytes 3145736 | tf_op jit(solution)/shard_map/ppermute | solution.py:41
  224.1 24.0 %collective-permute-start.28 = (bf16[128,896]{1,0:T(8,128)(2,1)S(1)}, bf16[128,896]{1,0:T(8,128)(2,1)S(1)}, u32[]{:S(2)}, u32[]{:S(2)}) collective-permute-start(bf16[128,896]{1,0:T(8,128)(2,1)S(1)} %add_convert_fusion.4), channel_id=1, source_target_pairs={{0,24},{4,28},{8,16},{12,20},{16,8},{20,12},{24,0},{28,4},{1,25},{... | collective-permute-start | bytes 688136 | tf_op jit(solution)/shard_map/ppermute | solution.py:41
  227.4 20.5 %copy-start.8 = (bf16[512,1024]{1,0:T(8,128)(2,1)S(1)}, bf16[512,1024]{1,0:T(8,128)(2,1)}, u32[]{:S(2)}) copy-start(bf16[512,1024]{1,0:T(8,128)(2,1)} %get-tuple-element.120.refs_0_) | copy-start | bytes 3145732
  227.4 20.7 %copy-start.12 = (bf16[512,512]{1,0:T(8,128)(2,1)}, bf16[512,512]{1,0:T(8,128)(2,1)S(1)}, u32[]{:S(2)}) copy-start(bf16[512,512]{1,0:T(8,128)(2,1)S(1)} %collective-permute-done.32.refs_9_) | copy-start | bytes 1572868
  227.4 17.4 %collective-permute-start.39 = (bf16[128,512]{1,0:T(8,128)(2,1)S(1)}, bf16[128,512]{1,0:T(8,128)(2,1)S(1)}, u32[]{:S(2)}, u32[]{:S(2)}) collective-permute-start(bf16[128,512]{1,0:T(8,128)(2,1)S(1)} %add_convert_fusion.5), channel_id=1, source_target_pairs={{0,4},{4,0},{8,12},{12,8},{16,20},{20,16},{24,28},{28,24},{1,5},{5... | collective-permute-start | bytes 393224 | tf_op jit(solution)/shard_map/ppermute | solution.py:41
  240.7 9.4 %collective-permute-start.35 = (bf16[128,512]{1,0:T(8,128)(2,1)S(1)}, bf16[128,512]{1,0:T(8,128)(2,1)}, u32[]{:S(2)}, u32[]{:S(2)}) collective-permute-start(bf16[128,512]{1,0:T(8,128)(2,1)S(1)} %get-tuple-element.156), channel_id=1, source_target_pairs={{0,8},{4,12},{8,0},{12,4},{16,24},{20,28},{24,16},{28,20},{1,9},{5... | collective-permute-start | bytes 393224 | tf_op jit(solution)/shard_map/ppermute | solution.py:41
  240.9 25.6 %copy-start.7 = (bf16[512,1024]{1,0:T(8,128)(2,1)}, bf16[512,1024]{1,0:T(8,128)(2,1)S(1)}, u32[]{:S(2)}) copy-start(bf16[512,1024]{1,0:T(8,128)(2,1)S(1)} %collective-permute-done.23.refs_2_) | copy-start | bytes 3145732
  240.9 10.1 %collective-permute-start.34 = (bf16[128,512]{1,0:T(8,128)(2,1)S(1)}, bf16[128,512]{1,0:T(8,128)(2,1)S(1)}, u32[]{:S(2)}, u32[]{:S(2)}) collective-permute-start(bf16[128,512]{1,0:T(8,128)(2,1)S(1)} %get-tuple-element.157), channel_id=1, source_target_pairs={{0,16},{4,20},{8,24},{12,28},{16,0},{20,4},{24,8},{28,12},{1,17},{... | collective-permute-start | bytes 393224 | tf_op jit(solution)/shard_map/ppermute | solution.py:41
  244.7 16.5 %collective-permute-start.31 = (bf16[128,896]{1,0:T(8,128)(2,1)S(1)}, bf16[128,896]{1,0:T(8,128)(2,1)S(1)}, u32[]{:S(2)}, u32[]{:S(2)}) collective-permute-start(bf16[128,896]{1,0:T(8,128)(2,1)S(1)} %get-tuple-element.154), channel_id=1, source_target_pairs={{0,8},{4,12},{8,0},{12,4},{16,24},{20,28},{24,16},{28,20},{1,9},{5... | collective-permute-start | bytes 688136 | tf_op jit(solution)/shard_map/ppermute | solution.py:41
  245.6 17.1 %collective-permute-start.30 = (bf16[128,896]{1,0:T(8,128)(2,1)S(1)}, bf16[128,896]{1,0:T(8,128)(2,1)S(1)}, u32[]{:S(2)}, u32[]{:S(2)}) collective-permute-start(bf16[128,896]{1,0:T(8,128)(2,1)S(1)} %get-tuple-element.155), channel_id=1, source_target_pairs={{0,16},{4,20},{8,24},{12,28},{16,0},{20,4},{24,8},{28,12},{1,17},{... | collective-permute-start | bytes 688136 | tf_op jit(solution)/shard_map/ppermute | solution.py:41
  248.1 13.1 %collective-permute-start.33 = (bf16[128,512]{1,0:T(8,128)(2,1)S(1)}, bf16[128,512]{1,0:T(8,128)(2,1)S(1)}, u32[]{:S(2)}, u32[]{:S(2)}) collective-permute-start(bf16[128,512]{1,0:T(8,128)(2,1)S(1)} %get-tuple-element.158), channel_id=1, source_target_pairs={{0,24},{4,28},{8,16},{12,20},{16,8},{20,12},{24,0},{28,4},{1,25},{... | collective-permute-start | bytes 393224 | tf_op jit(solution)/shard_map/ppermute | solution.py:41
  250.2 37.5 %collective-permute-start.24 = (bf16[256,1024]{1,0:T(8,128)(2,1)S(1)}, bf16[256,1024]{1,0:T(8,128)(2,1)S(1)}, u32[]{:S(2)}, u32[]{:S(2)}) collective-permute-start(bf16[256,1024]{1,0:T(8,128)(2,1)S(1)} %add_convert_fusion.1), channel_id=1, source_target_pairs={{0,2},{1,3},{2,0},{3,1},{4,6},{5,7},{6,4},{7,5},{8,10},{9,11},{10,... | collective-permute-start | bytes 1572872 | tf_op jit(solution)/shard_map/ppermute | solution.py:41
  251.0 12.5 %copy-start.43 = (bf16[128,512]{1,0:T(8,128)(2,1)}, bf16[128,512]{1,0:T(8,128)(2,1)S(1)}, u32[]{:S(2)}) copy-start(bf16[128,512]{1,0:T(8,128)(2,1)S(1)} %collective-permute-done.34.refs_7_) | copy-start | bytes 393220
  251.0 32.3 %collective-permute-start.26 = (bf16[256,1024]{1,0:T(8,128)(2,1)S(1)}, bf16[256,1024]{1,0:T(8,128)(2,1)S(1)}, u32[]{:S(2)}, u32[]{:S(2)}) collective-permute-start(bf16[256,1024]{1,0:T(8,128)(2,1)S(1)} %add_convert_fusion), channel_id=1, source_target_pairs={{0,2},{1,3},{2,0},{3,1},{4,6},{5,7},{6,4},{7,5},{8,10},{9,11},{10,... | collective-permute-start | bytes 1572872 | tf_op jit(solution)/shard_map/ppermute | solution.py:41
  267.4 12.7 %copy-start.17 = (f32[160,256]{1,0:T(8,128)}, f32[160,256]{1,0:T(8,128)S(1)}, u32[]{:S(2)}) copy-start(f32[160,256]{1,0:T(8,128)S(1)} %pad_maximum_fusion.1.refs_0_) | copy-start | bytes 491524
  267.4 9.2 %collective-permute-start.46 = (f32[160,256]{1,0:T(8,128)S(1)}, f32[160,256]{1,0:T(8,128)S(1)}, u32[]{:S(2)}, u32[]{:S(2)}) collective-permute-start(f32[160,256]{1,0:T(8,128)S(1)} %pad_maximum_fusion.1.refs_0_), channel_id=1, source_target_pairs={{0,3},{1,2},{2,1},{3,0},{4,7},{5,6},{6,5},{7,4},{8,11},{9,10},{10,... | collective-permute-start | bytes 491528 | tf_op jit(solution)/shard_map/ppermute | solution.py:41
  267.5 12.6 %collective-permute-start.45 = (f32[160,256]{1,0:T(8,128)S(1)}, f32[160,256]{1,0:T(8,128)S(1)}, u32[]{:S(2)}, u32[]{:S(2)}) collective-permute-start(f32[160,256]{1,0:T(8,128)S(1)} %pad_maximum_fusion.1.refs_0_), channel_id=1, source_target_pairs={{0,2},{1,3},{2,0},{3,1},{4,6},{5,7},{6,4},{7,5},{8,10},{9,11},{10,... | collective-permute-start | bytes 491528 | tf_op jit(solution)/shard_map/ppermute | solution.py:41
  268.3 11.7 %collective-permute-start.44 = (f32[160,256]{1,0:T(8,128)S(1)}, f32[160,256]{1,0:T(8,128)S(1)}, u32[]{:S(2)}, u32[]{:S(2)}) collective-permute-start(f32[160,256]{1,0:T(8,128)S(1)} %pad_maximum_fusion.1.refs_0_), channel_id=1, source_target_pairs={{0,1},{1,0},{2,3},{3,2},{4,5},{5,4},{6,7},{7,6},{8,9},{9,8},{10,11... | collective-permute-start | bytes 491528 | tf_op jit(solution)/shard_map/ppermute | solution.py:41
  (35 other events, 120.3 us)
